TPU v7x, 128 devices: a whole 4x4x4 slice. The times are simulated.
128 devices in a mesh: wide: 32 (over y, x, core), narrow: 4 (over z).
Axes of the slice: x: 4, y: 4, z: 4, core: 2. Of those that a mesh axis runs over, the one named last changes fastest.
Arguments:
- volume: bfloat16 [256, 256, 128], P('wide', 'narrow'), may hold values from -6 to 6
- angles: float32 [2, 8], replicated, may hold values from -3.140625 to 3.140625
- tile_points: int32 [32768, 128], P(('wide', 'narrow')), may hold values from 0 to 65535
- tile_dest: int32 [32768, 1], P(('wide', 'narrow')), may hold values from 0 to 127; in each aligned block of 256 rows (0 to 255, 256 to 511, ...) at most 4 rows name the same one
Outputs:
- responses: bfloat16 [16, 256, 256, 128], P(None, 'wide', 'narrow')
- fiber_out: bfloat16 [16384, 4, 16, 128], P(('wide', 'narrow'))
Inputs may be any that keep to these rules, and one draw needn't show every extreme that they name: `tile_dest`: among the 256 tiles of one device no owner is named more than 4 times, and in every draw some owner is named exactly 4 times by the tiles of some device.
All inputs are finite; a program needn't handle non-finite values.
Results may differ from a plain program's by a relative error of at most 0.0076.
Values may be sent and summed in bfloat16 or wider, within the bound.
No kernel may reach another device: no remote copies, remote signals or barrier semaphores. Data moves between devices by JAX's collectives and lax.ppermute only.
A program may use at most 64 MiB of HBM per device.

v0:
```python
import math

import jax
import jax.numpy as jnp
from jax import lax
from jax.sharding import PartitionSpec as P

TAPS_PER_SIDE = 3
DILATION_SECOND = 2
CAP = 4


response_gain = 6.0
smooth_sigma = 4.0


def with_halo(block, sides, width):
    for axis, dim in sides:
        count = lax.axis_size(axis)
        forward = [(i, i + 1) for i in range(count - 1)]
        backward = [(target, source) for source, target in forward]
        low = lax.ppermute(
            lax.slice_in_dim(block, block.shape[dim] - width, None, axis=dim), axis, forward
        )
        high = lax.ppermute(lax.slice_in_dim(block, 0, width, axis=dim), axis, backward)
        block = jnp.concatenate([low, block, high], axis=dim)
    return block


def tap_table():
    offsets = jnp.arange(-TAPS_PER_SIDE, TAPS_PER_SIDE + 1).astype(jnp.float32)
    gauss_bell = jnp.exp(-0.5 * offsets * offsets)
    normalized = gauss_bell / jnp.sum(gauss_bell)
    return jnp.stack(
        [normalized, -offsets * normalized, (offsets * offsets - 1.0) * normalized]
    ).astype(jnp.bfloat16)


def make_band(tap_values, tap_spacing, column_list):
    row_ids = lax.broadcasted_iota(jnp.int32, (column_list, column_list), 0)
    col_ids = lax.broadcasted_iota(jnp.int32, (column_list, column_list), 1)
    distance = col_ids - row_ids
    tap_floats = tap_values.astype(jnp.float32)
    pieces = []
    for tap_kind in range(3):
        summed = jnp.zeros((column_list, column_list), jnp.float32)
        for offset in range(2 * TAPS_PER_SIDE + 1):
            summed = summed + jnp.where(
                distance == (offset - TAPS_PER_SIDE) * tap_spacing,
                tap_floats[tap_kind, offset],
                0.0,
            )
        pieces.append(summed)
    return jnp.concatenate(pieces, axis=1).astype(jnp.bfloat16)


def pass_along(field_in, tap_floats, tap_kind, tap_spacing, along_axis, output_count, border_depth):
    summed = None
    for offset in range(2 * TAPS_PER_SIDE + 1):
        shift = (offset - TAPS_PER_SIDE) * tap_spacing
        contribution = tap_floats[tap_kind, offset] * lax.slice_in_dim(
            field_in, border_depth - shift, border_depth - shift + output_count, axis=along_axis
        )
        summed = contribution if summed is None else summed + contribution
    return summed


def hessian_mix(along_x, tap_floats, tap_spacing, orient_weights, border_depth):
    z_count = along_x[0].shape[0] - 2 * border_depth
    y_count = along_x[0].shape[1] - 2 * border_depth

    def along_z(field_in, tap_kind):
        return pass_along(field_in, tap_floats, tap_kind, tap_spacing, 0, z_count, border_depth)

    def along_y(field_in, tap_kind):
        return pass_along(field_in, tap_floats, tap_kind, tap_spacing, 1, y_count, border_depth)

    z_plain = along_z(along_x[0], 0)
    hessian_terms = [
        along_y(along_z(along_x[2], 0), 0),
        along_y(z_plain, 2),
        along_y(along_z(along_x[0], 2), 0),
        along_y(along_z(along_x[1], 0), 1),
        along_y(along_z(along_x[1], 1), 0),
        along_y(along_z(along_x[0], 1), 1),
    ]
    stacked = jnp.stack(hessian_terms)
    return jnp.einsum("ok,kzyx->ozyx", orient_weights, stacked, precision=lax.Precision.HIGHEST)


def orientation_weights(angles):
    polar_angle = angles[0]
    azimuth = angles[1]
    dir_x = jnp.sin(polar_angle) * jnp.cos(azimuth)
    dir_y = jnp.sin(polar_angle) * jnp.sin(azimuth)
    dir_z = jnp.cos(polar_angle)
    return response_gain * jnp.stack(
        [
            dir_x * dir_x,
            dir_y * dir_y,
            dir_z * dir_z,
            2.0 * dir_x * dir_y,
            2.0 * dir_x * dir_z,
            2.0 * dir_y * dir_z,
        ],
        axis=1,
    )


def smooth_matrix(points_count):
    source_pos = lax.broadcasted_iota(jnp.int32, (points_count, points_count), 0).astype(
        jnp.float32
    )
    target_pos = lax.broadcasted_iota(jnp.int32, (points_count, points_count), 1).astype(
        jnp.float32
    )
    distance = target_pos - source_pos
    gauss_bell = jnp.exp(-distance * distance / (2.0 * smooth_sigma * smooth_sigma))
    return (gauss_bell / jnp.sum(gauss_bell, axis=0, keepdims=True)).astype(jnp.bfloat16)


def sample_tiles(responses, tile_points):
    channels = responses.shape[0]
    cell_total = responses.size // channels
    lane_width = math.gcd(responses.shape[-1], 128)
    grouped = responses.reshape(channels, cell_total // lane_width, lane_width).transpose(1, 0, 2)
    flat_points = tile_points.reshape(-1)
    point_total = flat_points.shape[0]
    block_size = math.gcd(point_total, 2048)
    point_blocks = flat_points.reshape(point_total // block_size, block_size)

    def pick_block(points_here):
        row_index = points_here // lane_width
        lane_index = points_here % lane_width
        rows_taken = jnp.take(grouped, row_index, axis=0)
        lane_ids = lax.broadcasted_iota(jnp.int32, (block_size, lane_width), 1)
        selector = (lane_ids == lane_index[:, None]).astype(responses.dtype)
        picked_here = jnp.einsum(
            "pcl,pl->pc", rows_taken, selector, preferred_element_type=jnp.float32
        )
        return picked_here.astype(responses.dtype)

    picked = lax.map(pick_block, point_blocks)
    return picked.reshape(tile_points.shape[0], tile_points.shape[1], channels).transpose(0, 2, 1)


def place_tiles(tile_rows, destination, block_count):
    tile_total = destination.shape[0]
    earlier = lax.broadcasted_iota(jnp.int32, (tile_total, tile_total), 0)
    later = lax.broadcasted_iota(jnp.int32, (tile_total, tile_total), 1)
    same_owner = (destination[:, None] == destination[None, :]) & (earlier < later)
    slot_rank = jnp.sum(same_owner.astype(jnp.int32), axis=0)
    slot_index = destination * CAP + slot_rank
    slot_ids = lax.broadcasted_iota(jnp.int32, (block_count * CAP, tile_total), 0)
    selector = (slot_ids == slot_index[None, :]).astype(jnp.bfloat16)
    moved = jnp.dot(selector, tile_rows.reshape(tile_total, -1), preferred_element_type=jnp.float32)
    return moved.astype(jnp.bfloat16).reshape((block_count, CAP) + tile_rows.shape[1:])


def per_device(volume, angles, tile_points, tile_dest):
    border_depth = TAPS_PER_SIDE * DILATION_SECOND
    extended = with_halo(volume, (("wide", 0), ("narrow", 1)), border_depth)
    tap_values = tap_table()
    tap_floats = tap_values.astype(jnp.float32)
    orient_weights = orientation_weights(angles)
    column_list = volume.shape[2]
    flattened = extended.reshape(-1, column_list)
    outputs = []
    for tap_spacing in (1, DILATION_SECOND):
        banded = make_band(tap_values, tap_spacing, column_list)
        product = jnp.dot(flattened, banded, preferred_element_type=jnp.float32)
        product = product.reshape(extended.shape[0], extended.shape[1], 3, column_list)
        along_x = [product[:, :, tap_kind, :] for tap_kind in range(3)]
        outputs.append(hessian_mix(along_x, tap_floats, tap_spacing, orient_weights, border_depth))
    responses = jnp.concatenate(outputs, axis=0).astype(jnp.bfloat16)
    wide_count = lax.axis_size("wide")
    narrow_count = lax.axis_size("narrow")
    block_count = wide_count * narrow_count
    smoothing_matrix = smooth_matrix(tile_points.shape[1])
    tile_rows = sample_tiles(responses, tile_points)
    outgoing = place_tiles(tile_rows, tile_dest[:, 0], block_count)
    bundle = lax.all_to_all(outgoing, ("wide", "narrow"), split_axis=0, concat_axis=0, tiled=True)
    reshaped = bundle.reshape(-1, bundle.shape[-1])
    arrived = (
        jnp.dot(reshaped, smoothing_matrix, preferred_element_type=jnp.float32)
        .astype(jnp.bfloat16)
        .reshape(bundle.shape)
    )
    return (responses, arrived)


def solution(mesh):
    return jax.shard_map(
        per_device,
        mesh=mesh,
        in_specs=(
            P("wide", "narrow", None),
            P(),
            P(("wide", "narrow"), None),
            P(("wide", "narrow"), None),
        ),
        out_specs=(P(None, "wide", "narrow", None), P(("wide", "narrow"), None, None, None)),
        check_vma=False,
    )
```

profile of v0, /device:TPU:1, one launch (start us, length us, event | category | flops | bytes accessed | tf_op | source)
XLA Modules:
  0.0 733.4 jit_solution(10027685952585798650)
XLA Ops:
  1.6 4.5 collective-permute-start
  11.4 4.6 fusion.152
  16.0 4.6 fusion.156
  32.0 4.4 fusion.168
  36.4 4.4 fusion.172
  50.8 4.7 fusion.35
  55.5 4.7 add_bitcast_fusion.7
  60.2 4.5 add_bitcast_fusion.6
  64.7 4.7 fusion.50
  69.3 4.5 fusion.48
  73.8 4.5 add_bitcast_fusion.5
  78.8 4.7 fusion.27
  83.4 4.7 add_bitcast_fusion.4
  88.1 4.5 add_bitcast_fusion.3
  92.6 4.7 add_bitcast_fusion.2
  97.3 4.5 add_bitcast_fusion.1
  101.8 4.5 add_bitcast_fusion
  106.2 4.7 fusion.141
  111.0 4.7 fusion.93
  115.7 4.6 fusion.133
  120.3 4.7 fusion.125
  125.0 4.5 fusion.117
  129.5 4.7 fusion.109
  134.3 4.5 fusion.101
  141.5 4.5 fusion.85
  146.1 4.7 fusion.77
  150.8 4.5 fusion.69
  155.3 4.7 fusion.61
  160.0 4.5 fusion.53
  168.2 515.6 %while.12 = (s32[]{:T(128)}, bf16[16,2048,16]{1,2,0:T(8,128)(2,1)}, s32[16,2048]{1,0:T(8,128)S(1)}, bf16[512,16,128]{2,1,0:T(8,128)(2,1)S(1)}, s32[]{:T(128)}) while((s32[]{:T(128)}, bf16[16,2048,16]{1,2,0:T(8,128)(2,1)}, s32[16,2048]{1,0:T(8,128)S(1)}, bf16[512,16,128]{2,1,0:T(8,128)(2,1)S(1)}, s32[]{:T(128)}) %tuple.66), condition=%wide.region_3.4_spmd, body=%wide.region_2.3_spmd.sunk | while | flops 12949506 | bytes 26104384 | solution.py:143
  168.2 16.3 %gather_fusion = bf16[2048,16,128]{2,1,0:T(8,128)(2,1)} fusion(bf16[512,16,128]{2,1,0:T(8,128)(2,1)S(1)} %get-tuple-element.155, s32[2048]{0:T(1024)S(1)} %broadcast_clamp_fusion.2), kind=kCustom, calls=%fused_computation.clone.1 | custom fusion | bytes 16785408 | tf_op jit(solution)/shard_map/while/body/eval_jaxpr/jit(_take)/gather | solution.py:135
  184.9 14.4 %fusion.223 = bf16[2048,1,16]{2,1,0:T(2,128)(2,1)S(1)} fusion(bf16[2048,16,128]{2,1,0:T(8,128)(2,1)} %gather_fusion, pred[2048]{0:T(1024)(128)(4,1)S(1)} %compare_and_fusion.2, pred[2048,128,1]{1,0,2:T(32,128)(4,1)S(1)} %fusion.222), kind=kOutput, calls=%fused_computation.1.clone.1 | convolution fusion | flops 12582912 | bytes 8718336 | tf_op jit(solution)/shard_map/while/body/eval_jaxpr/pcl,pl->pc/dot_general | solution.py:138
  200.5 16.3 %gather_fusion = bf16[2048,16,128]{2,1,0:T(8,128)(2,1)} fusion(bf16[512,16,128]{2,1,0:T(8,128)(2,1)S(1)} %get-tuple-element.155, s32[2048]{0:T(1024)S(1)} %broadcast_clamp_fusion.2), kind=kCustom, calls=%fused_computation.clone.1 | custom fusion | bytes 16785408 | tf_op jit(solution)/shard_map/while/body/eval_jaxpr/jit(_take)/gather | solution.py:135
  217.1 14.4 %fusion.223 = bf16[2048,1,16]{2,1,0:T(2,128)(2,1)S(1)} fusion(bf16[2048,16,128]{2,1,0:T(8,128)(2,1)} %gather_fusion, pred[2048]{0:T(1024)(128)(4,1)S(1)} %compare_and_fusion.2, pred[2048,128,1]{1,0,2:T(32,128)(4,1)S(1)} %fusion.222), kind=kOutput, calls=%fused_computation.1.clone.1 | convolution fusion | flops 12582912 | bytes 8718336 | tf_op jit(solution)/shard_map/while/body/eval_jaxpr/pcl,pl->pc/dot_general | solution.py:138
  232.7 16.3 %gather_fusion = bf16[2048,16,128]{2,1,0:T(8,128)(2,1)} fusion(bf16[512,16,128]{2,1,0:T(8,128)(2,1)S(1)} %get-tuple-element.155, s32[2048]{0:T(1024)S(1)} %broadcast_clamp_fusion.2), kind=kCustom, calls=%fused_computation.clone.1 | custom fusion | bytes 16785408 | tf_op jit(solution)/shard_map/while/body/eval_jaxpr/jit(_take)/gather | solution.py:135
  249.3 14.4 %fusion.223 = bf16[2048,1,16]{2,1,0:T(2,128)(2,1)S(1)} fusion(bf16[2048,16,128]{2,1,0:T(8,128)(2,1)} %gather_fusion, pred[2048]{0:T(1024)(128)(4,1)S(1)} %compare_and_fusion.2, pred[2048,128,1]{1,0,2:T(32,128)(4,1)S(1)} %fusion.222), kind=kOutput, calls=%fused_computation.1.clone.1 | convolution fusion | flops 12582912 | bytes 8718336 | tf_op jit(solution)/shard_map/while/body/eval_jaxpr/pcl,pl->pc/dot_general | solution.py:138
  264.9 16.3 %gather_fusion = bf16[2048,16,128]{2,1,0:T(8,128)(2,1)} fusion(bf16[512,16,128]{2,1,0:T(8,128)(2,1)S(1)} %get-tuple-element.155, s32[2048]{0:T(1024)S(1)} %broadcast_clamp_fusion.2), kind=kCustom, calls=%fused_computation.clone.1 | custom fusion | bytes 16785408 | tf_op jit(solution)/shard_map/while/body/eval_jaxpr/jit(_take)/gather | solution.py:135
  281.5 14.4 %fusion.223 = bf16[2048,1,16]{2,1,0:T(2,128)(2,1)S(1)} fusion(bf16[2048,16,128]{2,1,0:T(8,128)(2,1)} %gather_fusion, pred[2048]{0:T(1024)(128)(4,1)S(1)} %compare_and_fusion.2, pred[2048,128,1]{1,0,2:T(32,128)(4,1)S(1)} %fusion.222), kind=kOutput, calls=%fused_computation.1.clone.1 | convolution fusion | flops 12582912 | bytes 8718336 | tf_op jit(solution)/shard_map/while/body/eval_jaxpr/pcl,pl->pc/dot_general | solution.py:138
  297.1 16.3 %gather_fusion = bf16[2048,16,128]{2,1,0:T(8,128)(2,1)} fusion(bf16[512,16,128]{2,1,0:T(8,128)(2,1)S(1)} %get-tuple-element.155, s32[2048]{0:T(1024)S(1)} %broadcast_clamp_fusion.2), kind=kCustom, calls=%fused_computation.clone.1 | custom fusion | bytes 16785408 | tf_op jit(solution)/shard_map/while/body/eval_jaxpr/jit(_take)/gather | solution.py:135
  313.8 14.4 %fusion.223 = bf16[2048,1,16]{2,1,0:T(2,128)(2,1)S(1)} fusion(bf16[2048,16,128]{2,1,0:T(8,128)(2,1)} %gather_fusion, pred[2048]{0:T(1024)(128)(4,1)S(1)} %compare_and_fusion.2, pred[2048,128,1]{1,0,2:T(32,128)(4,1)S(1)} %fusion.222), kind=kOutput, calls=%fused_computation.1.clone.1 | convolution fusion | flops 12582912 | bytes 8718336 | tf_op jit(solution)/shard_map/while/body/eval_jaxpr/pcl,pl->pc/dot_general | solution.py:138
  329.4 16.3 %gather_fusion = bf16[2048,16,128]{2,1,0:T(8,128)(2,1)} fusion(bf16[512,16,128]{2,1,0:T(8,128)(2,1)S(1)} %get-tuple-element.155, s32[2048]{0:T(1024)S(1)} %broadcast_clamp_fusion.2), kind=kCustom, calls=%fused_computation.clone.1 | custom fusion | bytes 16785408 | tf_op jit(solution)/shard_map/while/body/eval_jaxpr/jit(_take)/gather | solution.py:135
  346.0 14.4 %fusion.223 = bf16[2048,1,16]{2,1,0:T(2,128)(2,1)S(1)} fusion(bf16[2048,16,128]{2,1,0:T(8,128)(2,1)} %gather_fusion, pred[2048]{0:T(1024)(128)(4,1)S(1)} %compare_and_fusion.2, pred[2048,128,1]{1,0,2:T(32,128)(4,1)S(1)} %fusion.222), kind=kOutput, calls=%fused_computation.1.clone.1 | convolution fusion | flops 12582912 | bytes 8718336 | tf_op jit(solution)/shard_map/while/body/eval_jaxpr/pcl,pl->pc/dot_general | solution.py:138
  361.6 16.3 %gather_fusion = bf16[2048,16,128]{2,1,0:T(8,128)(2,1)} fusion(bf16[512,16,128]{2,1,0:T(8,128)(2,1)S(1)} %get-tuple-element.155, s32[2048]{0:T(1024)S(1)} %broadcast_clamp_fusion.2), kind=kCustom, calls=%fused_computation.clone.1 | custom fusion | bytes 16785408 | tf_op jit(solution)/shard_map/while/body/eval_jaxpr/jit(_take)/gather | solution.py:135
  378.2 14.4 %fusion.223 = bf16[2048,1,16]{2,1,0:T(2,128)(2,1)S(1)} fusion(bf16[2048,16,128]{2,1,0:T(8,128)(2,1)} %gather_fusion, pred[2048]{0:T(1024)(128)(4,1)S(1)} %compare_and_fusion.2, pred[2048,128,1]{1,0,2:T(32,128)(4,1)S(1)} %fusion.222), kind=kOutput, calls=%fused_computation.1.clone.1 | convolution fusion | flops 12582912 | bytes 8718336 | tf_op jit(solution)/shard_map/while/body/eval_jaxpr/pcl,pl->pc/dot_general | solution.py:138
  393.8 16.3 %gather_fusion = bf16[2048,16,128]{2,1,0:T(8,128)(2,1)} fusion(bf16[512,16,128]{2,1,0:T(8,128)(2,1)S(1)} %get-tuple-element.155, s32[2048]{0:T(1024)S(1)} %broadcast_clamp_fusion.2), kind=kCustom, calls=%fused_computation.clone.1 | custom fusion | bytes 16785408 | tf_op jit(solution)/shard_map/while/body/eval_jaxpr/jit(_take)/gather | solution.py:135
  410.4 14.4 %fusion.223 = bf16[2048,1,16]{2,1,0:T(2,128)(2,1)S(1)} fusion(bf16[2048,16,128]{2,1,0:T(8,128)(2,1)} %gather_fusion, pred[2048]{0:T(1024)(128)(4,1)S(1)} %compare_and_fusion.2, pred[2048,128,1]{1,0,2:T(32,128)(4,1)S(1)} %fusion.222), kind=kOutput, calls=%fused_computation.1.clone.1 | convolution fusion | flops 12582912 | bytes 8718336 | tf_op jit(solution)/shard_map/while/body/eval_jaxpr/pcl,pl->pc/dot_general | solution.py:138
  426.0 16.3 %gather_fusion = bf16[2048,16,128]{2,1,0:T(8,128)(2,1)} fusion(bf16[512,16,128]{2,1,0:T(8,128)(2,1)S(1)} %get-tuple-element.155, s32[2048]{0:T(1024)S(1)} %broadcast_clamp_fusion.2), kind=kCustom, calls=%fused_computation.clone.1 | custom fusion | bytes 16785408 | tf_op jit(solution)/shard_map/while/body/eval_jaxpr/jit(_take)/gather | solution.py:135
  442.6 14.4 %fusion.223 = bf16[2048,1,16]{2,1,0:T(2,128)(2,1)S(1)} fusion(bf16[2048,16,128]{2,1,0:T(8,128)(2,1)} %gather_fusion, pred[2048]{0:T(1024)(128)(4,1)S(1)} %compare_and_fusion.2, pred[2048,128,1]{1,0,2:T(32,128)(4,1)S(1)} %fusion.222), kind=kOutput, calls=%fused_computation.1.clone.1 | convolution fusion | flops 12582912 | bytes 8718336 | tf_op jit(solution)/shard_map/while/body/eval_jaxpr/pcl,pl->pc/dot_general | solution.py:138
  458.2 16.3 %gather_fusion = bf16[2048,16,128]{2,1,0:T(8,128)(2,1)} fusion(bf16[512,16,128]{2,1,0:T(8,128)(2,1)S(1)} %get-tuple-element.155, s32[2048]{0:T(1024)S(1)} %broadcast_clamp_fusion.2), kind=kCustom, calls=%fused_computation.clone.1 | custom fusion | bytes 16785408 | tf_op jit(solution)/shard_map/while/body/eval_jaxpr/jit(_take)/gather | solution.py:135
  474.9 14.4 %fusion.223 = bf16[2048,1,16]{2,1,0:T(2,128)(2,1)S(1)} fusion(bf16[2048,16,128]{2,1,0:T(8,128)(2,1)} %gather_fusion, pred[2048]{0:T(1024)(128)(4,1)S(1)} %compare_and_fusion.2, pred[2048,128,1]{1,0,2:T(32,128)(4,1)S(1)} %fusion.222), kind=kOutput, calls=%fused_computation.1.clone.1 | convolution fusion | flops 12582912 | bytes 8718336 | tf_op jit(solution)/shard_map/while/body/eval_jaxpr/pcl,pl->pc/dot_general | solution.py:138
  490.5 16.3 %gather_fusion = bf16[2048,16,128]{2,1,0:T(8,128)(2,1)} fusion(bf16[512,16,128]{2,1,0:T(8,128)(2,1)S(1)} %get-tuple-element.155, s32[2048]{0:T(1024)S(1)} %broadcast_clamp_fusion.2), kind=kCustom, calls=%fused_computation.clone.1 | custom fusion | bytes 16785408 | tf_op jit(solution)/shard_map/while/body/eval_jaxpr/jit(_take)/gather | solution.py:135
  507.1 14.4 %fusion.223 = bf16[2048,1,16]{2,1,0:T(2,128)(2,1)S(1)} fusion(bf16[2048,16,128]{2,1,0:T(8,128)(2,1)} %gather_fusion, pred[2048]{0:T(1024)(128)(4,1)S(1)} %compare_and_fusion.2, pred[2048,128,1]{1,0,2:T(32,128)(4,1)S(1)} %fusion.222), kind=kOutput, calls=%fused_computation.1.clone.1 | convolution fusion | flops 12582912 | bytes 8718336 | tf_op jit(solution)/shard_map/while/body/eval_jaxpr/pcl,pl->pc/dot_general | solution.py:138
  522.7 16.3 %gather_fusion = bf16[2048,16,128]{2,1,0:T(8,128)(2,1)} fusion(bf16[512,16,128]{2,1,0:T(8,128)(2,1)S(1)} %get-tuple-element.155, s32[2048]{0:T(1024)S(1)} %broadcast_clamp_fusion.2), kind=kCustom, calls=%fused_computation.clone.1 | custom fusion | bytes 16785408 | tf_op jit(solution)/shard_map/while/body/eval_jaxpr/jit(_take)/gather | solution.py:135
  539.3 14.4 %fusion.223 = bf16[2048,1,16]{2,1,0:T(2,128)(2,1)S(1)} fusion(bf16[2048,16,128]{2,1,0:T(8,128)(2,1)} %gather_fusion, pred[2048]{0:T(1024)(128)(4,1)S(1)} %compare_and_fusion.2, pred[2048,128,1]{1,0,2:T(32,128)(4,1)S(1)} %fusion.222), kind=kOutput, calls=%fused_computation.1.clone.1 | convolution fusion | flops 12582912 | bytes 8718336 | tf_op jit(solution)/shard_map/while/body/eval_jaxpr/pcl,pl->pc/dot_general | solution.py:138
  554.9 16.3 %gather_fusion = bf16[2048,16,128]{2,1,0:T(8,128)(2,1)} fusion(bf16[512,16,128]{2,1,0:T(8,128)(2,1)S(1)} %get-tuple-element.155, s32[2048]{0:T(1024)S(1)} %broadcast_clamp_fusion.2), kind=kCustom, calls=%fused_computation.clone.1 | custom fusion | bytes 16785408 | tf_op jit(solution)/shard_map/while/body/eval_jaxpr/jit(_take)/gather | solution.py:135
  571.5 14.4 %fusion.223 = bf16[2048,1,16]{2,1,0:T(2,128)(2,1)S(1)} fusion(bf16[2048,16,128]{2,1,0:T(8,128)(2,1)} %gather_fusion, pred[2048]{0:T(1024)(128)(4,1)S(1)} %compare_and_fusion.2, pred[2048,128,1]{1,0,2:T(32,128)(4,1)S(1)} %fusion.222), kind=kOutput, calls=%fused_computation.1.clone.1 | convolution fusion | flops 12582912 | bytes 8718336 | tf_op jit(solution)/shard_map/while/body/eval_jaxpr/pcl,pl->pc/dot_general | solution.py:138
  587.1 16.3 %gather_fusion = bf16[2048,16,128]{2,1,0:T(8,128)(2,1)} fusion(bf16[512,16,128]{2,1,0:T(8,128)(2,1)S(1)} %get-tuple-element.155, s32[2048]{0:T(1024)S(1)} %broadcast_clamp_fusion.2), kind=kCustom, calls=%fused_computation.clone.1 | custom fusion | bytes 16785408 | tf_op jit(solution)/shard_map/while/body/eval_jaxpr/jit(_take)/gather | solution.py:135
  603.8 14.4 %fusion.223 = bf16[2048,1,16]{2,1,0:T(2,128)(2,1)S(1)} fusion(bf16[2048,16,128]{2,1,0:T(8,128)(2,1)} %gather_fusion, pred[2048]{0:T(1024)(128)(4,1)S(1)} %compare_and_fusion.2, pred[2048,128,1]{1,0,2:T(32,128)(4,1)S(1)} %fusion.222), kind=kOutput, calls=%fused_computation.1.clone.1 | convolution fusion | flops 12582912 | bytes 8718336 | tf_op jit(solution)/shard_map/while/body/eval_jaxpr/pcl,pl->pc/dot_general | solution.py:138
  619.4 16.3 %gather_fusion = bf16[2048,16,128]{2,1,0:T(8,128)(2,1)} fusion(bf16[512,16,128]{2,1,0:T(8,128)(2,1)S(1)} %get-tuple-element.155, s32[2048]{0:T(1024)S(1)} %broadcast_clamp_fusion.2), kind=kCustom, calls=%fused_computation.clone.1 | custom fusion | bytes 16785408 | tf_op jit(solution)/shard_map/while/body/eval_jaxpr/jit(_take)/gather | solution.py:135
  636.0 14.4 %fusion.223 = bf16[2048,1,16]{2,1,0:T(2,128)(2,1)S(1)} fusion(bf16[2048,16,128]{2,1,0:T(8,128)(2,1)} %gather_fusion, pred[2048]{0:T(1024)(128)(4,1)S(1)} %compare_and_fusion.2, pred[2048,128,1]{1,0,2:T(32,128)(4,1)S(1)} %fusion.222), kind=kOutput, calls=%fused_computation.1.clone.1 | convolution fusion | flops 12582912 | bytes 8718336 | tf_op jit(solution)/shard_map/while/body/eval_jaxpr/pcl,pl->pc/dot_general | solution.py:138
  651.6 16.3 %gather_fusion = bf16[2048,16,128]{2,1,0:T(8,128)(2,1)} fusion(bf16[512,16,128]{2,1,0:T(8,128)(2,1)S(1)} %get-tuple-element.155, s32[2048]{0:T(1024)S(1)} %broadcast_clamp_fusion.2), kind=kCustom, calls=%fused_computation.clone.1 | custom fusion | bytes 16785408 | tf_op jit(solution)/shard_map/while/body/eval_jaxpr/jit(_take)/gather | solution.py:135
  668.2 14.4 %fusion.223 = bf16[2048,1,16]{2,1,0:T(2,128)(2,1)S(1)} fusion(bf16[2048,16,128]{2,1,0:T(8,128)(2,1)} %gather_fusion, pred[2048]{0:T(1024)(128)(4,1)S(1)} %compare_and_fusion.2, pred[2048,128,1]{1,0,2:T(32,128)(4,1)S(1)} %fusion.222), kind=kOutput, calls=%fused_computation.1.clone.1 | convolution fusion | flops 12582912 | bytes 8718336 | tf_op jit(solution)/shard_map/while/body/eval_jaxpr/pcl,pl->pc/dot_general | solution.py:138
  689.3 11.4 %all-to-all-start = ((bf16[128,4,16,128]{3,2,1,0:T(8,128)(2,1)}), bf16[128,4,16,128]{3,2,1,0:T(8,128)(2,1)S(1)}, u32[]{:S(2)}, u32[]{:S(2)}) async-start(bf16[128,4,16,128]{3,2,1,0:T(8,128)(2,1)} %bitcast.345), calls=%async_computation | async-start | bytes 4194304 | tf_op jit(solution)/shard_map/all_to_all | solution.py:182
  704.4 27.0 %all-to-all-done = bf16[128,4,16,128]{3,2,1,0:T(8,128)(2,1)S(1)} async-done(((bf16[128,4,16,128]{3,2,1,0:T(8,128)(2,1)}), bf16[128,4,16,128]{3,2,1,0:T(8,128)(2,1)S(1)}, u32[]{:S(2)}, u32[]{:S(2)}) %all-to-all-start) | async-done | bytes 2097184 | tf_op jit(solution)/shard_map/all_to_all | solution.py:182
  (169 shorter events, 70.6 us)
Async XLA Ops:
  0.6 46.2 %copy-start.3 = (s32[256,128]{1,0:T(8,128)S(1)}, s32[256,128]{1,0:T(8,128)}, u32[]{:S(2)}) copy-start(s32[256,128]{1,0:T(8,128)} %param.8) | copy-start | bytes 393220
  1.6 39.2 %collective-permute-start = (bf16[6,64,128]{2,1,0:T(8,128)(2,1)S(1)}, bf16[6,64,128]{2,1,0:T(8,128)(2,1)S(1)}, u32[]{:S(2)}, u32[]{:S(2)}) collective-permute-start(bf16[6,64,128]{2,1,0:T(8,128)(2,1)S(1)} %get-tuple-element.80), channel_id=1, source_target_pairs={{0,4},{4,8},{8,12},{12,16},{16,20},{20,24},{24,28},{28,32},{32,36}... | collective-permute-start | bytes 294920 | tf_op jit(solution)/shard_map/ppermute | solution.py:22
  6.2 35.6 %collective-permute-start.1 = (bf16[6,64,128]{2,1,0:T(8,128)(2,1)S(1)}, bf16[6,64,128]{2,1,0:T(8,128)(2,1)S(1)}, u32[]{:S(2)}, u32[]{:S(2)}) collective-permute-start(bf16[6,64,128]{2,1,0:T(8,128)(2,1)S(1)} %get-tuple-element.79), channel_id=1, source_target_pairs={{4,0},{8,4},{12,8},{16,12},{20,16},{24,20},{28,24},{32,28},{36,32}... | collective-permute-start | bytes 294920 | tf_op jit(solution)/shard_map/ppermute | solution.py:25
  41.9 5.1 collective-permute-start.2
  45.4 4.9 collective-permute-start.3
  141.5 25.7 %copy-start = (bf16[8,8,64,128]{3,0,2,1:T(8,128)(2,1)}, bf16[8,8,64,128]{3,0,2,1:T(8,128)(2,1)S(1)}, u32[]{:S(2)}) copy-start(bf16[8,8,64,128]{3,0,2,1:T(8,128)(2,1)S(1)} %fusion.16) | copy-start | bytes 3145732
  167.2 1.0 copy-start.2
  689.3 11.6 %copy-start.1 = (bf16[8,8,64,128]{3,0,2,1:T(8,128)(2,1)S(1)}, bf16[8,8,64,128]{3,0,2,1:T(8,128)(2,1)}, u32[]{:S(2)}) copy-start(bf16[8,8,64,128]{3,0,2,1:T(8,128)(2,1)} %copy-done) | copy-start | bytes 3145732
  689.3 42.0 %all-to-all-start = ((bf16[128,4,16,128]{3,2,1,0:T(8,128)(2,1)}), bf16[128,4,16,128]{3,2,1,0:T(8,128)(2,1)S(1)}, u32[]{:S(2)}, u32[]{:S(2)}) async-start(bf16[128,4,16,128]{3,2,1,0:T(8,128)(2,1)} %bitcast.345), calls=%async_computation | async-start | bytes 4194304 | tf_op jit(solution)/shard_map/all_to_all | solution.py:182
where the time goes:
time: 736 us; the launch traced here: 733 us
  local copies, waits for them, and re-layouts  289 us (39%)
  matrix products  239 us (32%)
  other arithmetic  150 us (20%)
  waiting for transfers between devices  30.4 us (4%)
  starting transfers between devices  22.7 us (3%)
    gather x16, local copies, waits for them, and re-layouts, pick_block(): rows_taken = jnp.take(grouped, row_index, axis=0)  260 us
    dot_general x16, matrix products, pick_block(): jnp.einsum('pcl,pl->pc', rows_taken, selector, preferred_element_type=jnp...  230 us
    add x12, other arithmetic, pass_along(): summed = contribution if summed is None else summed + contribution  54.8 us
    unnamed x10, other arithmetic  46.4 us
    another operation x8, other arithmetic  28 us
    all_to_all x1, waiting for transfers between devices, per_device(): lax.all_to_all(outgoing, ('wide', 'narrow'), split_axis=0, concat_axis=0,...  27 us
  transfers between devices with their start and end apart: 5, of which 2 were waited for; matrix products, arithmetic and copies ran while one was open for 5% of the time, Pallas kernels for 0%

commit v1 on v0

v1 whole, which is shorter than its diff:
```python
import jax
import jax.numpy as jnp
import ml_dtypes
import numpy as np
from jax import lax
from jax.experimental import pallas as pl
from jax.experimental.pallas import tpu as pltpu
from jax.sharding import PartitionSpec as P

TAPS_PER_SIDE = 3
SPACINGS = (1, 2)
CAP = 4
BORDER = 6
Y_PAD = 8
RESPONSE_GAIN = 6.0
SMOOTH_SIGMA = 4.0

SZ, CY, NX = 8, 64, 128
ROWS = SZ * CY
DEEP = SZ + 2 * BORDER
TALL = CY + 2 * Y_PAD
COMPS = 6
LANES = 128
TILES = 256
PTS = 128
STEP_TILES = 16
STEPS = TILES // STEP_TILES
OWNERS = 128
SLOTS = OWNERS * CAP
SEND_ROWS = CAP * 2 * COMPS

KINDS = ((2, 0, 0), (0, 2, 0), (0, 0, 2), (1, 1, 0), (1, 0, 1), (0, 1, 1))


def tap_table():
    offsets = np.arange(-TAPS_PER_SIDE, TAPS_PER_SIDE + 1).astype(np.float32)
    bell = np.exp(np.float32(-0.5) * offsets * offsets)
    normalized = bell / np.sum(bell)
    taps = np.stack([normalized, -offsets * normalized, (offsets * offsets - 1.0) * normalized])
    return taps.astype(ml_dtypes.bfloat16).astype(np.float32)


TAPS = tap_table()


def band(kind, spacing, rows_in, count_out, start):
    result = np.zeros((count_out, rows_in), np.float32)
    for tap in range(2 * TAPS_PER_SIDE + 1):
        shift = (tap - TAPS_PER_SIDE) * spacing
        for out in range(count_out):
            source = out + start - shift
            if 0 <= source < rows_in:
                result[out, source] += TAPS[kind, tap]
    return result


def y_bands():
    return np.concatenate(
        [band(kind, d, TALL, CY, Y_PAD) for d in SPACINGS for kind in range(3)], axis=0
    ).astype(ml_dtypes.bfloat16)


def x_bands():
    return np.stack(
        [np.stack([band(kind, d, NX, NX, 0).T for kind in range(3)]) for d in SPACINGS]
    ).astype(ml_dtypes.bfloat16)


def table_bands():
    bands = np.stack([np.stack([band(kind, d, NX, NX, 0).T for kind in range(3)]) for d in SPACINGS])
    result = np.zeros((2, COMPS, NX, NX * 8), np.float32)
    for s in range(2):
        for x in range(NX):
            half = ((x // 8) % 2) ^ s
            column = (x // 16) * 128 + half * 64 + (x % 8) * 8
            for comp in range(COMPS):
                result[s, comp, :, column + comp] = bands[s, KINDS[comp][0], :, x]
    return result.reshape(2, COMPS * NX, NX * 8).astype(ml_dtypes.bfloat16)


def pack_matrix():
    result = np.zeros((4 * SEND_ROWS, 4 * CAP * 16), np.float32)
    for slot in range(4 * CAP):
        for s in range(2):
            for comp in range(COMPS):
                result[slot * 12 + s * COMPS + comp, slot * 16 + s * 8 + comp] = 1.0
    return result.astype(ml_dtypes.bfloat16)


def z_pass(y_fields, s, kind_y, kinds_z, z):
    d = SPACINGS[s]
    planes = [y_fields[z + BORDER - k * d, s, kind_y] for k in range(-TAPS_PER_SIDE, TAPS_PER_SIDE + 1)]
    results = {}
    for kind in kinds_z:
        total = None
        for side in range(TAPS_PER_SIDE):
            pair = planes[side] - planes[6 - side] if kind == 1 else planes[side] + planes[6 - side]
            if TAPS[kind, side] == 0.0:
                continue
            term = float(TAPS[kind, side]) * pair
            total = term if total is None else total + term
        if kind != 1:
            total = total + float(TAPS[kind, TAPS_PER_SIDE]) * planes[TAPS_PER_SIDE]
        results[kind] = total
    return results


def sample_kernel(
    slot_ref, rows_hbm, block_ref, low_ref, high_ref, left_ref, right_ref, column_ref, y_band_ref, table_band_ref,
    smoother_ref, pack_ref, send_ref, fields_ref, ext, y_fields, table, tiles, index_rows, sem, *gathered
):
    def copy_rows(step, side):
        return pltpu.make_async_copy(
            rows_hbm.at[pl.ds(pl.multiple_of(step * STEP_TILES, STEP_TILES), STEP_TILES)], index_rows[side], sem.at[side]
        )

    copy_rows(0, 0).start()
    copy_rows(1, 1).start()

    ext[BORDER:BORDER + SZ, Y_PAD:Y_PAD + CY, :] = block_ref[...]
    ext[0:BORDER, Y_PAD:Y_PAD + CY, :] = low_ref[...]
    ext[BORDER + SZ:DEEP, Y_PAD:Y_PAD + CY, :] = high_ref[...]
    ext[:, 0:Y_PAD, :] = left_ref[...]
    ext[:, Y_PAD + CY:TALL, :] = right_ref[...]
    tiles[...] = jnp.zeros_like(tiles)
    gathered[1][...] = jnp.zeros_like(gathered[1])

    for z in range(0, DEEP, 2):
        pair = jnp.concatenate([ext[z], ext[z + 1]], axis=1)
        out = jnp.dot(y_band_ref[...], pair, preferred_element_type=jnp.float32)
        for s in range(2):
            for kind in range(3):
                rows = slice((s * 3 + kind) * CY, (s * 3 + kind + 1) * CY)
                y_fields[z, s, kind] = out[rows, 0:NX]
                y_fields[z + 1, s, kind] = out[rows, NX:2 * NX]

    for s in range(2):
        for z in range(SZ):
            passed = [z_pass(y_fields, s, 0, (0, 1, 2), z), z_pass(y_fields, s, 1, (0, 1), z), z_pass(y_fields, s, 2, (0,), z)]
            for comp, (_, kind_y, kind_z) in enumerate(KINDS):
                fields_ref[s, z * CY:(z + 1) * CY, comp * NX:(comp + 1) * NX] = passed[kind_y][kind_z].astype(jnp.bfloat16)

    lower = lax.broadcasted_iota(jnp.int32, (ROWS, LANES), 1) < 64
    for m in range(0, NX // 16, 2):
        outs = [
            jnp.dot(fields_ref[s], table_band_ref[s, :, m * 128:(m + 2) * 128], preferred_element_type=jnp.float32)
            for s in range(2)
        ]
        for half in range(2):
            first, second = (out[:, half * 128:(half + 1) * 128] for out in outs)
            group = (m + half) * 2
            table[group * ROWS:(group + 1) * ROWS, :] = jnp.where(lower, first, second)
            table[(group + 1) * ROWS:(group + 2) * ROWS, :] = jnp.where(lower, second, first)

    eye = (
        lax.broadcasted_iota(jnp.int32, (LANES, LANES), 0) == lax.broadcasted_iota(jnp.int32, (LANES, LANES), 1)
    ).astype(jnp.bfloat16)

    def gather(step, side):
        copy_rows(0, side).wait()
        for tile in range(STEP_TILES):
            for p in range(PTS):
                row = index_rows[side][tile, p]
                gathered[side][pl.ds(tile * PTS + p, 1), :] = table[pl.ds(row, 1), :]
        copy_rows(jnp.minimum(step + 2, STEPS - 1), side).start()

    def finish(step, side):
        flat = gathered[side][...].astype(jnp.bfloat16)
        turned = lax.dot_general(eye, flat, (((1,), (1,)), ((), ())), preferred_element_type=jnp.float32)
        picked = []
        for tile in range(STEP_TILES):
            column = column_ref[pl.ds(jnp.maximum(step, 0) * STEP_TILES + tile, 1), :]
            column = jnp.broadcast_to(column, (8, PTS))
            here = turned[:, tile * PTS:(tile + 1) * PTS]
            lane = [(0, 64), (64, 0)]
            both = [here[0:8], here[64:72]]
            for x in range(1, 16):
                hit = column == x
                for s in range(2):
                    start = lane[x // 8][s] + (x % 8) * 8
                    both[s] = jnp.where(hit, here[start:start + 8], both[s])
            picked.append(jnp.concatenate(both, axis=0).astype(jnp.bfloat16))
        smooth = jnp.dot(
            jnp.concatenate(picked, axis=0), smoother_ref[...], preferred_element_type=jnp.float32
        ).astype(jnp.bfloat16)
        for tile in range(STEP_TILES):
            tiles[slot_ref[(step + 1) * STEP_TILES + tile]] = smooth[tile * 16:(tile + 1) * 16]

    @pl.loop(0, STEPS // 2)
    def _(i):
        gather(2 * i, 0)
        finish(2 * i - 1, 1)
        gather(2 * i + 1, 1)
        finish(2 * i, 0)

    finish(STEPS - 1, 1)
    copy_rows(0, 0).wait()
    copy_rows(0, 1).wait()

    @pl.loop(0, OWNERS // 4)
    def _(quad):
        here = tiles[pl.ds(quad * 16, 16)].reshape(256, PTS)
        packed = jnp.dot(pack_ref[...], here, preferred_element_type=jnp.float32).astype(jnp.bfloat16)
        send_ref[pl.ds(pl.multiple_of(quad * 4 * SEND_ROWS, 4 * SEND_ROWS), 4 * SEND_ROWS), :] = packed


def response_kernel(weight_ref, fields_ref, x_band_ref, out_ref):
    for s in range(2):
        parts = [
            jnp.dot(
                fields_ref[s, :, comp * NX:(comp + 1) * NX], x_band_ref[s, KINDS[comp][0]], preferred_element_type=jnp.float32
            )
            for comp in range(COMPS)
        ]
        for o in range(8):
            total = parts[0] * weight_ref[o, 0]
            for comp in range(1, COMPS):
                total = total + parts[comp] * weight_ref[o, comp]
            out_ref[s * 8 + o, 0] = total.astype(jnp.bfloat16)


def mix_kernel(high_ref, low_ref, arrived_ref, out_ref):
    here = arrived_ref[...]
    for quad in range(8):
        part = here[quad * 4 * SEND_ROWS:(quad + 1) * 4 * SEND_ROWS]
        mixed = jnp.dot(high_ref[...], part, preferred_element_type=jnp.float32)
        mixed = mixed + jnp.dot(low_ref[...], part, preferred_element_type=jnp.float32)
        out_ref[quad * 256:(quad + 1) * 256, :] = mixed.astype(jnp.bfloat16)


def orientation_weights(angles):
    polar_angle = angles[0]
    azimuth = angles[1]
    dir_x = jnp.sin(polar_angle) * jnp.cos(azimuth)
    dir_y = jnp.sin(polar_angle) * jnp.sin(azimuth)
    dir_z = jnp.cos(polar_angle)
    return RESPONSE_GAIN * jnp.stack(
        [
            dir_x * dir_x,
            dir_y * dir_y,
            dir_z * dir_z,
            2.0 * dir_x * dir_y,
            2.0 * dir_x * dir_z,
            2.0 * dir_y * dir_z,
        ],
        axis=1,
    )


def smooth_matrix():
    source = np.arange(PTS, dtype=np.float32)[:, None]
    target = np.arange(PTS, dtype=np.float32)[None, :]
    distance = target - source
    bell = np.exp(-distance * distance / np.float32(2.0 * SMOOTH_SIGMA * SMOOTH_SIGMA))
    return (bell / np.sum(bell, axis=0, keepdims=True)).astype(ml_dtypes.bfloat16)


def shifted(value, axis, step):
    count = lax.axis_size(axis)
    forward = [(i, i + 1) for i in range(count - 1)]
    backward = [(i + 1, i) for i in range(count - 1)]
    return lax.ppermute(value, axis, forward if step > 0 else backward)


def mix_matrix(weights):
    scales = jnp.zeros((16, 12), jnp.float32)
    scales = scales.at[0:8, 0:6].set(weights).at[8:16, 6:12].set(weights)
    rows = lax.broadcasted_iota(jnp.int32, (256, 192), 0) // 16
    columns = lax.broadcasted_iota(jnp.int32, (256, 192), 1) // 12
    full = jnp.where(rows == columns, jnp.tile(scales, (16, 16)), 0.0)
    high = full.astype(jnp.bfloat16)
    low = (full - high.astype(jnp.float32)).astype(jnp.bfloat16)
    return high, low


def per_device(volume, angles, tile_points, tile_dest):
    low = shifted(volume[SZ - BORDER:], "wide", 1)
    high = shifted(volume[:BORDER], "wide", -1)
    edge_low = jnp.concatenate([part[:, CY - Y_PAD:] for part in (low, volume, high)], axis=0)
    edge_high = jnp.concatenate([part[:, :Y_PAD] for part in (low, volume, high)], axis=0)
    left = shifted(edge_low, "narrow", 1)
    right = shifted(edge_high, "narrow", -1)

    table_rows = ((tile_points >> 3) & 15) * ROWS + (tile_points >> 7)
    columns = tile_points & 15
    dest = tile_dest[:, 0]
    earlier = lax.broadcasted_iota(jnp.int32, (TILES, TILES), 0)
    later = lax.broadcasted_iota(jnp.int32, (TILES, TILES), 1)
    same_owner = (dest[:, None] == dest[None, :]) & (earlier < later)
    slot = dest * CAP + jnp.sum(same_owner.astype(jnp.int32), axis=0)
    slot = jnp.concatenate([jnp.full((STEP_TILES,), SLOTS, jnp.int32), slot])

    weights = orientation_weights(angles)
    mix_high, mix_low = mix_matrix(weights)

    vmem = pl.BlockSpec(memory_space=pltpu.VMEM)
    send, fields = pl.pallas_call(
        sample_kernel,
        out_shape=(
            jax.ShapeDtypeStruct((OWNERS * SEND_ROWS, PTS), jnp.bfloat16),
            jax.ShapeDtypeStruct((2, ROWS, COMPS * NX), jnp.bfloat16),
        ),
        in_specs=[pl.BlockSpec(memory_space=pltpu.SMEM), pl.BlockSpec(memory_space=pl.ANY)] + [vmem] * 10,
        out_specs=(vmem, vmem),
        scratch_shapes=[
            pltpu.VMEM((DEEP, TALL, NX), jnp.bfloat16),
            pltpu.VMEM((DEEP, 2, 3, CY, NX), jnp.float32),
            pltpu.VMEM((NX // 8 * ROWS, LANES), jnp.float32),
            pltpu.VMEM((SLOTS + 1, 16, PTS), jnp.bfloat16),
            [pltpu.SMEM((STEP_TILES, PTS), jnp.int32)] * 2,
            pltpu.SemaphoreType.DMA((2,)),
            pltpu.VMEM((STEP_TILES * PTS, LANES), jnp.float32),
            pltpu.VMEM((STEP_TILES * PTS, LANES), jnp.float32),
        ],
        compiler_params=pltpu.CompilerParams(vmem_limit_bytes=48 << 20),
        cost_estimate=pl.CostEstimate(flops=4_000_000_000, bytes_accessed=8_000_000, transcendentals=0),
        name="sample",
    )(
        slot, table_rows, volume, low, high, left, right, columns,
        jnp.asarray(y_bands()), jnp.asarray(table_bands()), jnp.asarray(smooth_matrix()), jnp.asarray(pack_matrix()),
    )

    arrived = lax.all_to_all(
        send.reshape(OWNERS, SEND_ROWS, PTS), ("wide", "narrow"), split_axis=0, concat_axis=0, tiled=True
    )

    responses = pl.pallas_call(
        response_kernel,
        grid=(SZ,),
        out_shape=jax.ShapeDtypeStruct((16, SZ, CY, NX), jnp.bfloat16),
        in_specs=[
            pl.BlockSpec(memory_space=pltpu.SMEM),
            pl.BlockSpec((2, CY, COMPS * NX), lambda z: (0, z, 0)),
            pl.BlockSpec((2, 3, NX, NX), lambda z: (0, 0, 0, 0)),
        ],
        out_specs=pl.BlockSpec((16, 1, CY, NX), lambda z: (0, z, 0, 0)),
        compiler_params=pltpu.CompilerParams(vmem_limit_bytes=16 << 20),
        cost_estimate=pl.CostEstimate(flops=200_000_000, bytes_accessed=4_000_000, transcendentals=0),
        name="respond",
    )(weights, fields, jnp.asarray(x_bands()))

    fibers = pl.pallas_call(
        mix_kernel,
        grid=(4,),
        out_shape=jax.ShapeDtypeStruct((SLOTS * 16, PTS), jnp.bfloat16),
        in_specs=[
            pl.BlockSpec((256, 192), lambda i: (0, 0)),
            pl.BlockSpec((256, 192), lambda i: (0, 0)),
            pl.BlockSpec((32 * SEND_ROWS, PTS), lambda i: (i, 0)),
        ],
        out_specs=pl.BlockSpec((SLOTS * 4, PTS), lambda i: (i, 0)),
        compiler_params=pltpu.CompilerParams(vmem_limit_bytes=16 << 20),
        cost_estimate=pl.CostEstimate(flops=1_600_000_000, bytes_accessed=4_000_000, transcendentals=0),
        name="mix",
    )(mix_high, mix_low, arrived.reshape(OWNERS * SEND_ROWS, PTS))
    return responses, fibers.reshape(OWNERS, CAP, 16, PTS)


def solution(mesh):
    return jax.shard_map(
        per_device,
        mesh=mesh,
        in_specs=(
            P("wide", "narrow", None),
            P(),
            P(("wide", "narrow"), None),
            P(("wide", "narrow"), None),
        ),
        out_specs=(P(None, "wide", "narrow", None), P(("wide", "narrow"), None, None, None)),
        check_vma=False,
    )
```

time: 736 us -> 102 us (0.14)
  local copies, waits for them, and re-layouts: 289 us -> 11.3 us
  matrix products: 239 us -> 0 us
  other arithmetic: 150 us -> 6.26 us
  Pallas kernels: 0 us -> 44.9 us
  waiting for transfers between devices: 30.4 us -> 14.8 us
    gather x16 -> x0, local copies, waits for them, and re-layouts: 260 us -> none  [pick_block(): rows_taken = jnp.take(grouped, row_index, axis=0)]
    dot_general x22 -> x0, matrix products: 239 us -> none  [the longest x16 230 us: pick_block(): jnp.einsum('pcl,pl->pc', rows_taken, selector, preferred_element_type=jnp...]
    add x13 -> x1, other arithmetic: 55.5 us -> 0.69 us  [per_device(): slot = dest * CAP + jnp.sum(same_owner.astype(jnp.int32), axis=0)]
    unnamed x10 -> x0, other arithmetic: 46.4 us -> none
    pallas_call x0 -> x3, Pallas kernels: none -> 44.9 us  [the longest x1 35.8 us: per_device(): pl.pallas_call(sample_kernel, out_shape=(jax.ShapeDtypeStruct((OWNERS * S...]
    another operation x10 -> x0, other arithmetic: 37.1 us -> none
    all_to_all x1, waiting for transfers between devices: 27 us -> 11.4 us  [per_device(): lax.all_to_all(send.reshape(OWNERS, SEND_ROWS, PTS), ('wide', 'narrow'),...]
    dynamic_update_slice x16 -> x0, local copies, waits for them, and re-layouts: 10.3 us -> none  [sample_tiles(): picked = lax.map(pick_block, point_blocks)]
  transfers between devices with their start and end apart: 5 -> 5, of which waited for: 2 -> 2; matrix products, arithmetic and copies ran while one was open for 5% -> 12% of each run, Pallas kernels for 0% -> 5%
where the time goes in v1:
time: 102 us; the launch traced here: 101 us
  Pallas kernels  44.9 us (44%)
  starting transfers between devices  22.9 us (22%)
  waiting for transfers between devices  14.8 us (15%)
  local copies, waits for them, and re-layouts  11.3 us (11%)
  other arithmetic  6.26 us (6%)
    pallas_call x1, Pallas kernels, per_device(): pl.pallas_call(sample_kernel, out_shape=(jax.ShapeDtypeStruct((OWNERS * S...  35.8 us
    all_to_all x1, starting transfers between devices, per_device(): lax.all_to_all(send.reshape(OWNERS, SEND_ROWS, PTS), ('wide', 'narrow'),...  11.6 us
    all_to_all x1, waiting for transfers between devices, per_device(): lax.all_to_all(send.reshape(OWNERS, SEND_ROWS, PTS), ('wide', 'narrow'),...  11.4 us
    ppermute x4, starting transfers between devices, shifted(): return lax.ppermute(value, axis, forward if step > 0 else backward)  11.3 us
    pallas_call x1, Pallas kernels, per_device(): pl.pallas_call(response_kernel, grid=(SZ,), out_shape=jax.ShapeDtypeStruc...  5.39 us
    unnamed x12, local copies, waits for them, and re-layouts  4.35 us
    another operation x3, local copies, waits for them, and re-layouts, mix_matrix(): full = jnp.where(rows == columns, jnp.tile(scales, (16, 16)), 0.0)  4.15 us
    pallas_call x1, Pallas kernels, per_device(): pl.pallas_call(mix_kernel, grid=(4,), out_shape=jax.ShapeDtypeStruct((SLO...  3.71 us
  transfers between devices with their start and end apart: 5, of which 2 were waited for; matrix products, arithmetic and copies ran while one was open for 12% of the time, Pallas kernels for 5%

profile of v1, /device:TPU:1, one launch (start us, length us, event | category | flops | bytes accessed | tf_op | source)
XLA Modules:
  0.0 101.0 jit_solution(6793708915837337684)
XLA Ops:
  0.6 1.0 fusion.4
  1.6 3.3 %collective-permute-start.1 = (bf16[6,64,128]{2,1,0:T(8,128)(2,1)S(1)}, bf16[6,64,128]{2,1,0:T(8,128)(2,1)S(1)}, u32[]{:S(2)}, u32[]{:S(2)}) collective-permute-start(bf16[6,64,128]{2,1,0:T(8,128)(2,1)S(1)} %get-tuple-element.36), channel_id=1, source_target_pairs={{4,0},{8,4},{12,8},{16,12},{20,16},{24,20},{28,24},{32,28},{36,32}... | collective-permute-start | bytes 294920 | tf_op jit(solution)/shard_map/ppermute | solution.py:262
  5.0 3.1 %collective-permute-start = (bf16[6,64,128]{2,1,0:T(8,128)(2,1)S(1)}, bf16[6,64,128]{2,1,0:T(8,128)(2,1)S(1)}, u32[]{:S(2)}, u32[]{:S(2)}) collective-permute-start(bf16[6,64,128]{2,1,0:T(8,128)(2,1)S(1)} %get-tuple-element.37), channel_id=1, source_target_pairs={{0,4},{4,8},{8,12},{12,16},{16,20},{20,24},{24,28},{28,32},{32,36}... | collective-permute-start | bytes 294920 | tf_op jit(solution)/shard_map/ppermute | solution.py:262
  8.1 0.7 fusion.3
  8.8 0.9 convert_reduce_fusion
  9.7 0.9 broadcast_and_fusion
  10.6 0.7 multiply_add_fusion
  11.3 0.0 collective-permute-done.1.high_ref
  11.3 0.0 collective-permute-done.low_ref
  11.3 3.5 %collective-permute-start.2 = (bf16[20,8,128]{2,1,0:T(8,128)(2,1)S(1)}, bf16[20,8,128]{2,1,0:T(8,128)(2,1)S(1)}, u32[]{:S(2)}, u32[]{:S(2)}) collective-permute-start(bf16[20,8,128]{2,1,0:T(8,128)(2,1)S(1)} %pad_maximum_fusion), channel_id=1, source_target_pairs={{0,1},{1,2},{2,3},{4,5},{5,6},{6,7},{8,9},{9,10},{10,11},{12,13},{... | collective-permute-start | bytes 122888 | tf_op jit(solution)/shard_map/ppermute | solution.py:262
  14.9 1.3 %collective-permute-start.3 = (bf16[20,8,128]{2,1,0:T(8,128)(2,1)S(1)}, bf16[20,8,128]{2,1,0:T(8,128)(2,1)S(1)}, u32[]{:S(2)}, u32[]{:S(2)}) collective-permute-start(bf16[20,8,128]{2,1,0:T(8,128)(2,1)S(1)} %pad_maximum_fusion.1), channel_id=1, source_target_pairs={{1,0},{2,1},{3,2},{5,4},{6,5},{7,6},{9,8},{10,9},{11,10},{13,12},{... | collective-permute-start | bytes 122888 | tf_op jit(solution)/shard_map/ppermute | solution.py:262
  16.2 0.8 cosine_bitcast_fusion
  17.0 0.1 concatenate.13.slot_ref
  17.1 0.0 collective-permute-done.2.left_ref
  17.1 3.4 %collective-permute-done.3.right_ref = bf16[20,8,128]{2,1,0:T(8,128)(2,1)S(1)} collective-permute-done((bf16[20,8,128]{2,1,0:T(8,128)(2,1)S(1)}, bf16[20,8,128]{2,1,0:T(8,128)(2,1)S(1)}, u32[]{:S(2)}, u32[]{:S(2)}) %collective-permute-start.3) | collective-permute-done | bytes 40992 | tf_op jit(solution)/shard_map/ppermute | solution.py:262
  20.5 0.0 copy-start
  20.5 0.9 copy-done
  21.4 0.0 copy-start.3
  21.4 0.9 copy-done.3
  22.3 0.0 copy-start.4
  22.3 0.9 copy-done.4
  23.2 0.0 copy-start.5
  23.2 0.8 copy-done.5
  23.9 35.8 %sample.1 = (bf16[6144,128]{1,0:T(8,128)(2,1)}, bf16[2,512,768]{2,1,0:T(8,128)(2,1)S(1)}) custom-call(s32[272]{0:T(512)S(1)} %concatenate.13.slot_ref, s32[256,128]{1,0:T(8,128)S(1)} %get-tuple-element.33.rows_hbm, bf16[8,64,128]{2,1,0:T(8,128)(2,1)S(1)} %copy-done, bf16[6,64,128]{2,1,0:T(8,128)(2,1)S(1)} %collective-permute-done.low_ref, ...), custom_call_target="tpu_custom_call" | custom-call | flops 4000000000 | bytes 8000000 | tf_op jit(solution)/shard_map/sample/pallas_call | solution.py:297
  59.8 11.6 %all-to-all-start = ((bf16[128,48,128]{2,1,0:T(8,128)(2,1)}), bf16[128,48,128]{2,1,0:T(8,128)(2,1)S(1)}, u32[]{:S(2)}, u32[]{:S(2)}) async-start(bf16[128,48,128]{2,1,0:T(8,128)(2,1)} %bitcast.5), calls=%async_computation | async-start | bytes 3145728 | tf_op jit(solution)/shard_map/all_to_all | solution.py:323
  71.4 0.1 copy.45
  71.5 0.1 copy.37
  71.6 0.1 copy.35
  71.7 0.1 copy.39
  71.7 0.1 stack.2
  71.8 0.5 scatter.9
  72.4 0.1 copy.46
  72.4 1.3 %tile.4 = f32[16,16,16,12]{1,0,3,2:T(8,128)} broadcast(f32[16,12]{0,1:T(8,128)S(1)} %copy.46), dimensions={1,3} | broadcast | bytes 197376 | tf_op jit(solution)/shard_map/tile | solution.py:270
  73.7 0.0 copy-start.1
  73.7 2.0 %tile.10 = f32[256,192]{0,1:T(8,128)S(1)} reshape(f32[16,16,16,12]{1,0,3,2:T(8,128)} %tile.4) | data formatting | bytes 393216 | tf_op jit(solution)/shard_map/tile | solution.py:270
  75.8 0.8 copy.47
  76.6 1.1 %subtract_convert_fusion.low_ref = bf16[256,192]{1,0:T(8,128)(2,1)S(1)} fusion(f32[256,192]{1,0:T(8,128)} %copy.47, s32[192]{0:T(256)S(1)} %get-tuple-element.51, s32[192]{0:T(256)S(1)} %get-tuple-element.52, s32[256]{0:T(256)S(1)} %get-tuple-element.53, s32[256]{0:T(256)S(1)} %get-tuple-element.54, pred[256]{0:T(512)(128)(4,1)S(1)} %compare_and_fusion.1, ...), kind=kLoop, calls=%fused_computation | loop fusion | flops 393216 | bytes 298944 | tf_op jit(solution)/shard_map/convert_element_type | solution.py:272
  77.8 1.8 %fusion.2.high_ref = bf16[256,192]{1,0:T(8,128)(2,1)} fusion(f32[256,192]{1,0:T(8,128)} %copy.47, s32[192]{0:T(256)S(1)} %get-tuple-element.51, s32[192]{0:T(256)S(1)} %get-tuple-element.52, s32[256]{0:T(256)S(1)} %get-tuple-element.53, s32[256]{0:T(256)S(1)} %get-tuple-element.54, pred[256]{0:T(512)(128)(4,1)S(1)} %compare_and_fusion.1, ...), kind=kLoop, calls=%fused_computation.6 | loop fusion | flops 196608 | bytes 298944 | tf_op jit(solution)/shard_map/convert_element_type | solution.py:271
  79.5 0.0 copy-done.1
  79.5 5.4 %respond.1 = bf16[16,8,64,128]{3,2,1,0:T(8,128)(2,1)} custom-call(f32[8,6]{1,0:T(8,128)S(1)} %broadcast_multiply_fusion.weight_ref, bf16[2,512,768]{2,1,0:T(8,128)(2,1)S(1)} %get-tuple-element.28.fields_ref, bf16[2,3,128,128]{3,2,1,0:T(8,128)(2,1)S(1)} %copy-done.1), custom_call_target="tpu_custom_call" | custom-call | flops 200000000 | bytes 4000000 | tf_op jit(solution)/shard_map/respond/pallas_call | solution.py:327
  84.9 11.4 %all-to-all-done = bf16[128,48,128]{2,1,0:T(8,128)(2,1)S(1)} async-done(((bf16[128,48,128]{2,1,0:T(8,128)(2,1)}), bf16[128,48,128]{2,1,0:T(8,128)(2,1)S(1)}, u32[]{:S(2)}, u32[]{:S(2)}) %all-to-all-start) | async-done | bytes 1572896 | tf_op jit(solution)/shard_map/all_to_all | solution.py:323
  96.3 0.0 copy-start.2
  96.4 0.9 copy-done.2
  97.3 3.7 %mix.1 = bf16[8192,128]{1,0:T(8,128)(2,1)} custom-call(bf16[256,192]{1,0:T(8,128)(2,1)S(1)} %copy-done.2, bf16[256,192]{1,0:T(8,128)(2,1)S(1)} %subtract_convert_fusion.low_ref, bf16[6144,128]{1,0:T(8,128)(2,1)S(1)} %bitcast.16), custom_call_target="tpu_custom_call" | custom-call | flops 1600000000 | bytes 4000000 | tf_op jit(solution)/shard_map/mix/pallas_call | solution.py:342
  (12 shorter events, 0.1 us)
Async XLA Ops:
  1.6 9.7 %collective-permute-start.1 = (bf16[6,64,128]{2,1,0:T(8,128)(2,1)S(1)}, bf16[6,64,128]{2,1,0:T(8,128)(2,1)S(1)}, u32[]{:S(2)}, u32[]{:S(2)}) collective-permute-start(bf16[6,64,128]{2,1,0:T(8,128)(2,1)S(1)} %get-tuple-element.36), channel_id=1, source_target_pairs={{4,0},{8,4},{12,8},{16,12},{20,16},{24,20},{28,24},{32,28},{36,32}... | collective-permute-start | bytes 294920 | tf_op jit(solution)/shard_map/ppermute | solution.py:262
  5.0 6.4 %collective-permute-start = (bf16[6,64,128]{2,1,0:T(8,128)(2,1)S(1)}, bf16[6,64,128]{2,1,0:T(8,128)(2,1)S(1)}, u32[]{:S(2)}, u32[]{:S(2)}) collective-permute-start(bf16[6,64,128]{2,1,0:T(8,128)(2,1)S(1)} %get-tuple-element.37), channel_id=1, source_target_pairs={{0,4},{4,8},{8,12},{12,16},{16,20},{20,24},{24,28},{28,32},{32,36}... | collective-permute-start | bytes 294920 | tf_op jit(solution)/shard_map/ppermute | solution.py:262
  11.3 5.8 %collective-permute-start.2 = (bf16[20,8,128]{2,1,0:T(8,128)(2,1)S(1)}, bf16[20,8,128]{2,1,0:T(8,128)(2,1)S(1)}, u32[]{:S(2)}, u32[]{:S(2)}) collective-permute-start(bf16[20,8,128]{2,1,0:T(8,128)(2,1)S(1)} %pad_maximum_fusion), channel_id=1, source_target_pairs={{0,1},{1,2},{2,3},{4,5},{5,6},{6,7},{8,9},{9,10},{10,11},{12,13},{... | collective-permute-start | bytes 122888 | tf_op jit(solution)/shard_map/ppermute | solution.py:262
  14.9 5.6 %collective-permute-start.3 = (bf16[20,8,128]{2,1,0:T(8,128)(2,1)S(1)}, bf16[20,8,128]{2,1,0:T(8,128)(2,1)S(1)}, u32[]{:S(2)}, u32[]{:S(2)}) collective-permute-start(bf16[20,8,128]{2,1,0:T(8,128)(2,1)S(1)} %pad_maximum_fusion.1), channel_id=1, source_target_pairs={{1,0},{2,1},{3,2},{5,4},{6,5},{7,6},{9,8},{10,9},{11,10},{13,12},{... | collective-permute-start | bytes 122888 | tf_op jit(solution)/shard_map/ppermute | solution.py:262
  20.5 0.9 copy-start
  21.4 0.9 copy-start.3
  22.3 0.9 copy-start.4
  23.2 0.8 copy-start.5
  59.8 36.6 %all-to-all-start = ((bf16[128,48,128]{2,1,0:T(8,128)(2,1)}), bf16[128,48,128]{2,1,0:T(8,128)(2,1)S(1)}, u32[]{:S(2)}, u32[]{:S(2)}) async-start(bf16[128,48,128]{2,1,0:T(8,128)(2,1)} %bitcast.5), calls=%async_computation | async-start | bytes 3145728 | tf_op jit(solution)/shard_map/all_to_all | solution.py:323
  73.7 5.8 %copy-start.1 = (bf16[2,3,128,128]{3,2,1,0:T(8,128)(2,1)S(1)}, bf16[2,3,128,128]{3,2,1,0:T(8,128)(2,1)}, u32[]{:S(2)}) copy-start(bf16[2,3,128,128]{3,2,1,0:T(8,128)(2,1)} %constant.112.clone.x_band_ref) | copy-start | bytes 589828
  96.3 0.9 copy-start.2

commit v2 on v1

--- a/solution.py
+++ b/solution.py
@@ -28,6 +28,7 @@
 OWNERS = 128
 SLOTS = OWNERS * CAP
 SEND_ROWS = CAP * 2 * COMPS
+MIX_PARTS = 4
 
 KINDS = ((2, 0, 0), (0, 2, 0), (0, 0, 2), (1, 1, 0), (1, 0, 1), (0, 1, 1))
 
@@ -67,15 +68,14 @@
 
 
 def table_bands():
-    bands = np.stack([np.stack([band(kind, d, NX, NX, 0).T for kind in range(3)]) for d in SPACINGS])
-    result = np.zeros((2, COMPS, NX, NX * 8), np.float32)
+    result = np.zeros((2, COMPS, 48, LANES), np.float32)
     for s in range(2):
-        for x in range(NX):
-            half = ((x // 8) % 2) ^ s
-            column = (x // 16) * 128 + half * 64 + (x % 8) * 8
+        for x in range(16):
+            column = ((x // 8) ^ s) * 64 + (x % 8) * 8
             for comp in range(COMPS):
-                result[s, comp, :, column + comp] = bands[s, KINDS[comp][0], :, x]
-    return result.reshape(2, COMPS * NX, NX * 8).astype(ml_dtypes.bfloat16)
+                bands = band(KINDS[comp][0], SPACINGS[s], 48, 48, 0)
+                result[s, comp, :, column + comp] = bands[x + 16]
+    return result.astype(ml_dtypes.bfloat16)
 
 
 def pack_matrix():
@@ -106,33 +106,54 @@
 
 
 def sample_kernel(
-    slot_ref, rows_hbm, block_ref, low_ref, high_ref, left_ref, right_ref, column_ref, y_band_ref, table_band_ref,
-    smoother_ref, pack_ref, send_ref, fields_ref, ext, y_fields, table, tiles, index_rows, sem, *gathered
+    slot_ref, rows_ref, block_hbm, low_ref, high_ref, left_ref, right_ref, column_ref, y_band_hbm, table_band_hbm,
+    smoother_hbm, pack_hbm, send_ref, fields_ref, ext, y_fields, bands, table, tiles, y_band, base_band, smoother, pack,
+    index_rows, sem, load_sem, *gathered
 ):
     def copy_rows(step, side):
         return pltpu.make_async_copy(
-            rows_hbm.at[pl.ds(pl.multiple_of(step * STEP_TILES, STEP_TILES), STEP_TILES)], index_rows[side], sem.at[side]
+            rows_ref.at[pl.ds(pl.multiple_of(step * STEP_TILES, STEP_TILES), STEP_TILES)], index_rows[side], sem.at[side]
         )
 
+    inside = (slice(BORDER, BORDER + SZ), slice(Y_PAD, Y_PAD + CY))
+    loads = [
+        pltpu.make_async_copy(source, target, load_sem.at[i])
+        for i, (source, target) in enumerate((
+            (block_hbm, ext.at[inside[0], inside[1], :]), (y_band_hbm, y_band), (table_band_hbm, base_band),
+            (smoother_hbm, smoother), (pack_hbm, pack),
+        ))
+    ]
+    for load in loads:
+        load.start()
     copy_rows(0, 0).start()
     copy_rows(1, 1).start()
 
-    ext[BORDER:BORDER + SZ, Y_PAD:Y_PAD + CY, :] = block_ref[...]
     ext[0:BORDER, Y_PAD:Y_PAD + CY, :] = low_ref[...]
     ext[BORDER + SZ:DEEP, Y_PAD:Y_PAD + CY, :] = high_ref[...]
     ext[:, 0:Y_PAD, :] = left_ref[...]
     ext[:, Y_PAD + CY:TALL, :] = right_ref[...]
+    bands[...] = jnp.zeros_like(bands)
     tiles[...] = jnp.zeros_like(tiles)
     gathered[1][...] = jnp.zeros_like(gathered[1])
+    for load in loads:
+        load.wait()
+
+    for s in range(2):
+        for comp in range(COMPS):
+            for m in range(NX // 16):
+                first, last = max(0, 16 * m - 16), min(NX, 16 * m + 32)
+                skip = first - (16 * m - 16)
+                bands[s, comp * NX + first:comp * NX + last, m * LANES:(m + 1) * LANES] = (
+                    base_band[s, comp, skip:skip + last - first, :]
+                )
 
     for z in range(0, DEEP, 2):
         pair = jnp.concatenate([ext[z], ext[z + 1]], axis=1)
-        out = jnp.dot(y_band_ref[...], pair, preferred_element_type=jnp.float32)
         for s in range(2):
+            out = jnp.dot(y_band[s * 3 * CY:(s + 1) * 3 * CY, :], pair, preferred_element_type=jnp.float32)
             for kind in range(3):
-                rows = slice((s * 3 + kind) * CY, (s * 3 + kind + 1) * CY)
-                y_fields[z, s, kind] = out[rows, 0:NX]
-                y_fields[z + 1, s, kind] = out[rows, NX:2 * NX]
+                y_fields[z, s, kind] = out[kind * CY:(kind + 1) * CY, 0:NX]
+                y_fields[z + 1, s, kind] = out[kind * CY:(kind + 1) * CY, NX:2 * NX]
 
     for s in range(2):
         for z in range(SZ):
@@ -140,67 +161,74 @@
             for comp, (_, kind_y, kind_z) in enumerate(KINDS):
                 fields_ref[s, z * CY:(z + 1) * CY, comp * NX:(comp + 1) * NX] = passed[kind_y][kind_z].astype(jnp.bfloat16)
 
-    lower = lax.broadcasted_iota(jnp.int32, (ROWS, LANES), 1) < 64
+    lower = lax.broadcasted_iota(jnp.int32, (ROWS // 2, LANES), 1) < 64
     for m in range(0, NX // 16, 2):
-        outs = [
-            jnp.dot(fields_ref[s], table_band_ref[s, :, m * 128:(m + 2) * 128], preferred_element_type=jnp.float32)
-            for s in range(2)
-        ]
-        for half in range(2):
-            first, second = (out[:, half * 128:(half + 1) * 128] for out in outs)
-            group = (m + half) * 2
-            table[group * ROWS:(group + 1) * ROWS, :] = jnp.where(lower, first, second)
-            table[(group + 1) * ROWS:(group + 2) * ROWS, :] = jnp.where(lower, second, first)
+        for part in range(0, ROWS, ROWS // 2):
+            outs = [
+                jnp.dot(
+                    fields_ref[s, part:part + ROWS // 2, :], bands[s, :, m * LANES:(m + 2) * LANES],
+                    preferred_element_type=jnp.float32,
+                )
+                for s in range(2)
+            ]
+            for half in range(2):
+                first, second = (out[:, half * LANES:(half + 1) * LANES] for out in outs)
+                start = (m + half) * 2 * ROWS + part
+                table[start:start + ROWS // 2, :] = jnp.where(lower, first, second)
+                table[start + ROWS:start + ROWS + ROWS // 2, :] = jnp.where(lower, second, first)
 
     eye = (
         lax.broadcasted_iota(jnp.int32, (LANES, LANES), 0) == lax.broadcasted_iota(jnp.int32, (LANES, LANES), 1)
     ).astype(jnp.bfloat16)
 
-    def gather(step, side):
-        copy_rows(0, side).wait()
-        for tile in range(STEP_TILES):
-            for p in range(PTS):
-                row = index_rows[side][tile, p]
-                gathered[side][pl.ds(tile * PTS + p, 1), :] = table[pl.ds(row, 1), :]
-        copy_rows(jnp.minimum(step + 2, STEPS - 1), side).start()
-
-    def finish(step, side):
-        flat = gathered[side][...].astype(jnp.bfloat16)
+    def gather(side, tile):
+        for p in range(PTS):
+            row = index_rows[side][tile, p]
+            gathered[side][pl.ds(tile * PTS + p, 1), :] = table[pl.ds(row, 1), :]
+
+    def finish(step, side, group):
+        flat = gathered[side][group * 4 * PTS:(group + 1) * 4 * PTS, :].astype(jnp.bfloat16)
         turned = lax.dot_general(eye, flat, (((1,), (1,)), ((), ())), preferred_element_type=jnp.float32)
         picked = []
-        for tile in range(STEP_TILES):
-            column = column_ref[pl.ds(jnp.maximum(step, 0) * STEP_TILES + tile, 1), :]
+        for t in range(4):
+            column = column_ref[pl.ds(jnp.maximum(step, 0) * STEP_TILES + group * 4 + t, 1), :]
             column = jnp.broadcast_to(column, (8, PTS))
-            here = turned[:, tile * PTS:(tile + 1) * PTS]
-            lane = [(0, 64), (64, 0)]
+            here = turned[:, t * PTS:(t + 1) * PTS]
             both = [here[0:8], here[64:72]]
             for x in range(1, 16):
                 hit = column == x
                 for s in range(2):
-                    start = lane[x // 8][s] + (x % 8) * 8
+                    start = ((x // 8) ^ s) * 64 + (x % 8) * 8
                     both[s] = jnp.where(hit, here[start:start + 8], both[s])
             picked.append(jnp.concatenate(both, axis=0).astype(jnp.bfloat16))
         smooth = jnp.dot(
-            jnp.concatenate(picked, axis=0), smoother_ref[...], preferred_element_type=jnp.float32
+            jnp.concatenate(picked, axis=0), smoother[...], preferred_element_type=jnp.float32
         ).astype(jnp.bfloat16)
+        for t in range(4):
+            tiles[slot_ref[(step + 1) * STEP_TILES + group * 4 + t]] = smooth[t * 16:(t + 1) * 16]
+
+    def advance(step, side):
+        copy_rows(0, side).wait()
         for tile in range(STEP_TILES):
-            tiles[slot_ref[(step + 1) * STEP_TILES + tile]] = smooth[tile * 16:(tile + 1) * 16]
+            gather(side, tile)
+        for group in range(STEP_TILES // 4):
+            finish(step - 1, 1 - side, group)
+        copy_rows(jnp.minimum(step + 2, STEPS - 1), side).start()
 
     @pl.loop(0, STEPS // 2)
     def _(i):
-        gather(2 * i, 0)
-        finish(2 * i - 1, 1)
-        gather(2 * i + 1, 1)
-        finish(2 * i, 0)
-
-    finish(STEPS - 1, 1)
+        advance(2 * i, 0)
+        advance(2 * i + 1, 1)
+
+    for group in range(STEP_TILES // 4):
+        finish(STEPS - 1, 1, group)
     copy_rows(0, 0).wait()
     copy_rows(0, 1).wait()
 
     @pl.loop(0, OWNERS // 4)
     def _(quad):
         here = tiles[pl.ds(quad * 16, 16)].reshape(256, PTS)
-        packed = jnp.dot(pack_ref[...], here, preferred_element_type=jnp.float32).astype(jnp.bfloat16)
+        packed = jnp.dot(pack[...], here, preferred_element_type=jnp.float32).astype(jnp.bfloat16)
         send_ref[pl.ds(pl.multiple_of(quad * 4 * SEND_ROWS, 4 * SEND_ROWS), 4 * SEND_ROWS), :] = packed
 
 
@@ -219,13 +247,24 @@
             out_ref[s * 8 + o, 0] = total.astype(jnp.bfloat16)
 
 
-def mix_kernel(high_ref, low_ref, arrived_ref, out_ref):
-    here = arrived_ref[...]
-    for quad in range(8):
-        part = here[quad * 4 * SEND_ROWS:(quad + 1) * 4 * SEND_ROWS]
-        mixed = jnp.dot(high_ref[...], part, preferred_element_type=jnp.float32)
-        mixed = mixed + jnp.dot(low_ref[...], part, preferred_element_type=jnp.float32)
-        out_ref[quad * 256:(quad + 1) * 256, :] = mixed.astype(jnp.bfloat16)
+def mix_kernel(mix_ref, arrived_ref, out_hbm, out, sem):
+    copies = []
+    for part in range(MIX_PARTS):
+        pairs = 16 // MIX_PARTS
+        for pair in range(part * pairs, (part + 1) * pairs):
+            first = arrived_ref[pair * 8 * SEND_ROWS:(pair * 8 + 4) * SEND_ROWS]
+            second = arrived_ref[(pair * 8 + 4) * SEND_ROWS:(pair * 8 + 8) * SEND_ROWS]
+            here = jnp.concatenate([first, second], axis=1)
+            mixed = jnp.dot(mix_ref[0], here, preferred_element_type=jnp.float32)
+            mixed = (mixed + jnp.dot(mix_ref[1], here, preferred_element_type=jnp.float32)).astype(jnp.bfloat16)
+            out[pair * 512:pair * 512 + 256, :] = mixed[:, 0:PTS]
+            out[pair * 512 + 256:pair * 512 + 512, :] = mixed[:, PTS:2 * PTS]
+        rows = slice(part * pairs * 512, (part + 1) * pairs * 512)
+        copy = pltpu.make_async_copy(out.at[rows, :], out_hbm.at[rows, :], sem.at[part])
+        copy.start()
+        copies.append(copy)
+    for copy in copies:
+        copy.wait()
 
 
 def orientation_weights(angles):
@@ -270,7 +309,7 @@
     full = jnp.where(rows == columns, jnp.tile(scales, (16, 16)), 0.0)
     high = full.astype(jnp.bfloat16)
     low = (full - high.astype(jnp.float32)).astype(jnp.bfloat16)
-    return high, low
+    return jnp.stack([high, low])
 
 
 def per_device(volume, angles, tile_points, tile_dest):
@@ -291,28 +330,35 @@
     slot = jnp.concatenate([jnp.full((STEP_TILES,), SLOTS, jnp.int32), slot])
 
     weights = orientation_weights(angles)
-    mix_high, mix_low = mix_matrix(weights)
+    mix = mix_matrix(weights)
 
     vmem = pl.BlockSpec(memory_space=pltpu.VMEM)
+    hbm = pl.BlockSpec(memory_space=pltpu.HBM)
     send, fields = pl.pallas_call(
         sample_kernel,
         out_shape=(
             jax.ShapeDtypeStruct((OWNERS * SEND_ROWS, PTS), jnp.bfloat16),
             jax.ShapeDtypeStruct((2, ROWS, COMPS * NX), jnp.bfloat16),
         ),
-        in_specs=[pl.BlockSpec(memory_space=pltpu.SMEM), pl.BlockSpec(memory_space=pl.ANY)] + [vmem] * 10,
+        in_specs=[pl.BlockSpec(memory_space=pltpu.SMEM), vmem, hbm] + [vmem] * 5 + [hbm] * 4,
         out_specs=(vmem, vmem),
         scratch_shapes=[
             pltpu.VMEM((DEEP, TALL, NX), jnp.bfloat16),
             pltpu.VMEM((DEEP, 2, 3, CY, NX), jnp.float32),
+            pltpu.VMEM((2, COMPS * NX, NX * 8), jnp.bfloat16),
             pltpu.VMEM((NX // 8 * ROWS, LANES), jnp.float32),
             pltpu.VMEM((SLOTS + 1, 16, PTS), jnp.bfloat16),
+            pltpu.VMEM((6 * CY, TALL), jnp.bfloat16),
+            pltpu.VMEM((2, COMPS, 48, LANES), jnp.bfloat16),
+            pltpu.VMEM((PTS, PTS), jnp.bfloat16),
+            pltpu.VMEM((4 * SEND_ROWS, 4 * CAP * 16), jnp.bfloat16),
             [pltpu.SMEM((STEP_TILES, PTS), jnp.int32)] * 2,
             pltpu.SemaphoreType.DMA((2,)),
+            pltpu.SemaphoreType.DMA((5,)),
             pltpu.VMEM((STEP_TILES * PTS, LANES), jnp.float32),
             pltpu.VMEM((STEP_TILES * PTS, LANES), jnp.float32),
         ],
-        compiler_params=pltpu.CompilerParams(vmem_limit_bytes=48 << 20),
+        compiler_params=pltpu.CompilerParams(vmem_limit_bytes=32 << 20),
         cost_estimate=pl.CostEstimate(flops=4_000_000_000, bytes_accessed=8_000_000, transcendentals=0),
         name="sample",
     )(
@@ -341,18 +387,14 @@
 
     fibers = pl.pallas_call(
         mix_kernel,
-        grid=(4,),
         out_shape=jax.ShapeDtypeStruct((SLOTS * 16, PTS), jnp.bfloat16),
-        in_specs=[
-            pl.BlockSpec((256, 192), lambda i: (0, 0)),
-            pl.BlockSpec((256, 192), lambda i: (0, 0)),
-            pl.BlockSpec((32 * SEND_ROWS, PTS), lambda i: (i, 0)),
-        ],
-        out_specs=pl.BlockSpec((SLOTS * 4, PTS), lambda i: (i, 0)),
+        in_specs=[vmem, vmem],
+        out_specs=hbm,
+        scratch_shapes=[pltpu.VMEM((SLOTS * 16, PTS), jnp.bfloat16), pltpu.SemaphoreType.DMA((MIX_PARTS,))],
         compiler_params=pltpu.CompilerParams(vmem_limit_bytes=16 << 20),
         cost_estimate=pl.CostEstimate(flops=1_600_000_000, bytes_accessed=4_000_000, transcendentals=0),
         name="mix",
-    )(mix_high, mix_low, arrived.reshape(OWNERS * SEND_ROWS, PTS))
+    )(mix, arrived.reshape(OWNERS * SEND_ROWS, PTS))
     return responses, fibers.reshape(OWNERS, CAP, 16, PTS)
 
 

time: 102 us -> 105 us (1.029)
  Pallas kernels: 44.9 us -> 48.7 us
  other arithmetic: 6.26 us -> 3.75 us
  local copies, waits for them, and re-layouts: 11.3 us -> 13.1 us
    pallas_call x1, Pallas kernels: 35.8 us -> 41.2 us  [per_device(): pl.pallas_call(sample_kernel, out_shape=(jax.ShapeDtypeStruct((OWNERS * S...]
    pallas_call x1, Pallas kernels: 3.71 us -> 2.09 us  [per_device(): pl.pallas_call(mix_kernel, out_shape=jax.ShapeDtypeStruct((SLOTS * 16, PT...]
    convert_element_type x1, other arithmetic: 1.78 us -> 0.17 us  [mix_matrix(): high = full.astype(jnp.bfloat16)]
  transfers between devices with their start and end apart: 5 -> 5, of which waited for: 2 -> 2; matrix products, arithmetic and copies ran while one was open for 12% -> 10% of each run, Pallas kernels for 5% -> 5%
where the time goes in v2:
time: 105 us
  Pallas kernels  48.7 us (46%)
  starting transfers between devices  22.9 us (22%)
  waiting for transfers between devices  15.5 us (15%)
  local copies, waits for them, and re-layouts  13.1 us (12%)
  other arithmetic  3.75 us (4%)
    pallas_call x1, Pallas kernels, per_device(): pl.pallas_call(sample_kernel, out_shape=(jax.ShapeDtypeStruct((OWNERS * S...  41.2 us
    all_to_all x1, waiting for transfers between devices, per_device(): lax.all_to_all(send.reshape(OWNERS, SEND_ROWS, PTS), ('wide', 'narrow'),...  12.1 us
    all_to_all x1, starting transfers between devices, per_device(): lax.all_to_all(send.reshape(OWNERS, SEND_ROWS, PTS), ('wide', 'narrow'),...  11.6 us
    ppermute x4, starting transfers between devices, shifted(): return lax.ppermute(value, axis, forward if step > 0 else backward)  11.3 us
    pallas_call x1, Pallas kernels, per_device(): pl.pallas_call(response_kernel, grid=(SZ,), out_shape=jax.ShapeDtypeStruc...  5.38 us
    unnamed x12, local copies, waits for them, and re-layouts  5.28 us
    another operation x3, local copies, waits for them, and re-layouts, mix_matrix(): full = jnp.where(rows == columns, jnp.tile(scales, (16, 16)), 0.0)  4.99 us
    ppermute x4, waiting for transfers between devices, shifted(): return lax.ppermute(value, axis, forward if step > 0 else backward)  3.4 us
  transfers between devices with their start and end apart: 5, of which 2 were waited for; matrix products, arithmetic and copies ran while one was open for 10% of the time, Pallas kernels for 5%

profile of v2, /device:TPU:1, one launch (start us, length us, event | category | flops | bytes accessed | tf_op | source)
XLA Modules:
  0.0 104.7 jit_solution(7562050366773602817)
XLA Ops:
  0.6 1.0 fusion.4
  1.6 3.3 %collective-permute-start.1 = (bf16[6,64,128]{2,1,0:T(8,128)(2,1)S(1)}, bf16[6,64,128]{2,1,0:T(8,128)(2,1)S(1)}, u32[]{:S(2)}, u32[]{:S(2)}) collective-permute-start(bf16[6,64,128]{2,1,0:T(8,128)(2,1)S(1)} %get-tuple-element.36), channel_id=1, source_target_pairs={{4,0},{8,4},{12,8},{16,12},{20,16},{24,20},{28,24},{32,28},{36,32}... | collective-permute-start | bytes 294920 | tf_op jit(solution)/shard_map/ppermute | solution.py:301
  5.0 3.1 %collective-permute-start = (bf16[6,64,128]{2,1,0:T(8,128)(2,1)S(1)}, bf16[6,64,128]{2,1,0:T(8,128)(2,1)S(1)}, u32[]{:S(2)}, u32[]{:S(2)}) collective-permute-start(bf16[6,64,128]{2,1,0:T(8,128)(2,1)S(1)} %get-tuple-element.37), channel_id=1, source_target_pairs={{0,4},{4,8},{8,12},{12,16},{16,20},{20,24},{24,28},{28,32},{32,36}... | collective-permute-start | bytes 294920 | tf_op jit(solution)/shard_map/ppermute | solution.py:301
  8.1 0.7 fusion.3
  8.8 0.9 convert_reduce_fusion
  9.7 0.9 broadcast_and_fusion
  10.6 0.7 multiply_add_fusion
  11.3 0.0 collective-permute-done.1.high_ref
  11.3 0.0 collective-permute-done.low_ref
  11.3 3.5 %collective-permute-start.2 = (bf16[20,8,128]{2,1,0:T(8,128)(2,1)S(1)}, bf16[20,8,128]{2,1,0:T(8,128)(2,1)S(1)}, u32[]{:S(2)}, u32[]{:S(2)}) collective-permute-start(bf16[20,8,128]{2,1,0:T(8,128)(2,1)S(1)} %pad_maximum_fusion.1), channel_id=1, source_target_pairs={{0,1},{1,2},{2,3},{4,5},{5,6},{6,7},{8,9},{9,10},{10,11},{12,13},{... | collective-permute-start | bytes 122888 | tf_op jit(solution)/shard_map/ppermute | solution.py:301
  14.9 1.3 %collective-permute-start.3 = (bf16[20,8,128]{2,1,0:T(8,128)(2,1)S(1)}, bf16[20,8,128]{2,1,0:T(8,128)(2,1)S(1)}, u32[]{:S(2)}, u32[]{:S(2)}) collective-permute-start(bf16[20,8,128]{2,1,0:T(8,128)(2,1)S(1)} %pad_maximum_fusion.2), channel_id=1, source_target_pairs={{1,0},{2,1},{3,2},{5,4},{6,5},{7,6},{9,8},{10,9},{11,10},{13,12},{... | collective-permute-start | bytes 122888 | tf_op jit(solution)/shard_map/ppermute | solution.py:301
  16.2 0.8 cosine_bitcast_fusion
  17.0 0.1 concatenate.13.slot_ref
  17.1 0.0 collective-permute-done.2.left_ref
  17.1 3.4 %collective-permute-done.3.right_ref = bf16[20,8,128]{2,1,0:T(8,128)(2,1)S(1)} collective-permute-done((bf16[20,8,128]{2,1,0:T(8,128)(2,1)S(1)}, bf16[20,8,128]{2,1,0:T(8,128)(2,1)S(1)}, u32[]{:S(2)}, u32[]{:S(2)}) %collective-permute-start.3) | collective-permute-done | bytes 40992 | tf_op jit(solution)/shard_map/ppermute | solution.py:301
  20.5 0.0 copy-start
  20.5 0.9 copy-done
  21.4 0.0 copy-start.2
  21.4 0.9 copy-done.2
  22.3 0.0 copy-start.3
  22.3 0.9 copy-done.3
  23.2 0.0 copy-start.4
  23.2 0.9 copy-done.4
  24.1 0.0 copy-start.5
  24.1 0.8 copy-done.5
  24.9 41.2 %sample.1 = (bf16[6144,128]{1,0:T(8,128)(2,1)}, bf16[2,512,768]{2,1,0:T(8,128)(2,1)S(1)}) custom-call(s32[272]{0:T(512)S(1)} %concatenate.13.slot_ref, s32[256,128]{1,0:T(8,128)S(1)} %get-tuple-element.33.rows_ref, bf16[8,64,128]{2,1,0:T(8,128)(2,1)S(1)} %copy-done, bf16[6,64,128]{2,1,0:T(8,128)(2,1)S(1)} %collective-permute-done.low_ref, ...), custom_call_target="tpu_custom_call" | custom-call | flops 4000000000 | bytes 8000000 | tf_op jit(solution)/shard_map/sample/pallas_call | solution.py:337
  66.1 11.6 %all-to-all-start = ((bf16[128,48,128]{2,1,0:T(8,128)(2,1)}), bf16[128,48,128]{2,1,0:T(8,128)(2,1)S(1)}, u32[]{:S(2)}, u32[]{:S(2)}) async-start(bf16[128,48,128]{2,1,0:T(8,128)(2,1)} %bitcast.5), calls=%async_computation | async-start | bytes 3145728 | tf_op jit(solution)/shard_map/all_to_all | solution.py:369
  77.7 0.1 copy.45
  77.8 0.1 copy.37
  77.9 0.1 copy.35
  77.9 0.1 copy.39
  78.0 0.1 stack.4
  78.1 0.5 scatter.9
  78.7 0.1 copy.46
  78.7 1.3 %tile.4 = f32[16,16,16,12]{1,0,3,2:T(8,128)} broadcast(f32[16,12]{0,1:T(8,128)S(1)} %copy.46), dimensions={1,3} | broadcast | bytes 197376 | tf_op jit(solution)/shard_map/tile | solution.py:309
  80.0 2.6 %tile.10 = f32[1,256,192]{1,2,0:T(8,128)} reshape(f32[16,16,16,12]{1,0,3,2:T(8,128)} %tile.4) | data formatting | bytes 393216 | tf_op jit(solution)/shard_map/tile | solution.py:309
  82.7 1.1 %copy.47 = f32[1,256,192]{2,1,0:T(8,128)S(1)} copy(f32[1,256,192]{1,2,0:T(8,128)} %tile.10) | data formatting | bytes 393216 | tf_op jit(solution)/shard_map/tile | solution.py:309
  83.8 0.2 subtract_convert_fusion
  84.0 0.2 fusion.2
  84.2 0.0 copy-start.1
  84.2 0.9 copy-done.1
  85.1 5.4 %respond.1 = bf16[16,8,64,128]{3,2,1,0:T(8,128)(2,1)} custom-call(f32[8,6]{1,0:T(8,128)S(1)} %broadcast_multiply_fusion.weight_ref, bf16[2,512,768]{2,1,0:T(8,128)(2,1)S(1)} %get-tuple-element.28.fields_ref, bf16[2,3,128,128]{3,2,1,0:T(8,128)(2,1)S(1)} %copy-done.1), custom_call_target="tpu_custom_call" | custom-call | flops 200000000 | bytes 4000000 | tf_op jit(solution)/shard_map/respond/pallas_call | solution.py:373
  90.5 12.1 %all-to-all-done = bf16[128,48,128]{2,1,0:T(8,128)(2,1)S(1)} async-done(((bf16[128,48,128]{2,1,0:T(8,128)(2,1)}), bf16[128,48,128]{2,1,0:T(8,128)(2,1)S(1)}, u32[]{:S(2)}, u32[]{:S(2)}) %all-to-all-start) | async-done | bytes 1572896 | tf_op jit(solution)/shard_map/all_to_all | solution.py:369
  102.6 2.1 %mix.1 = bf16[8192,128]{1,0:T(8,128)(2,1)} custom-call(bf16[2,256,192]{2,1,0:T(8,128)(2,1)S(1)} %pad_maximum_fusion.mix_ref, bf16[6144,128]{1,0:T(8,128)(2,1)S(1)} %bitcast.16), custom_call_target="tpu_custom_call" | custom-call | flops 1600000000 | bytes 4000000 | tf_op jit(solution)/shard_map/mix/pallas_call | solution.py:388
  (13 shorter events, 0.1 us)
Async XLA Ops:
  1.6 9.7 %collective-permute-start.1 = (bf16[6,64,128]{2,1,0:T(8,128)(2,1)S(1)}, bf16[6,64,128]{2,1,0:T(8,128)(2,1)S(1)}, u32[]{:S(2)}, u32[]{:S(2)}) collective-permute-start(bf16[6,64,128]{2,1,0:T(8,128)(2,1)S(1)} %get-tuple-element.36), channel_id=1, source_target_pairs={{4,0},{8,4},{12,8},{16,12},{20,16},{24,20},{28,24},{32,28},{36,32}... | collective-permute-start | bytes 294920 | tf_op jit(solution)/shard_map/ppermute | solution.py:301
  5.0 6.4 %collective-permute-start = (bf16[6,64,128]{2,1,0:T(8,128)(2,1)S(1)}, bf16[6,64,128]{2,1,0:T(8,128)(2,1)S(1)}, u32[]{:S(2)}, u32[]{:S(2)}) collective-permute-start(bf16[6,64,128]{2,1,0:T(8,128)(2,1)S(1)} %get-tuple-element.37), channel_id=1, source_target_pairs={{0,4},{4,8},{8,12},{12,16},{16,20},{20,24},{24,28},{28,32},{32,36}... | collective-permute-start | bytes 294920 | tf_op jit(solution)/shard_map/ppermute | solution.py:301
  11.3 5.8 %collective-permute-start.2 = (bf16[20,8,128]{2,1,0:T(8,128)(2,1)S(1)}, bf16[20,8,128]{2,1,0:T(8,128)(2,1)S(1)}, u32[]{:S(2)}, u32[]{:S(2)}) collective-permute-start(bf16[20,8,128]{2,1,0:T(8,128)(2,1)S(1)} %pad_maximum_fusion.1), channel_id=1, source_target_pairs={{0,1},{1,2},{2,3},{4,5},{5,6},{6,7},{8,9},{9,10},{10,11},{12,13},{... | collective-permute-start | bytes 122888 | tf_op jit(solution)/shard_map/ppermute | solution.py:301
  14.9 5.6 %collective-permute-start.3 = (bf16[20,8,128]{2,1,0:T(8,128)(2,1)S(1)}, bf16[20,8,128]{2,1,0:T(8,128)(2,1)S(1)}, u32[]{:S(2)}, u32[]{:S(2)}) collective-permute-start(bf16[20,8,128]{2,1,0:T(8,128)(2,1)S(1)} %pad_maximum_fusion.2), channel_id=1, source_target_pairs={{1,0},{2,1},{3,2},{5,4},{6,5},{7,6},{9,8},{10,9},{11,10},{13,12},{... | collective-permute-start | bytes 122888 | tf_op jit(solution)/shard_map/ppermute | solution.py:301
  20.5 0.9 copy-start
  21.4 0.9 copy-start.2
  22.3 0.9 copy-start.3
  23.2 0.9 copy-start.4
  24.1 0.8 copy-start.5
  66.1 36.6 %all-to-all-start = ((bf16[128,48,128]{2,1,0:T(8,128)(2,1)}), bf16[128,48,128]{2,1,0:T(8,128)(2,1)S(1)}, u32[]{:S(2)}, u32[]{:S(2)}) async-start(bf16[128,48,128]{2,1,0:T(8,128)(2,1)} %bitcast.5), calls=%async_computation | async-start | bytes 3145728 | tf_op jit(solution)/shard_map/all_to_all | solution.py:369
  84.2 0.9 copy-start.1

commit v3 on v2

--- a/solution.py
+++ b/solution.py
@@ -25,6 +25,7 @@
 PTS = 128
 STEP_TILES = 16
 STEPS = TILES // STEP_TILES
+GROUP = 4
 OWNERS = 128
 SLOTS = OWNERS * CAP
 SEND_ROWS = CAP * 2 * COMPS
@@ -44,46 +45,63 @@
 TAPS = tap_table()
 
 
-def band(kind, spacing, rows_in, count_out, start):
-    result = np.zeros((count_out, rows_in), np.float32)
+def tap_values(distance, kind, spacing):
+    total = jnp.zeros(distance.shape, jnp.float32)
     for tap in range(2 * TAPS_PER_SIDE + 1):
-        shift = (tap - TAPS_PER_SIDE) * spacing
-        for out in range(count_out):
-            source = out + start - shift
-            if 0 <= source < rows_in:
-                result[out, source] += TAPS[kind, tap]
-    return result
-
-
-def y_bands():
-    return np.concatenate(
-        [band(kind, d, TALL, CY, Y_PAD) for d in SPACINGS for kind in range(3)], axis=0
-    ).astype(ml_dtypes.bfloat16)
+        if TAPS[kind, tap] != 0.0:
+            hit = distance == (tap - TAPS_PER_SIDE) * spacing
+            total = jnp.where(hit, float(TAPS[kind, tap]), total)
+    return total
+
+
+def index(shape, axis):
+    return lax.broadcasted_iota(jnp.int32, shape, axis)
+
+
+def fill_y_band(y_band):
+    distance = index((CY, TALL), 0) + Y_PAD - index((CY, TALL), 1)
+    for s in range(2):
+        for kind in range(3):
+            start = (s * 3 + kind) * CY
+            y_band[start:start + CY, :] = tap_values(distance, kind, SPACINGS[s]).astype(jnp.bfloat16)
+
+
+def fill_x_bands(bands):
+    bands[...] = jnp.zeros_like(bands)
+    column = index((48, LANES), 1)
+    for s in range(2):
+        local = (((column >> 6) ^ s) << 3) + ((column >> 3) & 7)
+        distance = local + 16 - index((48, LANES), 0)
+        taps = [tap_values(distance, kind, SPACINGS[s]) for kind in range(3)]
+        for comp in range(COMPS):
+            base = jnp.where((column & 7) == comp, taps[KINDS[comp][0]], 0.0).astype(jnp.bfloat16)
+            for m in range(NX // 16):
+                first, last = max(0, 16 * m - 16), min(NX, 16 * m + 32)
+                skip = first - (16 * m - 16)
+                bands[s, comp * NX + first:comp * NX + last, m * LANES:(m + 1) * LANES] = base[skip:skip + last - first]
+
+
+def smooth_matrix():
+    distance = (index((PTS, PTS), 1) - index((PTS, PTS), 0)).astype(jnp.float32)
+    bell = jnp.exp(-distance * distance / (2.0 * SMOOTH_SIGMA * SMOOTH_SIGMA))
+    return (bell / jnp.sum(bell, axis=0, keepdims=True)).astype(jnp.bfloat16)
+
+
+def pack_matrix():
+    shape = (4 * SEND_ROWS, 4 * CAP * 16)
+    row = index(shape, 0)
+    slot = (row * 43691) >> 19
+    six = (row * 43691) >> 18
+    source = slot * 16 + (six - 2 * slot) * 8 + (row - 6 * six)
+    return jnp.where(source == index(shape, 1), 1.0, 0.0).astype(jnp.bfloat16)
 
 
 def x_bands():
-    return np.stack(
-        [np.stack([band(kind, d, NX, NX, 0).T for kind in range(3)]) for d in SPACINGS]
-    ).astype(ml_dtypes.bfloat16)
-
-
-def table_bands():
-    result = np.zeros((2, COMPS, 48, LANES), np.float32)
-    for s in range(2):
-        for x in range(16):
-            column = ((x // 8) ^ s) * 64 + (x % 8) * 8
-            for comp in range(COMPS):
-                bands = band(KINDS[comp][0], SPACINGS[s], 48, 48, 0)
-                result[s, comp, :, column + comp] = bands[x + 16]
-    return result.astype(ml_dtypes.bfloat16)
-
-
-def pack_matrix():
-    result = np.zeros((4 * SEND_ROWS, 4 * CAP * 16), np.float32)
-    for slot in range(4 * CAP):
-        for s in range(2):
-            for comp in range(COMPS):
-                result[slot * 12 + s * COMPS + comp, slot * 16 + s * 8 + comp] = 1.0
+    result = np.zeros((2, 3, NX, NX), np.float32)
+    for s in range(2):
+        for kind in range(3):
+            for tap in range(2 * TAPS_PER_SIDE + 1):
+                result[s, kind] += TAPS[kind, tap] * np.eye(NX, k=(tap - TAPS_PER_SIDE) * SPACINGS[s], dtype=np.float32)
     return result.astype(ml_dtypes.bfloat16)
 
 
@@ -106,46 +124,24 @@
 
 
 def sample_kernel(
-    slot_ref, rows_ref, block_hbm, low_ref, high_ref, left_ref, right_ref, column_ref, y_band_hbm, table_band_hbm,
-    smoother_hbm, pack_hbm, send_ref, fields_ref, ext, y_fields, bands, table, tiles, y_band, base_band, smoother, pack,
-    index_rows, sem, load_sem, *gathered
+    slot_ref, rows_ref, center_ref, left_ref, right_ref, column_ref, send_ref, fields_ref, ext, y_fields, bands, table, tiles,
+    y_band, smoother, index_rows, sem
 ):
     def copy_rows(step, side):
         return pltpu.make_async_copy(
             rows_ref.at[pl.ds(pl.multiple_of(step * STEP_TILES, STEP_TILES), STEP_TILES)], index_rows[side], sem.at[side]
         )
 
-    inside = (slice(BORDER, BORDER + SZ), slice(Y_PAD, Y_PAD + CY))
-    loads = [
-        pltpu.make_async_copy(source, target, load_sem.at[i])
-        for i, (source, target) in enumerate((
-            (block_hbm, ext.at[inside[0], inside[1], :]), (y_band_hbm, y_band), (table_band_hbm, base_band),
-            (smoother_hbm, smoother), (pack_hbm, pack),
-        ))
-    ]
-    for load in loads:
-        load.start()
     copy_rows(0, 0).start()
     copy_rows(1, 1).start()
 
-    ext[0:BORDER, Y_PAD:Y_PAD + CY, :] = low_ref[...]
-    ext[BORDER + SZ:DEEP, Y_PAD:Y_PAD + CY, :] = high_ref[...]
+    ext[:, Y_PAD:Y_PAD + CY, :] = center_ref[...]
     ext[:, 0:Y_PAD, :] = left_ref[...]
     ext[:, Y_PAD + CY:TALL, :] = right_ref[...]
-    bands[...] = jnp.zeros_like(bands)
     tiles[...] = jnp.zeros_like(tiles)
-    gathered[1][...] = jnp.zeros_like(gathered[1])
-    for load in loads:
-        load.wait()
-
-    for s in range(2):
-        for comp in range(COMPS):
-            for m in range(NX // 16):
-                first, last = max(0, 16 * m - 16), min(NX, 16 * m + 32)
-                skip = first - (16 * m - 16)
-                bands[s, comp * NX + first:comp * NX + last, m * LANES:(m + 1) * LANES] = (
-                    base_band[s, comp, skip:skip + last - first, :]
-                )
+    fill_y_band(y_band)
+    fill_x_bands(bands)
+    smoother[...] = smooth_matrix()
 
     for z in range(0, DEEP, 2):
         pair = jnp.concatenate([ext[z], ext[z + 1]], axis=1)
@@ -161,7 +157,7 @@
             for comp, (_, kind_y, kind_z) in enumerate(KINDS):
                 fields_ref[s, z * CY:(z + 1) * CY, comp * NX:(comp + 1) * NX] = passed[kind_y][kind_z].astype(jnp.bfloat16)
 
-    lower = lax.broadcasted_iota(jnp.int32, (ROWS // 2, LANES), 1) < 64
+    lower = index((ROWS // 2, LANES), 1) < 64
     for m in range(0, NX // 16, 2):
         for part in range(0, ROWS, ROWS // 2):
             outs = [
@@ -173,46 +169,43 @@
             ]
             for half in range(2):
                 first, second = (out[:, half * LANES:(half + 1) * LANES] for out in outs)
-                start = (m + half) * 2 * ROWS + part
+                start = 8 + (m + half) * 2 * ROWS + part
                 table[start:start + ROWS // 2, :] = jnp.where(lower, first, second)
                 table[start + ROWS:start + ROWS + ROWS // 2, :] = jnp.where(lower, second, first)
 
-    eye = (
-        lax.broadcasted_iota(jnp.int32, (LANES, LANES), 0) == lax.broadcasted_iota(jnp.int32, (LANES, LANES), 1)
-    ).astype(jnp.bfloat16)
-
-    def gather(side, tile):
-        for p in range(PTS):
-            row = index_rows[side][tile, p]
-            gathered[side][pl.ds(tile * PTS + p, 1), :] = table[pl.ds(row, 1), :]
-
-    def finish(step, side, group):
-        flat = gathered[side][group * 4 * PTS:(group + 1) * 4 * PTS, :].astype(jnp.bfloat16)
-        turned = lax.dot_general(eye, flat, (((1,), (1,)), ((), ())), preferred_element_type=jnp.float32)
-        picked = []
-        for t in range(4):
-            column = column_ref[pl.ds(jnp.maximum(step, 0) * STEP_TILES + group * 4 + t, 1), :]
-            column = jnp.broadcast_to(column, (8, PTS))
-            here = turned[:, t * PTS:(t + 1) * PTS]
-            both = [here[0:8], here[64:72]]
-            for x in range(1, 16):
-                hit = column == x
-                for s in range(2):
-                    start = ((x // 8) ^ s) * 64 + (x % 8) * 8
-                    both[s] = jnp.where(hit, here[start:start + 8], both[s])
-            picked.append(jnp.concatenate(both, axis=0).astype(jnp.bfloat16))
-        smooth = jnp.dot(
-            jnp.concatenate(picked, axis=0), smoother[...], preferred_element_type=jnp.float32
-        ).astype(jnp.bfloat16)
-        for t in range(4):
-            tiles[slot_ref[(step + 1) * STEP_TILES + group * 4 + t]] = smooth[t * 16:(t + 1) * 16]
+    eye = (index((LANES, LANES), 0) == index((LANES, LANES), 1)).astype(jnp.bfloat16)
+    sublane = index((8, LANES), 0)
 
     def advance(step, side):
         copy_rows(0, side).wait()
-        for tile in range(STEP_TILES):
-            gather(side, tile)
-        for group in range(STEP_TILES // 4):
-            finish(step - 1, 1 - side, group)
+        for group in range(STEP_TILES // GROUP):
+            blocks = []
+            for tile in range(group * GROUP, (group + 1) * GROUP):
+                for p in range(0, PTS, 8):
+                    merged = None
+                    for k in range(8):
+                        row = index_rows[side][tile, p + k]
+                        loaded = table[pl.ds(row + (8 - k), 8), :]
+                        merged = loaded if merged is None else jnp.where(sublane == k, loaded, merged)
+                    blocks.append(merged)
+            flat = jnp.concatenate(blocks, axis=0).astype(jnp.bfloat16)
+            turned = lax.dot_general(eye, flat, (((1,), (1,)), ((), ())), preferred_element_type=jnp.float32)
+            picked = []
+            for t in range(GROUP):
+                column = jnp.broadcast_to(column_ref[pl.ds(step * STEP_TILES + group * GROUP + t, 1), :], (8, PTS))
+                here = turned[:, t * PTS:(t + 1) * PTS]
+                both = [here[0:8], here[64:72]]
+                for x in range(1, 16):
+                    hit = column == x
+                    for s in range(2):
+                        start = ((x // 8) ^ s) * 64 + (x % 8) * 8
+                        both[s] = jnp.where(hit, here[start:start + 8], both[s])
+                picked.append(jnp.concatenate(both, axis=0).astype(jnp.bfloat16))
+            smooth = jnp.dot(
+                jnp.concatenate(picked, axis=0), smoother[...], preferred_element_type=jnp.float32
+            ).astype(jnp.bfloat16)
+            for t in range(GROUP):
+                tiles[slot_ref[step * STEP_TILES + group * GROUP + t]] = smooth[t * 16:(t + 1) * 16]
         copy_rows(jnp.minimum(step + 2, STEPS - 1), side).start()
 
     @pl.loop(0, STEPS // 2)
@@ -220,16 +213,17 @@
         advance(2 * i, 0)
         advance(2 * i + 1, 1)
 
-    for group in range(STEP_TILES // 4):
-        finish(STEPS - 1, 1, group)
     copy_rows(0, 0).wait()
     copy_rows(0, 1).wait()
-
-    @pl.loop(0, OWNERS // 4)
-    def _(quad):
-        here = tiles[pl.ds(quad * 16, 16)].reshape(256, PTS)
-        packed = jnp.dot(pack[...], here, preferred_element_type=jnp.float32).astype(jnp.bfloat16)
-        send_ref[pl.ds(pl.multiple_of(quad * 4 * SEND_ROWS, 4 * SEND_ROWS), 4 * SEND_ROWS), :] = packed
+    pack = pack_matrix()
+
+    @pl.loop(0, OWNERS // 8)
+    def _(oct):
+        for quad in range(2):
+            here = tiles[pl.ds(oct * 32 + quad * 16, 16)].reshape(256, PTS)
+            packed = jnp.dot(pack, here, preferred_element_type=jnp.float32).astype(jnp.bfloat16)
+            start = pl.multiple_of(oct * 8 * SEND_ROWS, 8 * SEND_ROWS) + quad * 4 * SEND_ROWS
+            send_ref[pl.ds(start, 4 * SEND_ROWS), :] = packed
 
 
 def response_kernel(weight_ref, fields_ref, x_band_ref, out_ref):
@@ -286,14 +280,6 @@
     )
 
 
-def smooth_matrix():
-    source = np.arange(PTS, dtype=np.float32)[:, None]
-    target = np.arange(PTS, dtype=np.float32)[None, :]
-    distance = target - source
-    bell = np.exp(-distance * distance / np.float32(2.0 * SMOOTH_SIGMA * SMOOTH_SIGMA))
-    return (bell / np.sum(bell, axis=0, keepdims=True)).astype(ml_dtypes.bfloat16)
-
-
 def shifted(value, axis, step):
     count = lax.axis_size(axis)
     forward = [(i, i + 1) for i in range(count - 1)]
@@ -327,7 +313,7 @@
     later = lax.broadcasted_iota(jnp.int32, (TILES, TILES), 1)
     same_owner = (dest[:, None] == dest[None, :]) & (earlier < later)
     slot = dest * CAP + jnp.sum(same_owner.astype(jnp.int32), axis=0)
-    slot = jnp.concatenate([jnp.full((STEP_TILES,), SLOTS, jnp.int32), slot])
+    center = jnp.concatenate([low, volume, high], axis=0)
 
     weights = orientation_weights(angles)
     mix = mix_matrix(weights)
@@ -340,30 +326,24 @@
             jax.ShapeDtypeStruct((OWNERS * SEND_ROWS, PTS), jnp.bfloat16),
             jax.ShapeDtypeStruct((2, ROWS, COMPS * NX), jnp.bfloat16),
         ),
-        in_specs=[pl.BlockSpec(memory_space=pltpu.SMEM), vmem, hbm] + [vmem] * 5 + [hbm] * 4,
+        in_specs=[pl.BlockSpec(memory_space=pltpu.SMEM)] + [vmem] * 5,
         out_specs=(vmem, vmem),
         scratch_shapes=[
             pltpu.VMEM((DEEP, TALL, NX), jnp.bfloat16),
             pltpu.VMEM((DEEP, 2, 3, CY, NX), jnp.float32),
             pltpu.VMEM((2, COMPS * NX, NX * 8), jnp.bfloat16),
-            pltpu.VMEM((NX // 8 * ROWS, LANES), jnp.float32),
-            pltpu.VMEM((SLOTS + 1, 16, PTS), jnp.bfloat16),
+            pltpu.VMEM((NX // 8 * ROWS + 16, LANES), jnp.float32),
+            pltpu.VMEM((SLOTS, 16, PTS), jnp.bfloat16),
             pltpu.VMEM((6 * CY, TALL), jnp.bfloat16),
-            pltpu.VMEM((2, COMPS, 48, LANES), jnp.bfloat16),
             pltpu.VMEM((PTS, PTS), jnp.bfloat16),
-            pltpu.VMEM((4 * SEND_ROWS, 4 * CAP * 16), jnp.bfloat16),
             [pltpu.SMEM((STEP_TILES, PTS), jnp.int32)] * 2,
             pltpu.SemaphoreType.DMA((2,)),
-            pltpu.SemaphoreType.DMA((5,)),
-            pltpu.VMEM((STEP_TILES * PTS, LANES), jnp.float32),
-            pltpu.VMEM((STEP_TILES * PTS, LANES), jnp.float32),
         ],
         compiler_params=pltpu.CompilerParams(vmem_limit_bytes=32 << 20),
         cost_estimate=pl.CostEstimate(flops=4_000_000_000, bytes_accessed=8_000_000, transcendentals=0),
         name="sample",
     )(
-        slot, table_rows, volume, low, high, left, right, columns,
-        jnp.asarray(y_bands()), jnp.asarray(table_bands()), jnp.asarray(smooth_matrix()), jnp.asarray(pack_matrix()),
+        slot, table_rows, center, left, right, columns,
     )
 
     arrived = lax.all_to_all(

time: 105 us -> 91.7 us (0.87)
  Pallas kernels: 48.7 us -> 39.5 us
  local copies, waits for them, and re-layouts: 13.1 us -> 8.69 us
    pallas_call x1, Pallas kernels: 41.2 us -> 32.1 us  [per_device(): pl.pallas_call(sample_kernel, out_shape=(jax.ShapeDtypeStruct((OWNERS * S...]
    unnamed x12 -> x2, local copies, waits for them, and re-layouts: 5.28 us -> 0.92 us
  transfers between devices with their start and end apart: 5 -> 5, of which waited for: 2 -> 2; matrix products, arithmetic and copies ran while one was open for 10% -> 13% of each run, Pallas kernels for 5% -> 6%
where the time goes in v3:
time: 91.7 us; the launch traced here: 91.2 us
  Pallas kernels  39.5 us (43%)
  starting transfers between devices  22.7 us (25%)
  waiting for transfers between devices  14.8 us (16%)
  local copies, waits for them, and re-layouts  8.69 us (9%)
  other arithmetic  4.69 us (5%)
    pallas_call x1, Pallas kernels, per_device(): pl.pallas_call(sample_kernel, out_shape=(jax.ShapeDtypeStruct((OWNERS * S...  32.1 us
    all_to_all x1, waiting for transfers between devices, per_device(): lax.all_to_all(send.reshape(OWNERS, SEND_ROWS, PTS), ('wide', 'narrow'),...  12.1 us
    all_to_all x1, starting transfers between devices, per_device(): lax.all_to_all(send.reshape(OWNERS, SEND_ROWS, PTS), ('wide', 'narrow'),...  11.4 us
    ppermute x4, starting transfers between devices, shifted(): return lax.ppermute(value, axis, forward if step > 0 else backward)  11.3 us
    pallas_call x1, Pallas kernels, per_device(): pl.pallas_call(response_kernel, grid=(SZ,), out_shape=jax.ShapeDtypeStruc...  5.38 us
    another operation x3, local copies, waits for them, and re-layouts, mix_matrix(): full = jnp.where(rows == columns, jnp.tile(scales, (16, 16)), 0.0)  5.01 us
    ppermute x4, waiting for transfers between devices, shifted(): return lax.ppermute(value, axis, forward if step > 0 else backward)  2.68 us
    pallas_call x1, Pallas kernels, per_device(): pl.pallas_call(mix_kernel, out_shape=jax.ShapeDtypeStruct((SLOTS * 16, PT...  2.09 us
  transfers between devices with their start and end apart: 5, of which 2 were waited for; matrix products, arithmetic and copies ran while one was open for 13% of the time, Pallas kernels for 6%

profile of v3, /device:TPU:1, one launch (start us, length us, event | category | flops | bytes accessed | tf_op | source)
XLA Modules:
  0.0 91.2 jit_solution(299594719987069091)
XLA Ops:
  0.6 1.0 %fusion.4 = (bf16[6,64,128]{2,1,0:T(8,128)(2,1)S(1)}, bf16[6,64,128]{2,1,0:T(8,128)(2,1)S(1)}) fusion(bf16[8,64,128]{2,1,0:T(8,128)(2,1)} %param.9), kind=kLoop, calls=%fused_computation.33 | loop fusion | bytes 393216 | tf_op jit(solution)/shard_map/slice | solution.py:302
  1.6 4.5 %collective-permute-start = (bf16[6,64,128]{2,1,0:T(8,128)(2,1)S(1)}, bf16[6,64,128]{2,1,0:T(8,128)(2,1)S(1)}, u32[]{:S(2)}, u32[]{:S(2)}) collective-permute-start(bf16[6,64,128]{2,1,0:T(8,128)(2,1)S(1)} %get-tuple-element.36), channel_id=1, source_target_pairs={{0,4},{4,8},{8,12},{12,16},{16,20},{20,24},{24,28},{28,32},{32,36}... | collective-permute-start | bytes 294920 | tf_op jit(solution)/shard_map/ppermute | solution.py:287
  6.1 1.9 %collective-permute-start.1 = (bf16[6,64,128]{2,1,0:T(8,128)(2,1)S(1)}, bf16[6,64,128]{2,1,0:T(8,128)(2,1)S(1)}, u32[]{:S(2)}, u32[]{:S(2)}) collective-permute-start(bf16[6,64,128]{2,1,0:T(8,128)(2,1)S(1)} %get-tuple-element.37), channel_id=1, source_target_pairs={{4,0},{8,4},{12,8},{16,12},{20,16},{24,20},{28,24},{32,28},{36,32}... | collective-permute-start | bytes 294920 | tf_op jit(solution)/shard_map/ppermute | solution.py:287
  8.1 0.7 fusion.3
  8.8 0.9 convert_reduce_fusion
  9.7 0.7 multiply_add_fusion.slot_ref
  10.4 0.9 %broadcast_and_fusion = (s32[256,128]{1,0:T(8,128)S(1)}, s32[256,128]{1,0:T(8,128)S(1)}) fusion(s32[256,128]{1,0:T(8,128)} %param.11), kind=kLoop, calls=%fused_computation.10 | loop fusion | flops 196608 | bytes 393216 | tf_op jit(solution)/shard_map/and | solution.py:310
  11.3 0.8 cosine_bitcast_fusion
  12.1 0.0 collective-permute-done
  12.1 0.0 collective-permute-done.1
  12.2 3.5 %collective-permute-start.2 = (bf16[20,8,128]{2,1,0:T(8,128)(2,1)S(1)}, bf16[20,8,128]{2,1,0:T(8,128)(2,1)S(1)}, u32[]{:S(2)}, u32[]{:S(2)}) collective-permute-start(bf16[20,8,128]{2,1,0:T(8,128)(2,1)S(1)} %pad_maximum_fusion.2), channel_id=1, source_target_pairs={{0,1},{1,2},{2,3},{4,5},{5,6},{6,7},{8,9},{9,10},{10,11},{12,13},{... | collective-permute-start | bytes 122888 | tf_op jit(solution)/shard_map/ppermute | solution.py:287
  15.7 1.3 %collective-permute-start.3 = (bf16[20,8,128]{2,1,0:T(8,128)(2,1)S(1)}, bf16[20,8,128]{2,1,0:T(8,128)(2,1)S(1)}, u32[]{:S(2)}, u32[]{:S(2)}) collective-permute-start(bf16[20,8,128]{2,1,0:T(8,128)(2,1)S(1)} %pad_maximum_fusion.3), channel_id=1, source_target_pairs={{1,0},{2,1},{3,2},{5,4},{6,5},{7,6},{9,8},{10,9},{11,10},{13,12},{... | collective-permute-start | bytes 122888 | tf_op jit(solution)/shard_map/ppermute | solution.py:287
  17.0 0.9 %pad_maximum_fusion.center_ref = bf16[20,64,128]{2,1,0:T(8,128)(2,1)S(1)} fusion(bf16[6,64,128]{2,1,0:T(8,128)(2,1)S(1)} %collective-permute-done.1, bf16[8,64,128]{2,1,0:T(8,128)(2,1)} %param.9, bf16[6,64,128]{2,1,0:T(8,128)(2,1)S(1)} %collective-permute-done), kind=kLoop, calls=%fused_computation | loop fusion | flops 327680 | bytes 655360 | tf_op jit(solution)/shard_map/concatenate | solution.py:316
  18.0 0.0 collective-permute-done.2.left_ref
  18.0 2.7 %collective-permute-done.3.right_ref = bf16[20,8,128]{2,1,0:T(8,128)(2,1)S(1)} collective-permute-done((bf16[20,8,128]{2,1,0:T(8,128)(2,1)S(1)}, bf16[20,8,128]{2,1,0:T(8,128)(2,1)S(1)}, u32[]{:S(2)}, u32[]{:S(2)}) %collective-permute-start.3) | collective-permute-done | bytes 40992 | tf_op jit(solution)/shard_map/ppermute | solution.py:287
  20.7 32.1 %sample.1 = (bf16[6144,128]{1,0:T(8,128)(2,1)}, bf16[2,512,768]{2,1,0:T(8,128)(2,1)S(1)}) custom-call(s32[256]{0:T(256)S(1)} %multiply_add_fusion.slot_ref, s32[256,128]{1,0:T(8,128)S(1)} %get-tuple-element.33.rows_ref, bf16[20,64,128]{2,1,0:T(8,128)(2,1)S(1)} %pad_maximum_fusion.center_ref, bf16[20,8,128]{2,1,0:T(8,128)(2,1)S(1)} %collective-permute-done.2.left_ref, ...), custom_call_target="tpu_custom_call" | custom-call | flops 4000000000 | bytes 8000000 | tf_op jit(solution)/shard_map/sample/pallas_call | solution.py:323
  52.7 11.4 %all-to-all-start = ((bf16[128,48,128]{2,1,0:T(8,128)(2,1)}), bf16[128,48,128]{2,1,0:T(8,128)(2,1)S(1)}, u32[]{:S(2)}, u32[]{:S(2)}) async-start(bf16[128,48,128]{2,1,0:T(8,128)(2,1)} %bitcast.5), calls=%async_computation | async-start | bytes 3145728 | tf_op jit(solution)/shard_map/all_to_all | solution.py:349
  64.2 0.1 copy.41
  64.3 0.1 copy.33
  64.3 0.1 copy.31
  64.4 0.1 copy.35
  64.5 0.1 stack.4
  64.6 0.5 scatter.9
  65.1 0.1 copy.42
  65.2 1.3 %tile.4 = f32[16,16,16,12]{1,0,3,2:T(8,128)} broadcast(f32[16,12]{0,1:T(8,128)S(1)} %copy.42), dimensions={1,3} | broadcast | bytes 197376 | tf_op jit(solution)/shard_map/tile | solution.py:295
  66.5 2.7 %tile.10 = f32[1,256,192]{1,2,0:T(8,128)} reshape(f32[16,16,16,12]{1,0,3,2:T(8,128)} %tile.4) | data formatting | bytes 393216 | tf_op jit(solution)/shard_map/tile | solution.py:295
  69.2 1.1 %copy.43 = f32[1,256,192]{2,1,0:T(8,128)S(1)} copy(f32[1,256,192]{1,2,0:T(8,128)} %tile.10) | data formatting | bytes 393216 | tf_op jit(solution)/shard_map/tile | solution.py:295
  70.3 0.2 subtract_convert_fusion
  70.5 0.2 fusion.2
  70.7 0.0 copy-start
  70.7 0.9 %copy-done = bf16[2,3,128,128]{3,2,1,0:T(8,128)(2,1)S(1)} copy-done((bf16[2,3,128,128]{3,2,1,0:T(8,128)(2,1)S(1)}, bf16[2,3,128,128]{3,2,1,0:T(8,128)(2,1)}, u32[]{:S(2)}) %copy-start) | copy-done | bytes 196632
  71.6 5.4 %respond.1 = bf16[16,8,64,128]{3,2,1,0:T(8,128)(2,1)} custom-call(f32[8,6]{1,0:T(8,128)S(1)} %broadcast_multiply_fusion.weight_ref, bf16[2,512,768]{2,1,0:T(8,128)(2,1)S(1)} %get-tuple-element.28.fields_ref, bf16[2,3,128,128]{3,2,1,0:T(8,128)(2,1)S(1)} %copy-done), custom_call_target="tpu_custom_call" | custom-call | flops 200000000 | bytes 4000000 | tf_op jit(solution)/shard_map/respond/pallas_call | solution.py:353
  77.0 12.1 %all-to-all-done = bf16[128,48,128]{2,1,0:T(8,128)(2,1)S(1)} async-done(((bf16[128,48,128]{2,1,0:T(8,128)(2,1)}), bf16[128,48,128]{2,1,0:T(8,128)(2,1)S(1)}, u32[]{:S(2)}, u32[]{:S(2)}) %all-to-all-start) | async-done | bytes 1572896 | tf_op jit(solution)/shard_map/all_to_all | solution.py:349
  89.1 2.1 %mix.1 = bf16[8192,128]{1,0:T(8,128)(2,1)} custom-call(bf16[2,256,192]{2,1,0:T(8,128)(2,1)S(1)} %pad_maximum_fusion.1.mix_ref, bf16[6144,128]{1,0:T(8,128)(2,1)S(1)} %bitcast.16), custom_call_target="tpu_custom_call" | custom-call | flops 1600000000 | bytes 4000000 | tf_op jit(solution)/shard_map/mix/pallas_call | solution.py:368
  (13 shorter events, 0.1 us)
Async XLA Ops:
  1.6 10.5 %collective-permute-start = (bf16[6,64,128]{2,1,0:T(8,128)(2,1)S(1)}, bf16[6,64,128]{2,1,0:T(8,128)(2,1)S(1)}, u32[]{:S(2)}, u32[]{:S(2)}) collective-permute-start(bf16[6,64,128]{2,1,0:T(8,128)(2,1)S(1)} %get-tuple-element.36), channel_id=1, source_target_pairs={{0,4},{4,8},{8,12},{12,16},{16,20},{20,24},{24,28},{28,32},{32,36}... | collective-permute-start | bytes 294920 | tf_op jit(solution)/shard_map/ppermute | solution.py:287
  6.1 6.0 %collective-permute-start.1 = (bf16[6,64,128]{2,1,0:T(8,128)(2,1)S(1)}, bf16[6,64,128]{2,1,0:T(8,128)(2,1)S(1)}, u32[]{:S(2)}, u32[]{:S(2)}) collective-permute-start(bf16[6,64,128]{2,1,0:T(8,128)(2,1)S(1)} %get-tuple-element.37), channel_id=1, source_target_pairs={{4,0},{8,4},{12,8},{16,12},{20,16},{24,20},{28,24},{32,28},{36,32}... | collective-permute-start | bytes 294920 | tf_op jit(solution)/shard_map/ppermute | solution.py:287
  12.2 5.8 %collective-permute-start.2 = (bf16[20,8,128]{2,1,0:T(8,128)(2,1)S(1)}, bf16[20,8,128]{2,1,0:T(8,128)(2,1)S(1)}, u32[]{:S(2)}, u32[]{:S(2)}) collective-permute-start(bf16[20,8,128]{2,1,0:T(8,128)(2,1)S(1)} %pad_maximum_fusion.2), channel_id=1, source_target_pairs={{0,1},{1,2},{2,3},{4,5},{5,6},{6,7},{8,9},{9,10},{10,11},{12,13},{... | collective-permute-start | bytes 122888 | tf_op jit(solution)/shard_map/ppermute | solution.py:287
  15.7 4.9 %collective-permute-start.3 = (bf16[20,8,128]{2,1,0:T(8,128)(2,1)S(1)}, bf16[20,8,128]{2,1,0:T(8,128)(2,1)S(1)}, u32[]{:S(2)}, u32[]{:S(2)}) collective-permute-start(bf16[20,8,128]{2,1,0:T(8,128)(2,1)S(1)} %pad_maximum_fusion.3), channel_id=1, source_target_pairs={{1,0},{2,1},{3,2},{5,4},{6,5},{7,6},{9,8},{10,9},{11,10},{13,12},{... | collective-permute-start | bytes 122888 | tf_op jit(solution)/shard_map/ppermute | solution.py:287
  52.7 36.4 %all-to-all-start = ((bf16[128,48,128]{2,1,0:T(8,128)(2,1)}), bf16[128,48,128]{2,1,0:T(8,128)(2,1)S(1)}, u32[]{:S(2)}, u32[]{:S(2)}) async-start(bf16[128,48,128]{2,1,0:T(8,128)(2,1)} %bitcast.5), calls=%async_computation | async-start | bytes 3145728 | tf_op jit(solution)/shard_map/all_to_all | solution.py:349
  70.7 0.9 %copy-start = (bf16[2,3,128,128]{3,2,1,0:T(8,128)(2,1)S(1)}, bf16[2,3,128,128]{3,2,1,0:T(8,128)(2,1)}, u32[]{:S(2)}) copy-start(bf16[2,3,128,128]{3,2,1,0:T(8,128)(2,1)} %constant.99.clone.x_band_ref) | copy-start | bytes 589828

commit v4 on v3

--- a/solution.py
+++ b/solution.py
@@ -23,9 +23,11 @@
 LANES = 128
 TILES = 256
 PTS = 128
-STEP_TILES = 16
+STEP_TILES = 32
 STEPS = TILES // STEP_TILES
 GROUP = 4
+PART = 512
+PACK_PARTS = 4
 OWNERS = 128
 SLOTS = OWNERS * CAP
 SEND_ROWS = CAP * 2 * COMPS
@@ -105,27 +107,27 @@
     return result.astype(ml_dtypes.bfloat16)
 
 
-def z_pass(y_fields, s, kind_y, kinds_z, z):
+def z_pass(planes, s, kinds, z):
     d = SPACINGS[s]
-    planes = [y_fields[z + BORDER - k * d, s, kind_y] for k in range(-TAPS_PER_SIDE, TAPS_PER_SIDE + 1)]
     results = {}
-    for kind in kinds_z:
+    for kind in kinds:
         total = None
         for side in range(TAPS_PER_SIDE):
-            pair = planes[side] - planes[6 - side] if kind == 1 else planes[side] + planes[6 - side]
             if TAPS[kind, side] == 0.0:
                 continue
-            term = float(TAPS[kind, side]) * pair
+            shift = (side - TAPS_PER_SIDE) * d
+            near, far = planes[z + BORDER - shift], planes[z + BORDER + shift]
+            term = float(TAPS[kind, side]) * (near - far if kind == 1 else near + far)
             total = term if total is None else total + term
         if kind != 1:
-            total = total + float(TAPS[kind, TAPS_PER_SIDE]) * planes[TAPS_PER_SIDE]
+            total = total + float(TAPS[kind, TAPS_PER_SIDE]) * planes[z + BORDER]
         results[kind] = total
     return results
 
 
 def sample_kernel(
-    slot_ref, rows_ref, center_ref, left_ref, right_ref, column_ref, send_ref, fields_ref, ext, y_fields, bands, table, tiles,
-    y_band, smoother, index_rows, sem
+    slot_ref, rows_ref, center_ref, first_ref, second_ref, column_ref, send_hbm, fields_ref, ext, y_fields, bands, table, tiles,
+    y_band, smoother, send, index_rows, sem, send_sem
 ):
     def copy_rows(step, side):
         return pltpu.make_async_copy(
@@ -136,8 +138,9 @@
     copy_rows(1, 1).start()
 
     ext[:, Y_PAD:Y_PAD + CY, :] = center_ref[...]
-    ext[:, 0:Y_PAD, :] = left_ref[...]
-    ext[:, Y_PAD + CY:TALL, :] = right_ref[...]
+    even = (lax.axis_index("narrow") & 1) == 0
+    ext[:, 0:Y_PAD, :] = jnp.where(even, second_ref[...], first_ref[...])
+    ext[:, Y_PAD + CY:TALL, :] = jnp.where(even, first_ref[...], second_ref[...])
     tiles[...] = jnp.zeros_like(tiles)
     fill_y_band(y_band)
     fill_x_bands(bands)
@@ -152,17 +155,23 @@
                 y_fields[z + 1, s, kind] = out[kind * CY:(kind + 1) * CY, NX:2 * NX]
 
     for s in range(2):
-        for z in range(SZ):
-            passed = [z_pass(y_fields, s, 0, (0, 1, 2), z), z_pass(y_fields, s, 1, (0, 1), z), z_pass(y_fields, s, 2, (0,), z)]
-            for comp, (_, kind_y, kind_z) in enumerate(KINDS):
-                fields_ref[s, z * CY:(z + 1) * CY, comp * NX:(comp + 1) * NX] = passed[kind_y][kind_z].astype(jnp.bfloat16)
-
-    lower = index((ROWS // 2, LANES), 1) < 64
+        for y in range(0, CY, 8):
+            for kind_y, kinds_z in ((0, (0, 1, 2)), (1, (0, 1)), (2, (0,))):
+                planes = [y_fields[z, s, kind_y, y:y + 8, :] for z in range(DEEP)]
+                for z in range(SZ):
+                    passed = z_pass(planes, s, kinds_z, z)
+                    for comp, (_, comp_y, comp_z) in enumerate(KINDS):
+                        if comp_y == kind_y:
+                            fields_ref[s, z * CY + y:z * CY + y + 8, comp * NX:(comp + 1) * NX] = (
+                                passed[comp_z].astype(jnp.bfloat16)
+                            )
+
+    lower = index((PART, LANES), 1) < 64
     for m in range(0, NX // 16, 2):
-        for part in range(0, ROWS, ROWS // 2):
+        for part in range(0, ROWS, PART):
             outs = [
                 jnp.dot(
-                    fields_ref[s, part:part + ROWS // 2, :], bands[s, :, m * LANES:(m + 2) * LANES],
+                    fields_ref[s, part:part + PART, :], bands[s, :, m * LANES:(m + 2) * LANES],
                     preferred_element_type=jnp.float32,
                 )
                 for s in range(2)
@@ -170,8 +179,8 @@
             for half in range(2):
                 first, second = (out[:, half * LANES:(half + 1) * LANES] for out in outs)
                 start = 8 + (m + half) * 2 * ROWS + part
-                table[start:start + ROWS // 2, :] = jnp.where(lower, first, second)
-                table[start + ROWS:start + ROWS + ROWS // 2, :] = jnp.where(lower, second, first)
+                table[start:start + PART, :] = jnp.where(lower, first, second)
+                table[start + ROWS:start + ROWS + PART, :] = jnp.where(lower, second, first)
 
     eye = (index((LANES, LANES), 0) == index((LANES, LANES), 1)).astype(jnp.bfloat16)
     sublane = index((8, LANES), 0)
@@ -216,14 +225,21 @@
     copy_rows(0, 0).wait()
     copy_rows(0, 1).wait()
     pack = pack_matrix()
-
-    @pl.loop(0, OWNERS // 8)
-    def _(oct):
-        for quad in range(2):
-            here = tiles[pl.ds(oct * 32 + quad * 16, 16)].reshape(256, PTS)
-            packed = jnp.dot(pack, here, preferred_element_type=jnp.float32).astype(jnp.bfloat16)
-            start = pl.multiple_of(oct * 8 * SEND_ROWS, 8 * SEND_ROWS) + quad * 4 * SEND_ROWS
-            send_ref[pl.ds(start, 4 * SEND_ROWS), :] = packed
+    rows = SEND_ROWS * OWNERS // PACK_PARTS
+    copies = []
+    for part in range(PACK_PARTS):
+        for pair in range(part * 16 // PACK_PARTS, (part + 1) * 16 // PACK_PARTS):
+            quads = [tiles[pair * 32 + quad * 16:pair * 32 + (quad + 1) * 16].reshape(256, PTS) for quad in range(2)]
+            packed = jnp.dot(pack, jnp.concatenate(quads, axis=1), preferred_element_type=jnp.float32).astype(jnp.bfloat16)
+            for quad in range(2):
+                start = (pair * 2 + quad) * 4 * SEND_ROWS
+                send[start:start + 4 * SEND_ROWS, :] = packed[:, quad * PTS:(quad + 1) * PTS]
+        here = slice(part * rows, (part + 1) * rows)
+        copy = pltpu.make_async_copy(send.at[here, :], send_hbm.at[here, :], send_sem.at[part])
+        copy.start()
+        copies.append(copy)
+    for copy in copies:
+        copy.wait()
 
 
 def response_kernel(weight_ref, fields_ref, x_band_ref, out_ref):
@@ -280,11 +296,11 @@
     )
 
 
-def shifted(value, axis, step):
-    count = lax.axis_size(axis)
-    forward = [(i, i + 1) for i in range(count - 1)]
-    backward = [(i + 1, i) for i in range(count - 1)]
-    return lax.ppermute(value, axis, forward if step > 0 else backward)
+def swap(value, axis, first):
+    pairs = []
+    for i in range(first, lax.axis_size(axis) - 1, 2):
+        pairs += [(i, i + 1), (i + 1, i)]
+    return lax.ppermute(value, axis, pairs)
 
 
 def mix_matrix(weights):
@@ -299,12 +315,15 @@
 
 
 def per_device(volume, angles, tile_points, tile_dest):
-    low = shifted(volume[SZ - BORDER:], "wide", 1)
-    high = shifted(volume[:BORDER], "wide", -1)
-    edge_low = jnp.concatenate([part[:, CY - Y_PAD:] for part in (low, volume, high)], axis=0)
-    edge_high = jnp.concatenate([part[:, :Y_PAD] for part in (low, volume, high)], axis=0)
-    left = shifted(edge_low, "narrow", 1)
-    right = shifted(edge_high, "narrow", -1)
+    even_wide = (lax.axis_index("wide") & 1) == 0
+    even_narrow = (lax.axis_index("narrow") & 1) == 0
+    first, second = swap(volume, "wide", 0), swap(volume, "wide", 1)
+    low = jnp.where(even_wide, second, first)[SZ - BORDER:]
+    high = jnp.where(even_wide, first, second)[:BORDER]
+    center = jnp.concatenate([low, volume, high], axis=0)
+    edge_low, edge_high = center[:, :Y_PAD], center[:, CY - Y_PAD:]
+    side_first = swap(jnp.where(even_narrow, edge_high, edge_low), "narrow", 0)
+    side_second = swap(jnp.where(even_narrow, edge_low, edge_high), "narrow", 1)
 
     table_rows = ((tile_points >> 3) & 15) * ROWS + (tile_points >> 7)
     columns = tile_points & 15
@@ -313,7 +332,6 @@
     later = lax.broadcasted_iota(jnp.int32, (TILES, TILES), 1)
     same_owner = (dest[:, None] == dest[None, :]) & (earlier < later)
     slot = dest * CAP + jnp.sum(same_owner.astype(jnp.int32), axis=0)
-    center = jnp.concatenate([low, volume, high], axis=0)
 
     weights = orientation_weights(angles)
     mix = mix_matrix(weights)
@@ -327,7 +345,7 @@
             jax.ShapeDtypeStruct((2, ROWS, COMPS * NX), jnp.bfloat16),
         ),
         in_specs=[pl.BlockSpec(memory_space=pltpu.SMEM)] + [vmem] * 5,
-        out_specs=(vmem, vmem),
+        out_specs=(hbm, vmem),
         scratch_shapes=[
             pltpu.VMEM((DEEP, TALL, NX), jnp.bfloat16),
             pltpu.VMEM((DEEP, 2, 3, CY, NX), jnp.float32),
@@ -336,14 +354,16 @@
             pltpu.VMEM((SLOTS, 16, PTS), jnp.bfloat16),
             pltpu.VMEM((6 * CY, TALL), jnp.bfloat16),
             pltpu.VMEM((PTS, PTS), jnp.bfloat16),
+            pltpu.VMEM((OWNERS * SEND_ROWS, PTS), jnp.bfloat16),
             [pltpu.SMEM((STEP_TILES, PTS), jnp.int32)] * 2,
             pltpu.SemaphoreType.DMA((2,)),
+            pltpu.SemaphoreType.DMA((PACK_PARTS,)),
         ],
         compiler_params=pltpu.CompilerParams(vmem_limit_bytes=32 << 20),
         cost_estimate=pl.CostEstimate(flops=4_000_000_000, bytes_accessed=8_000_000, transcendentals=0),
         name="sample",
     )(
-        slot, table_rows, center, left, right, columns,
+        slot, table_rows, center, side_first, side_second, columns,
     )
 
     arrived = lax.all_to_all(

time: 91.7 us -> 79.9 us (0.87)
  Pallas kernels: 39.5 us -> 34.1 us
  starting transfers between devices: 22.7 us -> 19.8 us
  local copies, waits for them, and re-layouts: 8.69 us -> 6.94 us
  waiting for transfers between devices: 14.8 us -> 13.7 us
    pallas_call x1, Pallas kernels: 32.1 us -> 26.7 us  [per_device(): pl.pallas_call(sample_kernel, out_shape=(jax.ShapeDtypeStruct((OWNERS * S...]
    slice x4 -> x0, local copies, waits for them, and re-layouts: 1.74 us -> none  [the longest x1 0.99 us: per_device(): low = shifted(volume[SZ - BORDER:], 'wide', 1)]
    all_to_all x1, starting transfers between devices: 11.4 us -> 9.97 us  [per_device(): lax.all_to_all(send.reshape(OWNERS, SEND_ROWS, PTS), ('wide', 'narrow'),...]
    ppermute x4, starting transfers between devices: 11.3 us -> 9.86 us  [swap(): return lax.ppermute(value, axis, pairs)]
    ppermute x4, waiting for transfers between devices: 2.68 us -> 1.58 us  [swap(): return lax.ppermute(value, axis, pairs)]
  transfers between devices with their start and end apart: 5 -> 5, of which waited for: 2 -> 3; matrix products, arithmetic and copies ran while one was open for 13% -> 11% of each run, Pallas kernels for 6% -> 7%
where the time goes in v4:
time: 79.9 us; the launch traced here: 79.5 us
  Pallas kernels  34.1 us (43%)
  starting transfers between devices  19.8 us (25%)
  waiting for transfers between devices  13.7 us (17%)
  local copies, waits for them, and re-layouts  6.94 us (9%)
  other arithmetic  3.96 us (5%)
  between operations  0.96 us (1%)
    pallas_call x1, Pallas kernels, per_device(): pl.pallas_call(sample_kernel, out_shape=(jax.ShapeDtypeStruct((OWNERS * S...  26.7 us
    all_to_all x1, waiting for transfers between devices, per_device(): lax.all_to_all(send.reshape(OWNERS, SEND_ROWS, PTS), ('wide', 'narrow'),...  12.1 us
    all_to_all x1, starting transfers between devices, per_device(): lax.all_to_all(send.reshape(OWNERS, SEND_ROWS, PTS), ('wide', 'narrow'),...  9.97 us
    ppermute x4, starting transfers between devices, swap(): return lax.ppermute(value, axis, pairs)  9.86 us
    pallas_call x1, Pallas kernels, per_device(): pl.pallas_call(response_kernel, grid=(SZ,), out_shape=jax.ShapeDtypeStruc...  5.38 us
    another operation x3, local copies, waits for them, and re-layouts, mix_matrix(): full = jnp.where(rows == columns, jnp.tile(scales, (16, 16)), 0.0)  5 us
    pallas_call x1, Pallas kernels, per_device(): pl.pallas_call(mix_kernel, out_shape=jax.ShapeDtypeStruct((SLOTS * 16, PT...  2.09 us
  transfers between devices with their start and end apart: 5, of which 3 were waited for; matrix products, arithmetic and copies ran while one was open for 11% of the time, Pallas kernels for 7%

profile of v4, /device:TPU:1, one launch (start us, length us, event | category | flops | bytes accessed | tf_op | source)
XLA Modules:
  0.0 79.5 jit_solution(9662970664079721313)
XLA Ops:
  0.6 0.0 copy-start.1
  0.6 4.5 %collective-permute-start = (bf16[8,64,128]{2,1,0:T(8,128)(2,1)}, bf16[8,64,128]{2,1,0:T(8,128)(2,1)S(1)}, u32[]{:S(2)}, u32[]{:S(2)}) collective-permute-start(bf16[8,64,128]{2,1,0:T(8,128)(2,1)} %param.9), channel_id=1, source_target_pairs={{4,8},{8,4},{12,16},{16,12},{20,24},{24,20},{28,32},{32,28},{36,40... | collective-permute-start | bytes 393224 | tf_op jit(solution)/shard_map/ppermute | solution.py:303
  5.2 0.1 collective-permute-start.1
  5.3 0.9 %convert_reduce_fusion = s32[256]{0:T(256)S(1)} fusion(s32[256]{0:T(256)} %bitcast.17), kind=kLoop, calls=%fused_computation.4 | loop fusion | flops 327424 | bytes 2048 | tf_op jit(solution)/shard_map/reduce_sum | solution.py:334
  6.1 0.9 %broadcast_and_fusion = (s32[256,128]{1,0:T(8,128)S(1)}, s32[256,128]{1,0:T(8,128)S(1)}) fusion(s32[256,128]{1,0:T(8,128)} %param.11), kind=kLoop, calls=%fused_computation.12 | loop fusion | flops 196608 | bytes 393216 | tf_op jit(solution)/shard_map/and | solution.py:329
  7.1 0.7 multiply_add_fusion.slot_ref
  7.8 0.2 collective-permute-done
  8.0 0.0 collective-permute-done.1
  8.0 0.9 %pad_maximum_fusion.center_ref = bf16[20,64,128]{2,1,0:T(8,128)(2,1)S(1)} fusion(bf16[6,64,128]{2,1,0:T(8,128)(2,1)S(1)} %get-tuple-element.35, bf16[8,64,128]{2,1,0:T(8,128)(2,1)} %param.9, bf16[6,64,128]{2,1,0:T(8,128)(2,1)S(1)} %get-tuple-element.34), kind=kLoop, calls=%fused_computation | loop fusion | flops 327680 | bytes 655360 | tf_op jit(solution)/shard_map/concatenate | solution.py:323
  9.0 0.7 collective-permute-start.3
  9.7 4.6 %collective-permute-start.2 = (bf16[20,8,128]{2,1,0:T(8,128)(2,1)S(1)}, bf16[20,8,128]{2,1,0:T(8,128)(2,1)S(1)}, u32[]{:S(2)}, u32[]{:S(2)}) collective-permute-start(bf16[20,8,128]{2,1,0:T(8,128)(2,1)S(1)} %get-tuple-element.33), channel_id=1, source_target_pairs={{0,1},{1,0},{2,3},{3,2},{4,5},{5,4},{6,7},{7,6},{8,9},{9,8},{10,11... | collective-permute-start | bytes 122888 | tf_op jit(solution)/shard_map/ppermute | solution.py:303
  14.3 0.0 copy-done.1
  14.3 0.1 cosine_bitcast_fusion
  14.3 0.0 collective-permute-done.3.second_ref
  14.3 1.3 %collective-permute-done.2.first_ref = bf16[20,8,128]{2,1,0:T(8,128)(2,1)S(1)} collective-permute-done((bf16[20,8,128]{2,1,0:T(8,128)(2,1)S(1)}, bf16[20,8,128]{2,1,0:T(8,128)(2,1)S(1)}, u32[]{:S(2)}, u32[]{:S(2)}) %collective-permute-start.2) | collective-permute-done | bytes 40992 | tf_op jit(solution)/shard_map/ppermute | solution.py:303
  15.7 26.7 %sample.1 = (bf16[6144,128]{1,0:T(8,128)(2,1)}, bf16[2,512,768]{2,1,0:T(8,128)(2,1)S(1)}) custom-call(s32[256]{0:T(256)S(1)} %multiply_add_fusion.slot_ref, s32[256,128]{1,0:T(8,128)S(1)} %get-tuple-element.37.rows_ref, bf16[20,64,128]{2,1,0:T(8,128)(2,1)S(1)} %pad_maximum_fusion.center_ref, bf16[20,8,128]{2,1,0:T(8,128)(2,1)S(1)} %collective-permute-done.2.first_ref, ...), custom_call_target="tpu_custom_call" | custom-call | flops 4000000000 | bytes 8000000 | tf_op jit(solution)/shard_map/sample/pallas_call | solution.py:341
  42.4 10.0 %all-to-all-start = ((bf16[128,48,128]{2,1,0:T(8,128)(2,1)}), bf16[128,48,128]{2,1,0:T(8,128)(2,1)S(1)}, u32[]{:S(2)}, u32[]{:S(2)}) async-start(bf16[128,48,128]{2,1,0:T(8,128)(2,1)} %bitcast.5), calls=%async_computation | async-start | bytes 3145728 | tf_op jit(solution)/shard_map/all_to_all | solution.py:369
  52.3 0.1 copy.41
  52.4 0.1 copy.33
  52.5 0.1 copy.31
  52.6 0.1 copy.35
  52.7 0.1 stack.4
  52.8 0.5 scatter.9
  53.3 0.1 copy.42
  53.4 1.3 %tile.4 = f32[16,16,16,12]{1,0,3,2:T(8,128)} broadcast(f32[16,12]{0,1:T(8,128)S(1)} %copy.42), dimensions={1,3} | broadcast | bytes 197376 | tf_op jit(solution)/shard_map/tile | solution.py:311
  54.7 2.6 %tile.10 = f32[1,256,192]{1,2,0:T(8,128)} reshape(f32[16,16,16,12]{1,0,3,2:T(8,128)} %tile.4) | data formatting | bytes 393216 | tf_op jit(solution)/shard_map/tile | solution.py:311
  57.3 1.1 %copy.43 = f32[1,256,192]{2,1,0:T(8,128)S(1)} copy(f32[1,256,192]{1,2,0:T(8,128)} %tile.10) | data formatting | bytes 393216 | tf_op jit(solution)/shard_map/tile | solution.py:311
  58.4 0.2 subtract_convert_fusion
  58.6 0.2 fusion.2
  58.9 0.0 copy-start
  58.9 0.9 %copy-done = bf16[2,3,128,128]{3,2,1,0:T(8,128)(2,1)S(1)} copy-done((bf16[2,3,128,128]{3,2,1,0:T(8,128)(2,1)S(1)}, bf16[2,3,128,128]{3,2,1,0:T(8,128)(2,1)}, u32[]{:S(2)}) %copy-start) | copy-done | bytes 196632
  59.8 5.4 %respond.1 = bf16[16,8,64,128]{3,2,1,0:T(8,128)(2,1)} custom-call(f32[8,6]{1,0:T(8,128)S(1)} %broadcast_multiply_fusion.weight_ref, bf16[2,512,768]{2,1,0:T(8,128)(2,1)S(1)} %get-tuple-element.28.fields_ref, bf16[2,3,128,128]{3,2,1,0:T(8,128)(2,1)S(1)} %copy-done), custom_call_target="tpu_custom_call" | custom-call | flops 200000000 | bytes 4000000 | tf_op jit(solution)/shard_map/respond/pallas_call | solution.py:373
  65.2 12.1 %all-to-all-done = bf16[128,48,128]{2,1,0:T(8,128)(2,1)S(1)} async-done(((bf16[128,48,128]{2,1,0:T(8,128)(2,1)}), bf16[128,48,128]{2,1,0:T(8,128)(2,1)S(1)}, u32[]{:S(2)}, u32[]{:S(2)}) %all-to-all-start) | async-done | bytes 1572896 | tf_op jit(solution)/shard_map/all_to_all | solution.py:369
  77.3 2.1 %mix.1 = bf16[8192,128]{1,0:T(8,128)(2,1)} custom-call(bf16[2,256,192]{2,1,0:T(8,128)(2,1)S(1)} %pad_maximum_fusion.1.mix_ref, bf16[6144,128]{1,0:T(8,128)(2,1)S(1)} %bitcast.16), custom_call_target="tpu_custom_call" | custom-call | flops 1600000000 | bytes 4000000 | tf_op jit(solution)/shard_map/mix/pallas_call | solution.py:388
  (11 shorter events, 0.1 us)
Async XLA Ops:
  0.6 13.7 %copy-start.1 = (f32[2,8]{1,0:T(2,128)S(1)}, f32[2,8]{1,0:T(2,128)}, u32[]{:S(2)}) copy-start(f32[2,8]{1,0:T(2,128)} %param.10) | copy-start | bytes 196
  0.6 7.4 %collective-permute-start = (bf16[8,64,128]{2,1,0:T(8,128)(2,1)}, bf16[8,64,128]{2,1,0:T(8,128)(2,1)S(1)}, u32[]{:S(2)}, u32[]{:S(2)}) collective-permute-start(bf16[8,64,128]{2,1,0:T(8,128)(2,1)} %param.9), channel_id=1, source_target_pairs={{4,8},{8,4},{12,16},{16,12},{20,24},{24,20},{28,32},{32,28},{36,40... | collective-permute-start | bytes 393224 | tf_op jit(solution)/shard_map/ppermute | solution.py:303
  5.2 2.9 %collective-permute-start.1 = (bf16[8,64,128]{2,1,0:T(8,128)(2,1)}, bf16[8,64,128]{2,1,0:T(8,128)(2,1)S(1)}, u32[]{:S(2)}, u32[]{:S(2)}) collective-permute-start(bf16[8,64,128]{2,1,0:T(8,128)(2,1)} %param.9), channel_id=1, source_target_pairs={{0,4},{4,0},{8,12},{12,8},{16,20},{20,16},{24,28},{28,24},{32,36},... | collective-permute-start | bytes 393224 | tf_op jit(solution)/shard_map/ppermute | solution.py:303
  9.0 5.3 %collective-permute-start.3 = (bf16[20,8,128]{2,1,0:T(8,128)(2,1)S(1)}, bf16[20,8,128]{2,1,0:T(8,128)(2,1)S(1)}, u32[]{:S(2)}, u32[]{:S(2)}) collective-permute-start(bf16[20,8,128]{2,1,0:T(8,128)(2,1)S(1)} %get-tuple-element.32), channel_id=1, source_target_pairs={{1,2},{2,1},{5,6},{6,5},{9,10},{10,9},{13,14},{14,13},{17,18},{18,... | collective-permute-start | bytes 122888 | tf_op jit(solution)/shard_map/ppermute | solution.py:303
  9.7 6.0 %collective-permute-start.2 = (bf16[20,8,128]{2,1,0:T(8,128)(2,1)S(1)}, bf16[20,8,128]{2,1,0:T(8,128)(2,1)S(1)}, u32[]{:S(2)}, u32[]{:S(2)}) collective-permute-start(bf16[20,8,128]{2,1,0:T(8,128)(2,1)S(1)} %get-tuple-element.33), channel_id=1, source_target_pairs={{0,1},{1,0},{2,3},{3,2},{4,5},{5,4},{6,7},{7,6},{8,9},{9,8},{10,11... | collective-permute-start | bytes 122888 | tf_op jit(solution)/shard_map/ppermute | solution.py:303
  42.4 34.9 %all-to-all-start = ((bf16[128,48,128]{2,1,0:T(8,128)(2,1)}), bf16[128,48,128]{2,1,0:T(8,128)(2,1)S(1)}, u32[]{:S(2)}, u32[]{:S(2)}) async-start(bf16[128,48,128]{2,1,0:T(8,128)(2,1)} %bitcast.5), calls=%async_computation | async-start | bytes 3145728 | tf_op jit(solution)/shard_map/all_to_all | solution.py:369
  58.9 0.9 %copy-start = (bf16[2,3,128,128]{3,2,1,0:T(8,128)(2,1)S(1)}, bf16[2,3,128,128]{3,2,1,0:T(8,128)(2,1)}, u32[]{:S(2)}) copy-start(bf16[2,3,128,128]{3,2,1,0:T(8,128)(2,1)} %constant.109.clone.x_band_ref) | copy-start | bytes 589828

commit v5 on v4

--- a/solution.py
+++ b/solution.py
@@ -80,7 +80,7 @@
             for m in range(NX // 16):
                 first, last = max(0, 16 * m - 16), min(NX, 16 * m + 32)
                 skip = first - (16 * m - 16)
-                bands[s, comp * NX + first:comp * NX + last, m * LANES:(m + 1) * LANES] = base[skip:skip + last - first]
+                bands[s, m, comp * NX + first:comp * NX + last, :] = base[skip:skip + last - first]
 
 
 def smooth_matrix():
@@ -154,24 +154,25 @@
                 y_fields[z, s, kind] = out[kind * CY:(kind + 1) * CY, 0:NX]
                 y_fields[z + 1, s, kind] = out[kind * CY:(kind + 1) * CY, NX:2 * NX]
 
-    for s in range(2):
-        for y in range(0, CY, 8):
+    @pl.loop(0, CY // 8)
+    def _(block):
+        y = pl.multiple_of(block * 8, 8)
+        for s in range(2):
             for kind_y, kinds_z in ((0, (0, 1, 2)), (1, (0, 1)), (2, (0,))):
-                planes = [y_fields[z, s, kind_y, y:y + 8, :] for z in range(DEEP)]
+                planes = [y_fields[z, s, kind_y, pl.ds(y, 8), :] for z in range(DEEP)]
                 for z in range(SZ):
                     passed = z_pass(planes, s, kinds_z, z)
                     for comp, (_, comp_y, comp_z) in enumerate(KINDS):
                         if comp_y == kind_y:
-                            fields_ref[s, z * CY + y:z * CY + y + 8, comp * NX:(comp + 1) * NX] = (
-                                passed[comp_z].astype(jnp.bfloat16)
-                            )
+                            fields_ref[s, comp, pl.ds(z * CY + y, 8), :] = passed[comp_z].astype(jnp.bfloat16)
 
     lower = index((PART, LANES), 1) < 64
     for m in range(0, NX // 16, 2):
         for part in range(0, ROWS, PART):
             outs = [
                 jnp.dot(
-                    fields_ref[s, part:part + PART, :], bands[s, :, m * LANES:(m + 2) * LANES],
+                    jnp.concatenate([fields_ref[s, comp, part:part + PART, :] for comp in range(COMPS)], axis=1),
+                    jnp.concatenate([bands[s, m], bands[s, m + 1]], axis=1),
                     preferred_element_type=jnp.float32,
                 )
                 for s in range(2)
@@ -246,7 +247,7 @@
     for s in range(2):
         parts = [
             jnp.dot(
-                fields_ref[s, :, comp * NX:(comp + 1) * NX], x_band_ref[s, KINDS[comp][0]], preferred_element_type=jnp.float32
+                fields_ref[s, comp], x_band_ref[s, KINDS[comp][0]], preferred_element_type=jnp.float32
             )
             for comp in range(COMPS)
         ]
@@ -318,12 +319,17 @@
     even_wide = (lax.axis_index("wide") & 1) == 0
     even_narrow = (lax.axis_index("narrow") & 1) == 0
     first, second = swap(volume, "wide", 0), swap(volume, "wide", 1)
-    low = jnp.where(even_wide, second, first)[SZ - BORDER:]
-    high = jnp.where(even_wide, first, second)[:BORDER]
-    center = jnp.concatenate([low, volume, high], axis=0)
-    edge_low, edge_high = center[:, :Y_PAD], center[:, CY - Y_PAD:]
+    def extended(rows):
+        below, above = first[:, rows], second[:, rows]
+        low = jnp.where(even_wide, above, below)[SZ - BORDER:]
+        high = jnp.where(even_wide, below, above)[:BORDER]
+        return jnp.concatenate([low, volume[:, rows], high], axis=0)
+
+    edge_low, edge_high = extended(slice(0, Y_PAD)), extended(slice(CY - Y_PAD, CY))
     side_first = swap(jnp.where(even_narrow, edge_high, edge_low), "narrow", 0)
     side_second = swap(jnp.where(even_narrow, edge_low, edge_high), "narrow", 1)
+    first, second, side_first = lax.optimization_barrier((first, second, side_first))
+    center = extended(slice(0, CY))
 
     table_rows = ((tile_points >> 3) & 15) * ROWS + (tile_points >> 7)
     columns = tile_points & 15
@@ -342,14 +348,14 @@
         sample_kernel,
         out_shape=(
             jax.ShapeDtypeStruct((OWNERS * SEND_ROWS, PTS), jnp.bfloat16),
-            jax.ShapeDtypeStruct((2, ROWS, COMPS * NX), jnp.bfloat16),
+            jax.ShapeDtypeStruct((2, COMPS, ROWS, NX), jnp.bfloat16),
         ),
         in_specs=[pl.BlockSpec(memory_space=pltpu.SMEM)] + [vmem] * 5,
         out_specs=(hbm, vmem),
         scratch_shapes=[
             pltpu.VMEM((DEEP, TALL, NX), jnp.bfloat16),
             pltpu.VMEM((DEEP, 2, 3, CY, NX), jnp.float32),
-            pltpu.VMEM((2, COMPS * NX, NX * 8), jnp.bfloat16),
+            pltpu.VMEM((2, NX // 16, COMPS * NX, LANES), jnp.bfloat16),
             pltpu.VMEM((NX // 8 * ROWS + 16, LANES), jnp.float32),
             pltpu.VMEM((SLOTS, 16, PTS), jnp.bfloat16),
             pltpu.VMEM((6 * CY, TALL), jnp.bfloat16),
@@ -376,7 +382,7 @@
         out_shape=jax.ShapeDtypeStruct((16, SZ, CY, NX), jnp.bfloat16),
         in_specs=[
             pl.BlockSpec(memory_space=pltpu.SMEM),
-            pl.BlockSpec((2, CY, COMPS * NX), lambda z: (0, z, 0)),
+            pl.BlockSpec((2, COMPS, CY, NX), lambda z: (0, 0, z, 0)),
             pl.BlockSpec((2, 3, NX, NX), lambda z: (0, 0, 0, 0)),
         ],
         out_specs=pl.BlockSpec((16, 1, CY, NX), lambda z: (0, z, 0, 0)),

time: 79.9 us -> 82.3 us (1.030)
  starting transfers between devices: 19.8 us -> 22.2 us
  waiting for transfers between devices: 13.7 us -> 12.1 us
  Pallas kernels: 34.1 us -> 35 us
    all_to_all x1, starting transfers between devices: 9.97 us -> 15.1 us  [per_device(): lax.all_to_all(send.reshape(OWNERS, SEND_ROWS, PTS), ('wide', 'narrow'),...]
    ppermute x4, starting transfers between devices: 9.86 us -> 7.11 us  [swap(): return lax.ppermute(value, axis, pairs)]
    ppermute x4, waiting for transfers between devices: 1.58 us -> 0.01 us  [swap(): return lax.ppermute(value, axis, pairs)]
    concatenate x1, other arithmetic: 0.94 us -> 0.04 us  [extended(): return jnp.concatenate([low, volume[:, rows], high], axis=0)]
    pallas_call x1, Pallas kernels: 26.7 us -> 27.5 us  [per_device(): pl.pallas_call(sample_kernel, out_shape=(jax.ShapeDtypeStruct((OWNERS * S...]
  transfers between devices with their start and end apart: 5 -> 5, of which waited for: 3 -> 1; matrix products, arithmetic and copies ran while one was open for 11% -> 13% of each run, Pallas kernels for 7% -> 7%
where the time goes in v5:
time: 82.3 us; the launch traced here: 81.9 us
  Pallas kernels  35 us (43%)
  starting transfers between devices  22.2 us (27%)
  waiting for transfers between devices  12.1 us (15%)
  local copies, waits for them, and re-layouts  7.69 us (9%)
  other arithmetic  3.82 us (5%)
  between operations  1 us (1%)
    pallas_call x1, Pallas kernels, per_device(): pl.pallas_call(sample_kernel, out_shape=(jax.ShapeDtypeStruct((OWNERS * S...  27.5 us
    all_to_all x1, starting transfers between devices, per_device(): lax.all_to_all(send.reshape(OWNERS, SEND_ROWS, PTS), ('wide', 'narrow'),...  15.1 us
    all_to_all x1, waiting for transfers between devices, per_device(): lax.all_to_all(send.reshape(OWNERS, SEND_ROWS, PTS), ('wide', 'narrow'),...  12.1 us
    ppermute x4, starting transfers between devices, swap(): return lax.ppermute(value, axis, pairs)  7.11 us
    pallas_call x1, Pallas kernels, per_device(): pl.pallas_call(response_kernel, grid=(SZ,), out_shape=jax.ShapeDtypeStruc...  5.38 us
    another operation x3, local copies, waits for them, and re-layouts, mix_matrix(): full = jnp.where(rows == columns, jnp.tile(scales, (16, 16)), 0.0)  4.99 us
    pallas_call x1, Pallas kernels, per_device(): pl.pallas_call(mix_kernel, out_shape=jax.ShapeDtypeStruct((SLOTS * 16, PT...  2.09 us
  transfers between devices with their start and end apart: 5, of which 1 were waited for; matrix products, arithmetic and copies ran while one was open for 13% of the time, Pallas kernels for 7%

profile of v5, /device:TPU:1, one launch (start us, length us, event | category | flops | bytes accessed | tf_op | source)
XLA Modules:
  0.0 81.9 jit_solution(9765740129676194142)
XLA Ops:
  0.6 0.0 copy-start.1
  0.6 4.6 %collective-permute-start.1 = (bf16[8,64,128]{2,1,0:T(8,128)(2,1)}, bf16[8,64,128]{2,1,0:T(8,128)(2,1)S(1)}, u32[]{:S(2)}, u32[]{:S(2)}) collective-permute-start(bf16[8,64,128]{2,1,0:T(8,128)(2,1)} %param.9), channel_id=1, source_target_pairs={{4,8},{8,4},{12,16},{16,12},{20,24},{24,20},{28,32},{32,28},{36,40... | collective-permute-start | bytes 393224 | tf_op jit(solution)/shard_map/ppermute | solution.py:304
  5.3 0.1 collective-permute-start
  5.4 0.7 fusion.3
  6.1 0.9 %convert_reduce_fusion = s32[256]{0:T(256)S(1)} fusion(s32[256]{0:T(256)} %bitcast.17), kind=kLoop, calls=%fused_computation.4 | loop fusion | flops 327424 | bytes 2048 | tf_op jit(solution)/shard_map/reduce_sum | solution.py:340
  7.0 0.9 %broadcast_and_fusion = (s32[256,128]{1,0:T(8,128)S(1)}, s32[256,128]{1,0:T(8,128)S(1)}) fusion(s32[256,128]{1,0:T(8,128)} %param.11), kind=kLoop, calls=%fused_computation.12 | loop fusion | flops 196608 | bytes 393216 | tf_op jit(solution)/shard_map/and | solution.py:335
  7.9 0.7 multiply_add_fusion.slot_ref
  8.6 0.0 collective-permute-done.1
  8.6 0.0 collective-permute-done
  8.7 1.7 %collective-permute-start.2 = (bf16[20,8,128]{2,1,0:T(8,128)(2,1)S(1)}, bf16[20,8,128]{2,1,0:T(8,128)(2,1)S(1)}, u32[]{:S(2)}, u32[]{:S(2)}) collective-permute-start(bf16[20,8,128]{2,1,0:T(8,128)(2,1)S(1)} %get-tuple-element.49), channel_id=1, source_target_pairs={{0,1},{1,0},{2,3},{3,2},{4,5},{5,4},{6,7},{7,6},{8,9},{9,8},{10,11... | collective-permute-start | bytes 122888 | tf_op jit(solution)/shard_map/ppermute | solution.py:304
  10.4 0.8 cosine_bitcast_fusion
  11.2 0.7 collective-permute-start.3
  11.9 0.0 collective-permute-done.2.first_ref
  11.9 0.0 copy-done.1
  12.0 0.0 collective-permute-done.3.second_ref
  12.0 27.5 %sample.1 = (bf16[6144,128]{1,0:T(8,128)(2,1)}, bf16[2,6,512,128]{3,2,1,0:T(8,128)(2,1)S(1)}) custom-call(s32[256]{0:T(256)S(1)} %multiply_add_fusion.slot_ref, s32[256,128]{1,0:T(8,128)S(1)} %get-tuple-element.41.rows_ref, bf16[20,64,128]{2,1,0:T(8,128)(2,1)S(1)} %pad_maximum_fusion.center_ref, bf16[20,8,128]{2,1,0:T(8,128)(2,1)S(1)} %collective-permute-done.2.first_ref, ...), custom_call_target="tpu_custom_call" | custom-call | flops 4000000000 | bytes 8000000 | tf_op jit(solution)/shard_map/sample/pallas_call | solution.py:347
  39.5 15.1 %all-to-all-start = ((bf16[128,48,128]{2,1,0:T(8,128)(2,1)}), bf16[128,48,128]{2,1,0:T(8,128)(2,1)S(1)}, u32[]{:S(2)}, u32[]{:S(2)}) async-start(bf16[128,48,128]{2,1,0:T(8,128)(2,1)} %bitcast.5), calls=%async_computation | async-start | bytes 3145728 | tf_op jit(solution)/shard_map/all_to_all | solution.py:375
  54.7 0.1 copy.41
  54.8 0.1 copy.33
  54.9 0.1 copy.31
  55.0 0.1 copy.35
  55.0 0.1 stack.4
  55.1 0.5 scatter.9
  55.7 0.1 copy.42
  55.7 1.3 %tile.4 = f32[16,16,16,12]{1,0,3,2:T(8,128)} broadcast(f32[16,12]{0,1:T(8,128)S(1)} %copy.42), dimensions={1,3} | broadcast | bytes 197376 | tf_op jit(solution)/shard_map/tile | solution.py:312
  57.0 2.6 %tile.10 = f32[1,256,192]{1,2,0:T(8,128)} reshape(f32[16,16,16,12]{1,0,3,2:T(8,128)} %tile.4) | data formatting | bytes 393216 | tf_op jit(solution)/shard_map/tile | solution.py:312
  59.7 1.1 %copy.43 = f32[1,256,192]{2,1,0:T(8,128)S(1)} copy(f32[1,256,192]{1,2,0:T(8,128)} %tile.10) | data formatting | bytes 393216 | tf_op jit(solution)/shard_map/tile | solution.py:312
  60.8 0.2 subtract_convert_fusion
  61.0 0.2 fusion.2
  61.2 0.0 copy-start
  61.2 0.9 %copy-done = bf16[2,3,128,128]{3,2,1,0:T(8,128)(2,1)S(1)} copy-done((bf16[2,3,128,128]{3,2,1,0:T(8,128)(2,1)S(1)}, bf16[2,3,128,128]{3,2,1,0:T(8,128)(2,1)}, u32[]{:S(2)}) %copy-start) | copy-done | bytes 196632
  62.1 5.4 %respond.1 = bf16[16,8,64,128]{3,2,1,0:T(8,128)(2,1)} custom-call(f32[8,6]{1,0:T(8,128)S(1)} %broadcast_multiply_fusion.weight_ref, bf16[2,6,512,128]{3,2,1,0:T(8,128)(2,1)S(1)} %get-tuple-element.34.fields_ref, bf16[2,3,128,128]{3,2,1,0:T(8,128)(2,1)S(1)} %copy-done), custom_call_target="tpu_custom_call" | custom-call | flops 200000000 | bytes 4000000 | tf_op jit(solution)/shard_map/respond/pallas_call | solution.py:379
  67.5 12.1 %all-to-all-done = bf16[128,48,128]{2,1,0:T(8,128)(2,1)S(1)} async-done(((bf16[128,48,128]{2,1,0:T(8,128)(2,1)}), bf16[128,48,128]{2,1,0:T(8,128)(2,1)S(1)}, u32[]{:S(2)}, u32[]{:S(2)}) %all-to-all-start) | async-done | bytes 1572896 | tf_op jit(solution)/shard_map/all_to_all | solution.py:375
  79.6 2.1 %mix.1 = bf16[8192,128]{1,0:T(8,128)(2,1)} custom-call(bf16[2,256,192]{2,1,0:T(8,128)(2,1)S(1)} %pad_maximum_fusion.1.mix_ref, bf16[6144,128]{1,0:T(8,128)(2,1)S(1)} %bitcast.16), custom_call_target="tpu_custom_call" | custom-call | flops 1600000000 | bytes 4000000 | tf_op jit(solution)/shard_map/mix/pallas_call | solution.py:394
  (15 shorter events, 0.2 us)
Async XLA Ops:
  0.6 11.3 %copy-start.1 = (bf16[8,64,128]{2,1,0:T(8,128)(2,1)S(1)}, bf16[8,64,128]{2,1,0:T(8,128)(2,1)}, u32[]{:S(2)}) copy-start(bf16[8,64,128]{2,1,0:T(8,128)(2,1)} %param.9) | copy-start | bytes 393220
  0.6 8.0 %collective-permute-start.1 = (bf16[8,64,128]{2,1,0:T(8,128)(2,1)}, bf16[8,64,128]{2,1,0:T(8,128)(2,1)S(1)}, u32[]{:S(2)}, u32[]{:S(2)}) collective-permute-start(bf16[8,64,128]{2,1,0:T(8,128)(2,1)} %param.9), channel_id=1, source_target_pairs={{4,8},{8,4},{12,16},{16,12},{20,24},{24,20},{28,32},{32,28},{36,40... | collective-permute-start | bytes 393224 | tf_op jit(solution)/shard_map/ppermute | solution.py:304
  5.3 3.3 %collective-permute-start = (bf16[8,64,128]{2,1,0:T(8,128)(2,1)}, bf16[8,64,128]{2,1,0:T(8,128)(2,1)S(1)}, u32[]{:S(2)}, u32[]{:S(2)}) collective-permute-start(bf16[8,64,128]{2,1,0:T(8,128)(2,1)} %param.9), channel_id=1, source_target_pairs={{0,4},{4,0},{8,12},{12,8},{16,20},{20,16},{24,28},{28,24},{32,36},... | collective-permute-start | bytes 393224 | tf_op jit(solution)/shard_map/ppermute | solution.py:304
  8.7 3.2 %collective-permute-start.2 = (bf16[20,8,128]{2,1,0:T(8,128)(2,1)S(1)}, bf16[20,8,128]{2,1,0:T(8,128)(2,1)S(1)}, u32[]{:S(2)}, u32[]{:S(2)}) collective-permute-start(bf16[20,8,128]{2,1,0:T(8,128)(2,1)S(1)} %get-tuple-element.49), channel_id=1, source_target_pairs={{0,1},{1,0},{2,3},{3,2},{4,5},{5,4},{6,7},{7,6},{8,9},{9,8},{10,11... | collective-permute-start | bytes 122888 | tf_op jit(solution)/shard_map/ppermute | solution.py:304
  11.2 0.8 collective-permute-start.3
  39.5 40.1 %all-to-all-start = ((bf16[128,48,128]{2,1,0:T(8,128)(2,1)}), bf16[128,48,128]{2,1,0:T(8,128)(2,1)S(1)}, u32[]{:S(2)}, u32[]{:S(2)}) async-start(bf16[128,48,128]{2,1,0:T(8,128)(2,1)} %bitcast.5), calls=%async_computation | async-start | bytes 3145728 | tf_op jit(solution)/shard_map/all_to_all | solution.py:375
  61.2 0.9 %copy-start = (bf16[2,3,128,128]{3,2,1,0:T(8,128)(2,1)S(1)}, bf16[2,3,128,128]{3,2,1,0:T(8,128)(2,1)}, u32[]{:S(2)}) copy-start(bf16[2,3,128,128]{3,2,1,0:T(8,128)(2,1)} %constant.109.clone.x_band_ref) | copy-start | bytes 589828

commit v6 on v4

--- a/solution.py
+++ b/solution.py
@@ -107,6 +107,14 @@
     return result.astype(ml_dtypes.bfloat16)
 
 
+def tile_slots(dest):
+    owner = jnp.broadcast_to(dest.astype(jnp.float32), (TILES, TILES))
+    other, tile = index((TILES, TILES), 0), index((TILES, TILES), 1)
+    turned = jnp.sum(jnp.where(other == tile, owner, 0.0), axis=1, keepdims=True)
+    rank = jnp.sum(jnp.where((turned == owner) & (other < tile), 1.0, 0.0), axis=0, keepdims=True)
+    return dest * CAP + rank.astype(jnp.int32)
+
+
 def z_pass(planes, s, kinds, z):
     d = SPACINGS[s]
     results = {}
@@ -126,21 +134,30 @@
 
 
 def sample_kernel(
-    slot_ref, rows_ref, center_ref, first_ref, second_ref, column_ref, send_hbm, fields_ref, ext, y_fields, bands, table, tiles,
-    y_band, smoother, send, index_rows, sem, send_sem
+    dest_ref, points_ref, block_ref, first_ref, second_ref, side_first_ref, side_second_ref, send_hbm, fields_ref, ext, y_fields, bands, table, tiles,
+    y_band, smoother, send, rows_ref, slots, slot_ref, index_rows, sem, send_sem, slot_sem
 ):
     def copy_rows(step, side):
         return pltpu.make_async_copy(
             rows_ref.at[pl.ds(pl.multiple_of(step * STEP_TILES, STEP_TILES), STEP_TILES)], index_rows[side], sem.at[side]
         )
 
+    points = points_ref[...]
+    rows_ref[...] = ((points >> 3) & 15) * ROWS + (points >> 7)
     copy_rows(0, 0).start()
     copy_rows(1, 1).start()
-
-    ext[:, Y_PAD:Y_PAD + CY, :] = center_ref[...]
+    slots[...] = tile_slots(dest_ref[...])
+    slot_copy = pltpu.make_async_copy(slots, slot_ref, slot_sem)
+    slot_copy.start()
+
+    inner = slice(Y_PAD, Y_PAD + CY)
+    even = (lax.axis_index("wide") & 1) == 0
+    ext[BORDER:BORDER + SZ, inner, :] = block_ref[...]
+    ext[0:BORDER, inner, :] = jnp.where(even, second_ref[SZ - BORDER:], first_ref[SZ - BORDER:])
+    ext[BORDER + SZ:DEEP, inner, :] = jnp.where(even, first_ref[:BORDER], second_ref[:BORDER])
     even = (lax.axis_index("narrow") & 1) == 0
-    ext[:, 0:Y_PAD, :] = jnp.where(even, second_ref[...], first_ref[...])
-    ext[:, Y_PAD + CY:TALL, :] = jnp.where(even, first_ref[...], second_ref[...])
+    ext[:, 0:Y_PAD, :] = jnp.where(even, side_second_ref[...], side_first_ref[...])
+    ext[:, Y_PAD + CY:TALL, :] = jnp.where(even, side_first_ref[...], side_second_ref[...])
     tiles[...] = jnp.zeros_like(tiles)
     fill_y_band(y_band)
     fill_x_bands(bands)
@@ -184,6 +201,7 @@
 
     eye = (index((LANES, LANES), 0) == index((LANES, LANES), 1)).astype(jnp.bfloat16)
     sublane = index((8, LANES), 0)
+    slot_copy.wait()
 
     def advance(step, side):
         copy_rows(0, side).wait()
@@ -201,7 +219,7 @@
             turned = lax.dot_general(eye, flat, (((1,), (1,)), ((), ())), preferred_element_type=jnp.float32)
             picked = []
             for t in range(GROUP):
-                column = jnp.broadcast_to(column_ref[pl.ds(step * STEP_TILES + group * GROUP + t, 1), :], (8, PTS))
+                column = jnp.broadcast_to(points_ref[pl.ds(step * STEP_TILES + group * GROUP + t, 1), :] & 15, (8, PTS))
                 here = turned[:, t * PTS:(t + 1) * PTS]
                 both = [here[0:8], here[64:72]]
                 for x in range(1, 16):
@@ -214,7 +232,7 @@
                 jnp.concatenate(picked, axis=0), smoother[...], preferred_element_type=jnp.float32
             ).astype(jnp.bfloat16)
             for t in range(GROUP):
-                tiles[slot_ref[step * STEP_TILES + group * GROUP + t]] = smooth[t * 16:(t + 1) * 16]
+                tiles[slot_ref[0, step * STEP_TILES + group * GROUP + t]] = smooth[t * 16:(t + 1) * 16]
         copy_rows(jnp.minimum(step + 2, STEPS - 1), side).start()
 
     @pl.loop(0, STEPS // 2)
@@ -318,21 +336,15 @@
     even_wide = (lax.axis_index("wide") & 1) == 0
     even_narrow = (lax.axis_index("narrow") & 1) == 0
     first, second = swap(volume, "wide", 0), swap(volume, "wide", 1)
-    low = jnp.where(even_wide, second, first)[SZ - BORDER:]
-    high = jnp.where(even_wide, first, second)[:BORDER]
-    center = jnp.concatenate([low, volume, high], axis=0)
-    edge_low, edge_high = center[:, :Y_PAD], center[:, CY - Y_PAD:]
+    def extended(rows):
+        below, above = first[:, rows], second[:, rows]
+        low = jnp.where(even_wide, above, below)[SZ - BORDER:]
+        high = jnp.where(even_wide, below, above)[:BORDER]
+        return jnp.concatenate([low, volume[:, rows], high], axis=0)
+
+    edge_low, edge_high = extended(slice(0, Y_PAD)), extended(slice(CY - Y_PAD, CY))
     side_first = swap(jnp.where(even_narrow, edge_high, edge_low), "narrow", 0)
     side_second = swap(jnp.where(even_narrow, edge_low, edge_high), "narrow", 1)
-
-    table_rows = ((tile_points >> 3) & 15) * ROWS + (tile_points >> 7)
-    columns = tile_points & 15
-    dest = tile_dest[:, 0]
-    earlier = lax.broadcasted_iota(jnp.int32, (TILES, TILES), 0)
-    later = lax.broadcasted_iota(jnp.int32, (TILES, TILES), 1)
-    same_owner = (dest[:, None] == dest[None, :]) & (earlier < later)
-    slot = dest * CAP + jnp.sum(same_owner.astype(jnp.int32), axis=0)
-
     weights = orientation_weights(angles)
     mix = mix_matrix(weights)
 
@@ -344,7 +356,7 @@
             jax.ShapeDtypeStruct((OWNERS * SEND_ROWS, PTS), jnp.bfloat16),
             jax.ShapeDtypeStruct((2, ROWS, COMPS * NX), jnp.bfloat16),
         ),
-        in_specs=[pl.BlockSpec(memory_space=pltpu.SMEM)] + [vmem] * 5,
+        in_specs=[vmem] * 7,
         out_specs=(hbm, vmem),
         scratch_shapes=[
             pltpu.VMEM((DEEP, TALL, NX), jnp.bfloat16),
@@ -355,15 +367,19 @@
             pltpu.VMEM((6 * CY, TALL), jnp.bfloat16),
             pltpu.VMEM((PTS, PTS), jnp.bfloat16),
             pltpu.VMEM((OWNERS * SEND_ROWS, PTS), jnp.bfloat16),
+            pltpu.VMEM((TILES, PTS), jnp.int32),
+            pltpu.VMEM((1, TILES), jnp.int32),
+            pltpu.SMEM((1, TILES), jnp.int32),
             [pltpu.SMEM((STEP_TILES, PTS), jnp.int32)] * 2,
             pltpu.SemaphoreType.DMA((2,)),
             pltpu.SemaphoreType.DMA((PACK_PARTS,)),
+            pltpu.SemaphoreType.DMA,
         ],
         compiler_params=pltpu.CompilerParams(vmem_limit_bytes=32 << 20),
         cost_estimate=pl.CostEstimate(flops=4_000_000_000, bytes_accessed=8_000_000, transcendentals=0),
         name="sample",
     )(
-        slot, table_rows, center, side_first, side_second, columns,
+        tile_dest.reshape(1, TILES), tile_points, volume, first, second, side_first, side_second,
     )
 
     arrived = lax.all_to_all(

time: 79.9 us -> 81.9 us (1.025)
  local copies, waits for them, and re-layouts: 6.94 us -> 10.2 us
  other arithmetic: 3.96 us -> 1.27 us
  waiting for transfers between devices: 13.7 us -> 14.7 us
    unnamed x4 -> x8, local copies, waits for them, and re-layouts: 0.93 us -> 3.41 us
    ppermute x4, waiting for transfers between devices: 1.58 us -> 2.58 us  [swap(): return lax.ppermute(value, axis, pairs)]
    concatenate x1 -> x0, other arithmetic: 0.94 us -> none  [per_device(): center = jnp.concatenate([low, volume, high], axis=0)]
    and x1 -> x0, other arithmetic: 0.94 us -> none  [per_device(): columns = tile_points & 15]
    reduce_sum x1 -> x0, other arithmetic: 0.87 us -> none  [per_device(): slot = dest * CAP + jnp.sum(same_owner.astype(jnp.int32), axis=0)]
  transfers between devices with their start and end apart: 5 -> 5, of which waited for: 3 -> 3; matrix products, arithmetic and copies ran while one was open for 11% -> 10% of each run, Pallas kernels for 7% -> 7%
where the time goes in v6:
time: 81.9 us; the launch traced here: 81.5 us
  Pallas kernels  34.6 us (42%)
  starting transfers between devices  19.8 us (24%)
  waiting for transfers between devices  14.7 us (18%)
  local copies, waits for them, and re-layouts  10.2 us (12%)
  other arithmetic  1.27 us (2%)
  between operations  0.96 us (1%)
    pallas_call x1, Pallas kernels, per_device(): pl.pallas_call(sample_kernel, out_shape=(jax.ShapeDtypeStruct((OWNERS * S...  27.1 us
    all_to_all x1, waiting for transfers between devices, per_device(): lax.all_to_all(send.reshape(OWNERS, SEND_ROWS, PTS), ('wide', 'narrow'),...  12.1 us
    all_to_all x1, starting transfers between devices, per_device(): lax.all_to_all(send.reshape(OWNERS, SEND_ROWS, PTS), ('wide', 'narrow'),...  9.98 us
    ppermute x4, starting transfers between devices, swap(): return lax.ppermute(value, axis, pairs)  9.86 us
    pallas_call x1, Pallas kernels, per_device(): pl.pallas_call(response_kernel, grid=(SZ,), out_shape=jax.ShapeDtypeStruc...  5.38 us
    another operation x3, local copies, waits for them, and re-layouts, mix_matrix(): full = jnp.where(rows == columns, jnp.tile(scales, (16, 16)), 0.0)  4.99 us
    unnamed x8, local copies, waits for them, and re-layouts  3.41 us
    ppermute x4, waiting for transfers between devices, swap(): return lax.ppermute(value, axis, pairs)  2.58 us
  transfers between devices with their start and end apart: 5, of which 3 were waited for; matrix products, arithmetic and copies ran while one was open for 10% of the time, Pallas kernels for 7%

profile of v6, /device:TPU:1, one launch (start us, length us, event | category | flops | bytes accessed | tf_op | source)
XLA Modules:
  0.0 81.5 jit_solution(1375516330047136182)
XLA Ops:
  0.6 4.5 %collective-permute-start.1 = (bf16[8,64,128]{2,1,0:T(8,128)(2,1)}, bf16[8,64,128]{2,1,0:T(8,128)(2,1)S(1)}, u32[]{:S(2)}, u32[]{:S(2)}) collective-permute-start(bf16[8,64,128]{2,1,0:T(8,128)(2,1)} %block_ref.1), channel_id=1, source_target_pairs={{4,8},{8,4},{12,16},{16,12},{20,24},{24,20},{28,32},{32,28},{36,40... | collective-permute-start | bytes 393224 | tf_op jit(solution)/shard_map/ppermute | solution.py:321
  5.1 0.1 collective-permute-start
  5.3 0.7 fusion.2
  6.0 2.0 %collective-permute-done.1.second_ref = bf16[8,64,128]{2,1,0:T(8,128)(2,1)S(1)} collective-permute-done((bf16[8,64,128]{2,1,0:T(8,128)(2,1)}, bf16[8,64,128]{2,1,0:T(8,128)(2,1)S(1)}, u32[]{:S(2)}, u32[]{:S(2)}) %collective-permute-start.1) | collective-permute-done | bytes 131104 | tf_op jit(solution)/shard_map/ppermute | solution.py:321
  8.0 0.0 collective-permute-done.first_ref
  8.1 0.7 collective-permute-start.3
  8.7 4.6 %collective-permute-start.2 = (bf16[20,8,128]{2,1,0:T(8,128)(2,1)S(1)}, bf16[20,8,128]{2,1,0:T(8,128)(2,1)S(1)}, u32[]{:S(2)}, u32[]{:S(2)}) collective-permute-start(bf16[20,8,128]{2,1,0:T(8,128)(2,1)S(1)} %get-tuple-element.39), channel_id=1, source_target_pairs={{0,1},{1,0},{2,3},{3,2},{4,5},{5,4},{6,7},{7,6},{8,9},{9,8},{10,11... | collective-permute-start | bytes 122888 | tf_op jit(solution)/shard_map/ppermute | solution.py:321
  13.3 0.8 cosine_bitcast_fusion
  14.1 0.0 collective-permute-done.3.side_second_ref
  14.2 0.6 collective-permute-done.2.side_first_ref
  14.7 0.0 copy-start.1
  14.7 0.9 %copy-done.1 = bf16[8,64,128]{2,1,0:T(8,128)(2,1)S(1)} copy-done((bf16[8,64,128]{2,1,0:T(8,128)(2,1)S(1)}, bf16[8,64,128]{2,1,0:T(8,128)(2,1)}, u32[]{:S(2)}) %copy-start.1) | copy-done | bytes 131096
  15.6 0.0 copy-start.2
  15.6 0.9 %copy-done.2 = s32[256,128]{1,0:T(8,128)S(1)} copy-done((s32[256,128]{1,0:T(8,128)S(1)}, s32[256,128]{1,0:T(8,128)}, u32[]{:S(2)}) %copy-start.2) | copy-done | bytes 131096
  16.5 0.0 copy-start.3
  16.5 0.7 copy-done.3
  17.2 27.1 %sample.1 = (bf16[6144,128]{1,0:T(8,128)(2,1)}, bf16[2,512,768]{2,1,0:T(8,128)(2,1)S(1)}) custom-call(s32[1,256]{1,0:T(1,128)S(1)} %bitcast.17, s32[256,128]{1,0:T(8,128)S(1)} %copy-done.2, bf16[8,64,128]{2,1,0:T(8,128)(2,1)S(1)} %copy-done.1, bf16[8,64,128]{2,1,0:T(8,128)(2,1)S(1)} %collective-permute-done.first_ref, ...), custom_call_target="tpu_custom_call" | custom-call | flops 4000000000 | bytes 8000000 | tf_op jit(solution)/shard_map/sample/pallas_call | solution.py:353
  44.4 10.0 %all-to-all-start = ((bf16[128,48,128]{2,1,0:T(8,128)(2,1)}), bf16[128,48,128]{2,1,0:T(8,128)(2,1)S(1)}, u32[]{:S(2)}, u32[]{:S(2)}) async-start(bf16[128,48,128]{2,1,0:T(8,128)(2,1)} %bitcast.5), calls=%async_computation | async-start | bytes 3145728 | tf_op jit(solution)/shard_map/all_to_all | solution.py:385
  54.4 0.1 copy.28
  54.4 0.1 copy.20
  54.5 0.1 copy.18
  54.6 0.1 copy.22
  54.7 0.1 stack.4
  54.8 0.5 scatter.9
  55.3 0.1 copy.29
  55.4 1.3 %tile.4 = f32[16,16,16,12]{1,0,3,2:T(8,128)} broadcast(f32[16,12]{0,1:T(8,128)S(1)} %copy.29), dimensions={1,3} | broadcast | bytes 197376 | tf_op jit(solution)/shard_map/tile | solution.py:329
  56.7 2.6 %tile.10 = f32[1,256,192]{1,2,0:T(8,128)} reshape(f32[16,16,16,12]{1,0,3,2:T(8,128)} %tile.4) | data formatting | bytes 393216 | tf_op jit(solution)/shard_map/tile | solution.py:329
  59.3 1.1 %copy.30 = f32[1,256,192]{2,1,0:T(8,128)S(1)} copy(f32[1,256,192]{1,2,0:T(8,128)} %tile.10) | data formatting | bytes 393216 | tf_op jit(solution)/shard_map/tile | solution.py:329
  60.4 0.2 subtract_convert_fusion
  60.6 0.2 fusion.1
  60.9 0.0 copy-start
  60.9 0.9 %copy-done = bf16[2,3,128,128]{3,2,1,0:T(8,128)(2,1)S(1)} copy-done((bf16[2,3,128,128]{3,2,1,0:T(8,128)(2,1)S(1)}, bf16[2,3,128,128]{3,2,1,0:T(8,128)(2,1)}, u32[]{:S(2)}) %copy-start) | copy-done | bytes 196632
  61.8 5.4 %respond.1 = bf16[16,8,64,128]{3,2,1,0:T(8,128)(2,1)} custom-call(f32[8,6]{1,0:T(8,128)S(1)} %broadcast_multiply_fusion.weight_ref, bf16[2,512,768]{2,1,0:T(8,128)(2,1)S(1)} %get-tuple-element.28.fields_ref, bf16[2,3,128,128]{3,2,1,0:T(8,128)(2,1)S(1)} %copy-done), custom_call_target="tpu_custom_call" | custom-call | flops 200000000 | bytes 4000000 | tf_op jit(solution)/shard_map/respond/pallas_call | solution.py:389
  67.2 12.1 %all-to-all-done = bf16[128,48,128]{2,1,0:T(8,128)(2,1)S(1)} async-done(((bf16[128,48,128]{2,1,0:T(8,128)(2,1)}), bf16[128,48,128]{2,1,0:T(8,128)(2,1)S(1)}, u32[]{:S(2)}, u32[]{:S(2)}) %all-to-all-start) | async-done | bytes 1572896 | tf_op jit(solution)/shard_map/all_to_all | solution.py:385
  79.3 2.1 %mix.1 = bf16[8192,128]{1,0:T(8,128)(2,1)} custom-call(bf16[2,256,192]{2,1,0:T(8,128)(2,1)S(1)} %pad_maximum_fusion.mix_ref, bf16[6144,128]{1,0:T(8,128)(2,1)S(1)} %bitcast.16), custom_call_target="tpu_custom_call" | custom-call | flops 1600000000 | bytes 4000000 | tf_op jit(solution)/shard_map/mix/pallas_call | solution.py:404
  (13 shorter events, 0.1 us)
Async XLA Ops:
  0.6 7.4 %collective-permute-start.1 = (bf16[8,64,128]{2,1,0:T(8,128)(2,1)}, bf16[8,64,128]{2,1,0:T(8,128)(2,1)S(1)}, u32[]{:S(2)}, u32[]{:S(2)}) collective-permute-start(bf16[8,64,128]{2,1,0:T(8,128)(2,1)} %block_ref.1), channel_id=1, source_target_pairs={{4,8},{8,4},{12,16},{16,12},{20,24},{24,20},{28,32},{32,28},{36,40... | collective-permute-start | bytes 393224 | tf_op jit(solution)/shard_map/ppermute | solution.py:321
  5.1 2.9 %collective-permute-start = (bf16[8,64,128]{2,1,0:T(8,128)(2,1)}, bf16[8,64,128]{2,1,0:T(8,128)(2,1)S(1)}, u32[]{:S(2)}, u32[]{:S(2)}) collective-permute-start(bf16[8,64,128]{2,1,0:T(8,128)(2,1)} %block_ref.1), channel_id=1, source_target_pairs={{0,4},{4,0},{8,12},{12,8},{16,20},{20,16},{24,28},{28,24},{32,36},... | collective-permute-start | bytes 393224 | tf_op jit(solution)/shard_map/ppermute | solution.py:321
  8.1 6.1 %collective-permute-start.3 = (bf16[20,8,128]{2,1,0:T(8,128)(2,1)S(1)}, bf16[20,8,128]{2,1,0:T(8,128)(2,1)S(1)}, u32[]{:S(2)}, u32[]{:S(2)}) collective-permute-start(bf16[20,8,128]{2,1,0:T(8,128)(2,1)S(1)} %get-tuple-element.38), channel_id=1, source_target_pairs={{1,2},{2,1},{5,6},{6,5},{9,10},{10,9},{13,14},{14,13},{17,18},{18,... | collective-permute-start | bytes 122888 | tf_op jit(solution)/shard_map/ppermute | solution.py:321
  8.7 6.0 %collective-permute-start.2 = (bf16[20,8,128]{2,1,0:T(8,128)(2,1)S(1)}, bf16[20,8,128]{2,1,0:T(8,128)(2,1)S(1)}, u32[]{:S(2)}, u32[]{:S(2)}) collective-permute-start(bf16[20,8,128]{2,1,0:T(8,128)(2,1)S(1)} %get-tuple-element.39), channel_id=1, source_target_pairs={{0,1},{1,0},{2,3},{3,2},{4,5},{5,4},{6,7},{7,6},{8,9},{9,8},{10,11... | collective-permute-start | bytes 122888 | tf_op jit(solution)/shard_map/ppermute | solution.py:321
  14.7 0.9 %copy-start.1 = (bf16[8,64,128]{2,1,0:T(8,128)(2,1)S(1)}, bf16[8,64,128]{2,1,0:T(8,128)(2,1)}, u32[]{:S(2)}) copy-start(bf16[8,64,128]{2,1,0:T(8,128)(2,1)} %block_ref.1) | copy-start | bytes 393220
  15.6 0.9 %copy-start.2 = (s32[256,128]{1,0:T(8,128)S(1)}, s32[256,128]{1,0:T(8,128)}, u32[]{:S(2)}) copy-start(s32[256,128]{1,0:T(8,128)} %points_ref.1) | copy-start | bytes 393220
  16.5 0.7 copy-start.3
  44.4 34.9 %all-to-all-start = ((bf16[128,48,128]{2,1,0:T(8,128)(2,1)}), bf16[128,48,128]{2,1,0:T(8,128)(2,1)S(1)}, u32[]{:S(2)}, u32[]{:S(2)}) async-start(bf16[128,48,128]{2,1,0:T(8,128)(2,1)} %bitcast.5), calls=%async_computation | async-start | bytes 3145728 | tf_op jit(solution)/shard_map/all_to_all | solution.py:385
  60.9 0.9 %copy-start = (bf16[2,3,128,128]{3,2,1,0:T(8,128)(2,1)S(1)}, bf16[2,3,128,128]{3,2,1,0:T(8,128)(2,1)}, u32[]{:S(2)}) copy-start(bf16[2,3,128,128]{3,2,1,0:T(8,128)(2,1)} %constant.101.clone.x_band_ref) | copy-start | bytes 589828

commit v7 on v6

--- a/solution.py
+++ b/solution.py
@@ -134,7 +134,7 @@
 
 
 def sample_kernel(
-    dest_ref, points_ref, block_ref, first_ref, second_ref, side_first_ref, side_second_ref, send_hbm, fields_ref, ext, y_fields, bands, table, tiles,
+    dest_ref, points_ref, center_ref, first_ref, second_ref, send_hbm, fields_ref, ext, y_fields, bands, table, tiles,
     y_band, smoother, send, rows_ref, slots, slot_ref, index_rows, sem, send_sem, slot_sem
 ):
     def copy_rows(step, side):
@@ -150,14 +150,10 @@
     slot_copy = pltpu.make_async_copy(slots, slot_ref, slot_sem)
     slot_copy.start()
 
-    inner = slice(Y_PAD, Y_PAD + CY)
-    even = (lax.axis_index("wide") & 1) == 0
-    ext[BORDER:BORDER + SZ, inner, :] = block_ref[...]
-    ext[0:BORDER, inner, :] = jnp.where(even, second_ref[SZ - BORDER:], first_ref[SZ - BORDER:])
-    ext[BORDER + SZ:DEEP, inner, :] = jnp.where(even, first_ref[:BORDER], second_ref[:BORDER])
+    ext[:, Y_PAD:Y_PAD + CY, :] = center_ref[...]
     even = (lax.axis_index("narrow") & 1) == 0
-    ext[:, 0:Y_PAD, :] = jnp.where(even, side_second_ref[...], side_first_ref[...])
-    ext[:, Y_PAD + CY:TALL, :] = jnp.where(even, side_first_ref[...], side_second_ref[...])
+    ext[:, 0:Y_PAD, :] = jnp.where(even, second_ref[...], first_ref[...])
+    ext[:, Y_PAD + CY:TALL, :] = jnp.where(even, first_ref[...], second_ref[...])
     tiles[...] = jnp.zeros_like(tiles)
     fill_y_band(y_band)
     fill_x_bands(bands)
@@ -345,6 +341,9 @@
     edge_low, edge_high = extended(slice(0, Y_PAD)), extended(slice(CY - Y_PAD, CY))
     side_first = swap(jnp.where(even_narrow, edge_high, edge_low), "narrow", 0)
     side_second = swap(jnp.where(even_narrow, edge_low, edge_high), "narrow", 1)
+    first, second, side_first = lax.optimization_barrier((first, second, side_first))
+    center = extended(slice(0, CY))
+
     weights = orientation_weights(angles)
     mix = mix_matrix(weights)
 
@@ -356,7 +355,7 @@
             jax.ShapeDtypeStruct((OWNERS * SEND_ROWS, PTS), jnp.bfloat16),
             jax.ShapeDtypeStruct((2, ROWS, COMPS * NX), jnp.bfloat16),
         ),
-        in_specs=[vmem] * 7,
+        in_specs=[vmem] * 5,
         out_specs=(hbm, vmem),
         scratch_shapes=[
             pltpu.VMEM((DEEP, TALL, NX), jnp.bfloat16),
@@ -379,7 +378,7 @@
         cost_estimate=pl.CostEstimate(flops=4_000_000_000, bytes_accessed=8_000_000, transcendentals=0),
         name="sample",
     )(
-        tile_dest.reshape(1, TILES), tile_points, volume, first, second, side_first, side_second,
+        tile_dest.reshape(1, TILES), tile_points, center, side_first, side_second,
     )
 
     arrived = lax.all_to_all(

time: 81.9 us -> 81.9 us (level)
  local copies, waits for them, and re-layouts: 10.2 us -> 7.7 us
  starting transfers between devices: 19.8 us -> 21.8 us
  other arithmetic: 1.27 us -> 2.24 us
    all_to_all x1, starting transfers between devices: 9.98 us -> 14.7 us  [per_device(): lax.all_to_all(send.reshape(OWNERS, SEND_ROWS, PTS), ('wide', 'narrow'),...]
    ppermute x4, starting transfers between devices: 9.86 us -> 7.11 us  [swap(): return lax.ppermute(value, axis, pairs)]
    unnamed x8 -> x6, local copies, waits for them, and re-layouts: 3.41 us -> 0.93 us
    concatenate x0 -> x1, other arithmetic: none -> 0.94 us  [extended(): return jnp.concatenate([low, volume[:, rows], high], axis=0)]
  transfers between devices with their start and end apart: 5 -> 5, of which waited for: 3 -> 2; matrix products, arithmetic and copies ran while one was open for 10% -> 11% of each run, Pallas kernels for 7% -> 7%
where the time goes in v7:
time: 81.9 us; the launch traced here: 81.5 us
  Pallas kernels  34.6 us (42%)
  starting transfers between devices  21.8 us (27%)
  waiting for transfers between devices  14.1 us (17%)
  local copies, waits for them, and re-layouts  7.7 us (9%)
  other arithmetic  2.24 us (3%)
  between operations  1 us (1%)
    pallas_call x1, Pallas kernels, per_device(): pl.pallas_call(sample_kernel, out_shape=(jax.ShapeDtypeStruct((OWNERS * S...  27.2 us
    all_to_all x1, starting transfers between devices, per_device(): lax.all_to_all(send.reshape(OWNERS, SEND_ROWS, PTS), ('wide', 'narrow'),...  14.7 us
    all_to_all x1, waiting for transfers between devices, per_device(): lax.all_to_all(send.reshape(OWNERS, SEND_ROWS, PTS), ('wide', 'narrow'),...  12.1 us
    ppermute x4, starting transfers between devices, swap(): return lax.ppermute(value, axis, pairs)  7.11 us
    pallas_call x1, Pallas kernels, per_device(): pl.pallas_call(response_kernel, grid=(SZ,), out_shape=jax.ShapeDtypeStruc...  5.38 us
    another operation x3, local copies, waits for them, and re-layouts, mix_matrix(): full = jnp.where(rows == columns, jnp.tile(scales, (16, 16)), 0.0)  4.99 us
    pallas_call x1, Pallas kernels, per_device(): pl.pallas_call(mix_kernel, out_shape=jax.ShapeDtypeStruct((SLOTS * 16, PT...  2.08 us
    ppermute x4, waiting for transfers between devices, swap(): return lax.ppermute(value, axis, pairs)  2.01 us
  transfers between devices with their start and end apart: 5, of which 2 were waited for; matrix products, arithmetic and copies ran while one was open for 11% of the time, Pallas kernels for 7%

profile of v7, /device:TPU:1, one launch (start us, length us, event | category | flops | bytes accessed | tf_op | source)
XLA Modules:
  0.0 81.5 jit_solution(6732552106991031396)
XLA Ops:
  0.6 0.0 copy-start.2
  0.6 0.0 copy-start.1
  0.6 4.6 %collective-permute-start.1 = (bf16[8,64,128]{2,1,0:T(8,128)(2,1)}, bf16[8,64,128]{2,1,0:T(8,128)(2,1)S(1)}, u32[]{:S(2)}, u32[]{:S(2)}) collective-permute-start(bf16[8,64,128]{2,1,0:T(8,128)(2,1)} %param.9), channel_id=1, source_target_pairs={{4,8},{8,4},{12,16},{16,12},{20,24},{24,20},{28,32},{32,28},{36,40... | collective-permute-start | bytes 393224 | tf_op jit(solution)/shard_map/ppermute | solution.py:317
  5.3 0.1 collective-permute-start
  5.4 0.7 fusion.2
  6.1 2.0 %collective-permute-done.1 = bf16[8,64,128]{2,1,0:T(8,128)(2,1)S(1)} collective-permute-done((bf16[8,64,128]{2,1,0:T(8,128)(2,1)}, bf16[8,64,128]{2,1,0:T(8,128)(2,1)S(1)}, u32[]{:S(2)}, u32[]{:S(2)}) %collective-permute-start.1) | collective-permute-done | bytes 131104 | tf_op jit(solution)/shard_map/ppermute | solution.py:317
  8.2 0.0 collective-permute-done
  8.2 1.7 %collective-permute-start.2 = (bf16[20,8,128]{2,1,0:T(8,128)(2,1)S(1)}, bf16[20,8,128]{2,1,0:T(8,128)(2,1)S(1)}, u32[]{:S(2)}, u32[]{:S(2)}) collective-permute-start(bf16[20,8,128]{2,1,0:T(8,128)(2,1)S(1)} %get-tuple-element.47), channel_id=1, source_target_pairs={{0,1},{1,0},{2,3},{3,2},{4,5},{5,4},{6,7},{7,6},{8,9},{9,8},{10,11... | collective-permute-start | bytes 122888 | tf_op jit(solution)/shard_map/ppermute | solution.py:317
  9.9 0.8 cosine_bitcast_fusion
  10.7 0.7 collective-permute-start.3
  11.4 0.0 collective-permute-done.2.first_ref
  11.5 0.9 %pad_maximum_fusion.center_ref = bf16[20,64,128]{2,1,0:T(8,128)(2,1)S(1)} fusion(bf16[6,64,128]{2,1,0:T(8,128)(2,1)S(1)} %get-tuple-element.39, bf16[8,64,128]{2,1,0:T(8,128)(2,1)} %param.9, bf16[6,64,128]{2,1,0:T(8,128)(2,1)S(1)} %get-tuple-element.38), kind=kLoop, calls=%fused_computation | loop fusion | flops 327680 | bytes 655360 | tf_op jit(solution)/shard_map/concatenate | solution.py:339
  12.4 0.0 collective-permute-done.3.second_ref
  12.4 0.0 copy-done.2
  12.4 0.0 copy-done.1
  12.4 27.2 %sample.1 = (bf16[6144,128]{1,0:T(8,128)(2,1)}, bf16[2,512,768]{2,1,0:T(8,128)(2,1)S(1)}) custom-call(s32[1,256]{1,0:T(1,128)S(1)} %bitcast.17, s32[256,128]{1,0:T(8,128)S(1)} %copy-done.1, bf16[20,64,128]{2,1,0:T(8,128)(2,1)S(1)} %pad_maximum_fusion.center_ref, bf16[20,8,128]{2,1,0:T(8,128)(2,1)S(1)} %collective-permute-done.2.first_ref, ...), custom_call_target="tpu_custom_call" | custom-call | flops 4000000000 | bytes 8000000 | tf_op jit(solution)/shard_map/sample/pallas_call | solution.py:352
  39.6 14.7 %all-to-all-start = ((bf16[128,48,128]{2,1,0:T(8,128)(2,1)}), bf16[128,48,128]{2,1,0:T(8,128)(2,1)S(1)}, u32[]{:S(2)}, u32[]{:S(2)}) async-start(bf16[128,48,128]{2,1,0:T(8,128)(2,1)} %bitcast.5), calls=%async_computation | async-start | bytes 3145728 | tf_op jit(solution)/shard_map/all_to_all | solution.py:384
  54.3 0.1 copy.28
  54.4 0.1 copy.20
  54.5 0.1 copy.18
  54.6 0.1 copy.22
  54.7 0.1 stack.4
  54.8 0.5 scatter.9
  55.3 0.1 copy.29
  55.4 1.3 %tile.4 = f32[16,16,16,12]{1,0,3,2:T(8,128)} broadcast(f32[16,12]{0,1:T(8,128)S(1)} %copy.29), dimensions={1,3} | broadcast | bytes 197376 | tf_op jit(solution)/shard_map/tile | solution.py:325
  56.7 2.6 %tile.10 = f32[1,256,192]{1,2,0:T(8,128)} reshape(f32[16,16,16,12]{1,0,3,2:T(8,128)} %tile.4) | data formatting | bytes 393216 | tf_op jit(solution)/shard_map/tile | solution.py:325
  59.3 1.1 %copy.30 = f32[1,256,192]{2,1,0:T(8,128)S(1)} copy(f32[1,256,192]{1,2,0:T(8,128)} %tile.10) | data formatting | bytes 393216 | tf_op jit(solution)/shard_map/tile | solution.py:325
  60.4 0.2 subtract_convert_fusion
  60.6 0.2 fusion.1
  60.8 0.0 copy-start
  60.8 0.9 %copy-done = bf16[2,3,128,128]{3,2,1,0:T(8,128)(2,1)S(1)} copy-done((bf16[2,3,128,128]{3,2,1,0:T(8,128)(2,1)S(1)}, bf16[2,3,128,128]{3,2,1,0:T(8,128)(2,1)}, u32[]{:S(2)}) %copy-start) | copy-done | bytes 196632
  61.8 5.4 %respond.1 = bf16[16,8,64,128]{3,2,1,0:T(8,128)(2,1)} custom-call(f32[8,6]{1,0:T(8,128)S(1)} %broadcast_multiply_fusion.weight_ref, bf16[2,512,768]{2,1,0:T(8,128)(2,1)S(1)} %get-tuple-element.34.fields_ref, bf16[2,3,128,128]{3,2,1,0:T(8,128)(2,1)S(1)} %copy-done), custom_call_target="tpu_custom_call" | custom-call | flops 200000000 | bytes 4000000 | tf_op jit(solution)/shard_map/respond/pallas_call | solution.py:388
  67.1 12.1 %all-to-all-done = bf16[128,48,128]{2,1,0:T(8,128)(2,1)S(1)} async-done(((bf16[128,48,128]{2,1,0:T(8,128)(2,1)}), bf16[128,48,128]{2,1,0:T(8,128)(2,1)S(1)}, u32[]{:S(2)}, u32[]{:S(2)}) %all-to-all-start) | async-done | bytes 1572896 | tf_op jit(solution)/shard_map/all_to_all | solution.py:384
  79.3 2.1 %mix.1 = bf16[8192,128]{1,0:T(8,128)(2,1)} custom-call(bf16[2,256,192]{2,1,0:T(8,128)(2,1)S(1)} %pad_maximum_fusion.1.mix_ref, bf16[6144,128]{1,0:T(8,128)(2,1)S(1)} %bitcast.16), custom_call_target="tpu_custom_call" | custom-call | flops 1600000000 | bytes 4000000 | tf_op jit(solution)/shard_map/mix/pallas_call | solution.py:403
  (14 shorter events, 0.2 us)
Async XLA Ops:
  0.6 11.8 %copy-start.2 = (s32[256,1]{0,1:T(1,128)S(1)}, s32[256,1]{0,1:T(1,128)}, u32[]{:S(2)}) copy-start(s32[256,1]{0,1:T(1,128)} %param.12) | copy-start | bytes 3076
  0.6 11.8 %copy-start.1 = (s32[256,128]{1,0:T(8,128)S(1)}, s32[256,128]{1,0:T(8,128)}, u32[]{:S(2)}) copy-start(s32[256,128]{1,0:T(8,128)} %points_ref.1) | copy-start | bytes 393220
  0.6 7.5 %collective-permute-start.1 = (bf16[8,64,128]{2,1,0:T(8,128)(2,1)}, bf16[8,64,128]{2,1,0:T(8,128)(2,1)S(1)}, u32[]{:S(2)}, u32[]{:S(2)}) collective-permute-start(bf16[8,64,128]{2,1,0:T(8,128)(2,1)} %param.9), channel_id=1, source_target_pairs={{4,8},{8,4},{12,16},{16,12},{20,24},{24,20},{28,32},{32,28},{36,40... | collective-permute-start | bytes 393224 | tf_op jit(solution)/shard_map/ppermute | solution.py:317
  5.3 2.9 %collective-permute-start = (bf16[8,64,128]{2,1,0:T(8,128)(2,1)}, bf16[8,64,128]{2,1,0:T(8,128)(2,1)S(1)}, u32[]{:S(2)}, u32[]{:S(2)}) collective-permute-start(bf16[8,64,128]{2,1,0:T(8,128)(2,1)} %param.9), channel_id=1, source_target_pairs={{0,4},{4,0},{8,12},{12,8},{16,20},{20,16},{24,28},{28,24},{32,36},... | collective-permute-start | bytes 393224 | tf_op jit(solution)/shard_map/ppermute | solution.py:317
  8.2 3.2 %collective-permute-start.2 = (bf16[20,8,128]{2,1,0:T(8,128)(2,1)S(1)}, bf16[20,8,128]{2,1,0:T(8,128)(2,1)S(1)}, u32[]{:S(2)}, u32[]{:S(2)}) collective-permute-start(bf16[20,8,128]{2,1,0:T(8,128)(2,1)S(1)} %get-tuple-element.47), channel_id=1, source_target_pairs={{0,1},{1,0},{2,3},{3,2},{4,5},{5,4},{6,7},{7,6},{8,9},{9,8},{10,11... | collective-permute-start | bytes 122888 | tf_op jit(solution)/shard_map/ppermute | solution.py:317
  10.7 1.7 %collective-permute-start.3 = (bf16[20,8,128]{2,1,0:T(8,128)(2,1)S(1)}, bf16[20,8,128]{2,1,0:T(8,128)(2,1)S(1)}, u32[]{:S(2)}, u32[]{:S(2)}) collective-permute-start(bf16[20,8,128]{2,1,0:T(8,128)(2,1)S(1)} %get-tuple-element.46), channel_id=1, source_target_pairs={{1,2},{2,1},{5,6},{6,5},{9,10},{10,9},{13,14},{14,13},{17,18},{18,... | collective-permute-start | bytes 122888 | tf_op jit(solution)/shard_map/ppermute | solution.py:317
  39.6 39.6 %all-to-all-start = ((bf16[128,48,128]{2,1,0:T(8,128)(2,1)}), bf16[128,48,128]{2,1,0:T(8,128)(2,1)S(1)}, u32[]{:S(2)}, u32[]{:S(2)}) async-start(bf16[128,48,128]{2,1,0:T(8,128)(2,1)} %bitcast.5), calls=%async_computation | async-start | bytes 3145728 | tf_op jit(solution)/shard_map/all_to_all | solution.py:384
  60.8 0.9 %copy-start = (bf16[2,3,128,128]{3,2,1,0:T(8,128)(2,1)S(1)}, bf16[2,3,128,128]{3,2,1,0:T(8,128)(2,1)}, u32[]{:S(2)}) copy-start(bf16[2,3,128,128]{3,2,1,0:T(8,128)(2,1)} %constant.101.clone.x_band_ref) | copy-start | bytes 589828

commit v8 on v4

--- a/solution.py
+++ b/solution.py
@@ -141,10 +141,7 @@
     even = (lax.axis_index("narrow") & 1) == 0
     ext[:, 0:Y_PAD, :] = jnp.where(even, second_ref[...], first_ref[...])
     ext[:, Y_PAD + CY:TALL, :] = jnp.where(even, first_ref[...], second_ref[...])
-    tiles[...] = jnp.zeros_like(tiles)
     fill_y_band(y_band)
-    fill_x_bands(bands)
-    smoother[...] = smooth_matrix()
 
     for z in range(0, DEEP, 2):
         pair = jnp.concatenate([ext[z], ext[z + 1]], axis=1)
@@ -154,6 +151,8 @@
                 y_fields[z, s, kind] = out[kind * CY:(kind + 1) * CY, 0:NX]
                 y_fields[z + 1, s, kind] = out[kind * CY:(kind + 1) * CY, NX:2 * NX]
 
+    fill_x_bands(bands)
+    lower = index((ROWS, LANES), 1) < 64
     for s in range(2):
         for y in range(0, CY, 8):
             for kind_y, kinds_z in ((0, (0, 1, 2)), (1, (0, 1)), (2, (0,))):
@@ -165,23 +164,17 @@
                             fields_ref[s, z * CY + y:z * CY + y + 8, comp * NX:(comp + 1) * NX] = (
                                 passed[comp_z].astype(jnp.bfloat16)
                             )
-
-    lower = index((PART, LANES), 1) < 64
-    for m in range(0, NX // 16, 2):
-        for part in range(0, ROWS, PART):
-            outs = [
-                jnp.dot(
-                    fields_ref[s, part:part + PART, :], bands[s, :, m * LANES:(m + 2) * LANES],
-                    preferred_element_type=jnp.float32,
-                )
-                for s in range(2)
-            ]
+        own = lower if s == 0 else jnp.logical_not(lower)
+        for m in range(0, NX // 16, 2):
+            out = jnp.dot(fields_ref[s], bands[s, :, m * LANES:(m + 2) * LANES], preferred_element_type=jnp.float32)
             for half in range(2):
-                first, second = (out[:, half * LANES:(half + 1) * LANES] for out in outs)
-                start = 8 + (m + half) * 2 * ROWS + part
-                table[start:start + PART, :] = jnp.where(lower, first, second)
-                table[start + ROWS:start + ROWS + PART, :] = jnp.where(lower, second, first)
-
+                here = out[:, half * LANES:(half + 1) * LANES]
+                start = 8 + (m + half) * 2 * ROWS
+                pltpu.store(table.at[start:start + ROWS, :], here, mask=own)
+                pltpu.store(table.at[start + ROWS:start + 2 * ROWS, :], here, mask=jnp.logical_not(own))
+
+    tiles[...] = jnp.zeros_like(tiles)
+    smoother[...] = smooth_matrix()
     eye = (index((LANES, LANES), 0) == index((LANES, LANES), 1)).astype(jnp.bfloat16)
     sublane = index((8, LANES), 0)
 
@@ -318,12 +311,17 @@
     even_wide = (lax.axis_index("wide") & 1) == 0
     even_narrow = (lax.axis_index("narrow") & 1) == 0
     first, second = swap(volume, "wide", 0), swap(volume, "wide", 1)
-    low = jnp.where(even_wide, second, first)[SZ - BORDER:]
-    high = jnp.where(even_wide, first, second)[:BORDER]
-    center = jnp.concatenate([low, volume, high], axis=0)
-    edge_low, edge_high = center[:, :Y_PAD], center[:, CY - Y_PAD:]
+    def extended(rows):
+        below, above = first[:, rows], second[:, rows]
+        low = jnp.where(even_wide, above, below)[SZ - BORDER:]
+        high = jnp.where(even_wide, below, above)[:BORDER]
+        return jnp.concatenate([low, volume[:, rows], high], axis=0)
+
+    edge_low, edge_high = extended(slice(0, Y_PAD)), extended(slice(CY - Y_PAD, CY))
     side_first = swap(jnp.where(even_narrow, edge_high, edge_low), "narrow", 0)
     side_second = swap(jnp.where(even_narrow, edge_low, edge_high), "narrow", 1)
+    first, second, side_first = lax.optimization_barrier((first, second, side_first))
+    center = extended(slice(0, CY))
 
     table_rows = ((tile_points >> 3) & 15) * ROWS + (tile_points >> 7)
     columns = tile_points & 15

time: 79.9 us -> 81.4 us (1.019)
  starting transfers between devices: 19.8 us -> 22.2 us
  waiting for transfers between devices: 13.7 us -> 12.1 us
    all_to_all x1, starting transfers between devices: 9.97 us -> 15.1 us  [per_device(): lax.all_to_all(send.reshape(OWNERS, SEND_ROWS, PTS), ('wide', 'narrow'),...]
    ppermute x4, starting transfers between devices: 9.86 us -> 7.11 us  [swap(): return lax.ppermute(value, axis, pairs)]
    ppermute x4, waiting for transfers between devices: 1.58 us -> 0.01 us  [swap(): return lax.ppermute(value, axis, pairs)]
    concatenate x1, other arithmetic: 0.94 us -> 0.04 us  [extended(): return jnp.concatenate([low, volume[:, rows], high], axis=0)]
  transfers between devices with their start and end apart: 5 -> 5, of which waited for: 3 -> 1; matrix products, arithmetic and copies ran while one was open for 11% -> 13% of each run, Pallas kernels for 7% -> 7%
where the time goes in v8:
time: 81.4 us; the launch traced here: 81 us
  Pallas kernels  34.2 us (42%)
  starting transfers between devices  22.2 us (27%)
  waiting for transfers between devices  12.1 us (15%)
  local copies, waits for them, and re-layouts  7.69 us (9%)
  other arithmetic  3.82 us (5%)
  between operations  1 us (1%)
    pallas_call x1, Pallas kernels, per_device(): pl.pallas_call(sample_kernel, out_shape=(jax.ShapeDtypeStruct((OWNERS * S...  26.7 us
    all_to_all x1, starting transfers between devices, per_device(): lax.all_to_all(send.reshape(OWNERS, SEND_ROWS, PTS), ('wide', 'narrow'),...  15.1 us
    all_to_all x1, waiting for transfers between devices, per_device(): lax.all_to_all(send.reshape(OWNERS, SEND_ROWS, PTS), ('wide', 'narrow'),...  12.1 us
    ppermute x4, starting transfers between devices, swap(): return lax.ppermute(value, axis, pairs)  7.11 us
    pallas_call x1, Pallas kernels, per_device(): pl.pallas_call(response_kernel, grid=(SZ,), out_shape=jax.ShapeDtypeStruc...  5.38 us
    another operation x3, local copies, waits for them, and re-layouts, mix_matrix(): full = jnp.where(rows == columns, jnp.tile(scales, (16, 16)), 0.0)  4.99 us
    pallas_call x1, Pallas kernels, per_device(): pl.pallas_call(mix_kernel, out_shape=jax.ShapeDtypeStruct((SLOTS * 16, PT...  2.09 us
  transfers between devices with their start and end apart: 5, of which 1 were waited for; matrix products, arithmetic and copies ran while one was open for 13% of the time, Pallas kernels for 7%

profile of v8, /device:TPU:1, one launch (start us, length us, event | category | flops | bytes accessed | tf_op | source)
XLA Modules:
  0.0 81.0 jit_solution(9241860313375876530)
XLA Ops:
  0.6 0.0 copy-start.1
  0.6 4.6 %collective-permute-start.1 = (bf16[8,64,128]{2,1,0:T(8,128)(2,1)}, bf16[8,64,128]{2,1,0:T(8,128)(2,1)S(1)}, u32[]{:S(2)}, u32[]{:S(2)}) collective-permute-start(bf16[8,64,128]{2,1,0:T(8,128)(2,1)} %param.9), channel_id=1, source_target_pairs={{4,8},{8,4},{12,16},{16,12},{20,24},{24,20},{28,32},{32,28},{36,40... | collective-permute-start | bytes 393224 | tf_op jit(solution)/shard_map/ppermute | solution.py:296
  5.3 0.1 collective-permute-start
  5.4 0.7 fusion.3
  6.1 0.9 %convert_reduce_fusion = s32[256]{0:T(256)S(1)} fusion(s32[256]{0:T(256)} %bitcast.17), kind=kLoop, calls=%fused_computation.4 | loop fusion | flops 327424 | bytes 2048 | tf_op jit(solution)/shard_map/reduce_sum | solution.py:332
  7.0 0.9 %broadcast_and_fusion = (s32[256,128]{1,0:T(8,128)S(1)}, s32[256,128]{1,0:T(8,128)S(1)}) fusion(s32[256,128]{1,0:T(8,128)} %param.11), kind=kLoop, calls=%fused_computation.12 | loop fusion | flops 196608 | bytes 393216 | tf_op jit(solution)/shard_map/and | solution.py:327
  7.9 0.7 multiply_add_fusion.slot_ref
  8.6 0.0 collective-permute-done.1
  8.6 0.0 collective-permute-done
  8.7 1.7 %collective-permute-start.2 = (bf16[20,8,128]{2,1,0:T(8,128)(2,1)S(1)}, bf16[20,8,128]{2,1,0:T(8,128)(2,1)S(1)}, u32[]{:S(2)}, u32[]{:S(2)}) collective-permute-start(bf16[20,8,128]{2,1,0:T(8,128)(2,1)S(1)} %get-tuple-element.49), channel_id=1, source_target_pairs={{0,1},{1,0},{2,3},{3,2},{4,5},{5,4},{6,7},{7,6},{8,9},{9,8},{10,11... | collective-permute-start | bytes 122888 | tf_op jit(solution)/shard_map/ppermute | solution.py:296
  10.4 0.8 cosine_bitcast_fusion
  11.2 0.7 collective-permute-start.3
  11.9 0.0 collective-permute-done.2.first_ref
  11.9 0.0 copy-done.1
  12.0 0.0 collective-permute-done.3.second_ref
  12.0 26.7 %sample.1 = (bf16[6144,128]{1,0:T(8,128)(2,1)}, bf16[2,512,768]{2,1,0:T(8,128)(2,1)S(1)}) custom-call(s32[256]{0:T(256)S(1)} %multiply_add_fusion.slot_ref, s32[256,128]{1,0:T(8,128)S(1)} %get-tuple-element.41.rows_ref, bf16[20,64,128]{2,1,0:T(8,128)(2,1)S(1)} %pad_maximum_fusion.center_ref, bf16[20,8,128]{2,1,0:T(8,128)(2,1)S(1)} %collective-permute-done.2.first_ref, ...), custom_call_target="tpu_custom_call" | custom-call | flops 4000000000 | bytes 8000000 | tf_op jit(solution)/shard_map/sample/pallas_call | solution.py:339
  38.7 15.1 %all-to-all-start = ((bf16[128,48,128]{2,1,0:T(8,128)(2,1)}), bf16[128,48,128]{2,1,0:T(8,128)(2,1)S(1)}, u32[]{:S(2)}, u32[]{:S(2)}) async-start(bf16[128,48,128]{2,1,0:T(8,128)(2,1)} %bitcast.5), calls=%async_computation | async-start | bytes 3145728 | tf_op jit(solution)/shard_map/all_to_all | solution.py:367
  53.9 0.1 copy.41
  53.9 0.1 copy.33
  54.0 0.1 copy.31
  54.1 0.1 copy.35
  54.2 0.1 stack.4
  54.3 0.5 scatter.9
  54.8 0.1 copy.42
  54.9 1.3 %tile.4 = f32[16,16,16,12]{1,0,3,2:T(8,128)} broadcast(f32[16,12]{0,1:T(8,128)S(1)} %copy.42), dimensions={1,3} | broadcast | bytes 197376 | tf_op jit(solution)/shard_map/tile | solution.py:304
  56.2 2.6 %tile.10 = f32[1,256,192]{1,2,0:T(8,128)} reshape(f32[16,16,16,12]{1,0,3,2:T(8,128)} %tile.4) | data formatting | bytes 393216 | tf_op jit(solution)/shard_map/tile | solution.py:304
  58.8 1.1 %copy.43 = f32[1,256,192]{2,1,0:T(8,128)S(1)} copy(f32[1,256,192]{1,2,0:T(8,128)} %tile.10) | data formatting | bytes 393216 | tf_op jit(solution)/shard_map/tile | solution.py:304
  60.0 0.2 subtract_convert_fusion
  60.1 0.2 fusion.2
  60.4 0.0 copy-start
  60.4 0.9 %copy-done = bf16[2,3,128,128]{3,2,1,0:T(8,128)(2,1)S(1)} copy-done((bf16[2,3,128,128]{3,2,1,0:T(8,128)(2,1)S(1)}, bf16[2,3,128,128]{3,2,1,0:T(8,128)(2,1)}, u32[]{:S(2)}) %copy-start) | copy-done | bytes 196632
  61.3 5.4 %respond.1 = bf16[16,8,64,128]{3,2,1,0:T(8,128)(2,1)} custom-call(f32[8,6]{1,0:T(8,128)S(1)} %broadcast_multiply_fusion.weight_ref, bf16[2,512,768]{2,1,0:T(8,128)(2,1)S(1)} %get-tuple-element.34.fields_ref, bf16[2,3,128,128]{3,2,1,0:T(8,128)(2,1)S(1)} %copy-done), custom_call_target="tpu_custom_call" | custom-call | flops 200000000 | bytes 4000000 | tf_op jit(solution)/shard_map/respond/pallas_call | solution.py:371
  66.7 12.1 %all-to-all-done = bf16[128,48,128]{2,1,0:T(8,128)(2,1)S(1)} async-done(((bf16[128,48,128]{2,1,0:T(8,128)(2,1)}), bf16[128,48,128]{2,1,0:T(8,128)(2,1)S(1)}, u32[]{:S(2)}, u32[]{:S(2)}) %all-to-all-start) | async-done | bytes 1572896 | tf_op jit(solution)/shard_map/all_to_all | solution.py:367
  78.8 2.1 %mix.1 = bf16[8192,128]{1,0:T(8,128)(2,1)} custom-call(bf16[2,256,192]{2,1,0:T(8,128)(2,1)S(1)} %pad_maximum_fusion.1.mix_ref, bf16[6144,128]{1,0:T(8,128)(2,1)S(1)} %bitcast.16), custom_call_target="tpu_custom_call" | custom-call | flops 1600000000 | bytes 4000000 | tf_op jit(solution)/shard_map/mix/pallas_call | solution.py:386
  (15 shorter events, 0.2 us)
Async XLA Ops:
  0.6 11.3 %copy-start.1 = (bf16[8,64,128]{2,1,0:T(8,128)(2,1)S(1)}, bf16[8,64,128]{2,1,0:T(8,128)(2,1)}, u32[]{:S(2)}) copy-start(bf16[8,64,128]{2,1,0:T(8,128)(2,1)} %param.9) | copy-start | bytes 393220
  0.6 8.0 %collective-permute-start.1 = (bf16[8,64,128]{2,1,0:T(8,128)(2,1)}, bf16[8,64,128]{2,1,0:T(8,128)(2,1)S(1)}, u32[]{:S(2)}, u32[]{:S(2)}) collective-permute-start(bf16[8,64,128]{2,1,0:T(8,128)(2,1)} %param.9), channel_id=1, source_target_pairs={{4,8},{8,4},{12,16},{16,12},{20,24},{24,20},{28,32},{32,28},{36,40... | collective-permute-start | bytes 393224 | tf_op jit(solution)/shard_map/ppermute | solution.py:296
  5.3 3.3 %collective-permute-start = (bf16[8,64,128]{2,1,0:T(8,128)(2,1)}, bf16[8,64,128]{2,1,0:T(8,128)(2,1)S(1)}, u32[]{:S(2)}, u32[]{:S(2)}) collective-permute-start(bf16[8,64,128]{2,1,0:T(8,128)(2,1)} %param.9), channel_id=1, source_target_pairs={{0,4},{4,0},{8,12},{12,8},{16,20},{20,16},{24,28},{28,24},{32,36},... | collective-permute-start | bytes 393224 | tf_op jit(solution)/shard_map/ppermute | solution.py:296
  8.7 3.2 %collective-permute-start.2 = (bf16[20,8,128]{2,1,0:T(8,128)(2,1)S(1)}, bf16[20,8,128]{2,1,0:T(8,128)(2,1)S(1)}, u32[]{:S(2)}, u32[]{:S(2)}) collective-permute-start(bf16[20,8,128]{2,1,0:T(8,128)(2,1)S(1)} %get-tuple-element.49), channel_id=1, source_target_pairs={{0,1},{1,0},{2,3},{3,2},{4,5},{5,4},{6,7},{7,6},{8,9},{9,8},{10,11... | collective-permute-start | bytes 122888 | tf_op jit(solution)/shard_map/ppermute | solution.py:296
  11.2 0.8 collective-permute-start.3
  38.7 40.1 %all-to-all-start = ((bf16[128,48,128]{2,1,0:T(8,128)(2,1)}), bf16[128,48,128]{2,1,0:T(8,128)(2,1)S(1)}, u32[]{:S(2)}, u32[]{:S(2)}) async-start(bf16[128,48,128]{2,1,0:T(8,128)(2,1)} %bitcast.5), calls=%async_computation | async-start | bytes 3145728 | tf_op jit(solution)/shard_map/all_to_all | solution.py:367
  60.4 0.9 %copy-start = (bf16[2,3,128,128]{3,2,1,0:T(8,128)(2,1)S(1)}, bf16[2,3,128,128]{3,2,1,0:T(8,128)(2,1)}, u32[]{:S(2)}) copy-start(bf16[2,3,128,128]{3,2,1,0:T(8,128)(2,1)} %constant.109.clone.x_band_ref) | copy-start | bytes 589828

commit v9 on v8

--- a/solution.py
+++ b/solution.py
@@ -320,7 +320,7 @@
     edge_low, edge_high = extended(slice(0, Y_PAD)), extended(slice(CY - Y_PAD, CY))
     side_first = swap(jnp.where(even_narrow, edge_high, edge_low), "narrow", 0)
     side_second = swap(jnp.where(even_narrow, edge_low, edge_high), "narrow", 1)
-    first, second, side_first = lax.optimization_barrier((first, second, side_first))
+    first, second, side_second = lax.optimization_barrier((first, second, side_second))
     center = extended(slice(0, CY))
 
     table_rows = ((tile_points >> 3) & 15) * ROWS + (tile_points >> 7)

time: 81.4 us -> 79.9 us (0.982)
  starting transfers between devices: 22.2 us -> 19.5 us
  waiting for transfers between devices: 12.1 us -> 13.4 us
    all_to_all x1, starting transfers between devices: 15.1 us -> 9.48 us  [per_device(): lax.all_to_all(send.reshape(OWNERS, SEND_ROWS, PTS), ('wide', 'narrow'),...]
    ppermute x4, starting transfers between devices: 7.11 us -> 9.99 us  [swap(): return lax.ppermute(value, axis, pairs)]
    ppermute x4, waiting for transfers between devices: 0.01 us -> 1.32 us  [swap(): return lax.ppermute(value, axis, pairs)]
  transfers between devices with their start and end apart: 5 -> 5, of which waited for: 1 -> 2; matrix products, arithmetic and copies ran while one was open for 13% -> 13% of each run, Pallas kernels for 7% -> 7%
where the time goes in v9:
time: 79.9 us; the launch traced here: 79.5 us
  Pallas kernels  34.1 us (43%)
  starting transfers between devices  19.5 us (24%)
  waiting for transfers between devices  13.4 us (17%)
  local copies, waits for them, and re-layouts  7.69 us (10%)
  other arithmetic  3.82 us (5%)
  between operations  0.98 us (1%)
    pallas_call x1, Pallas kernels, per_device(): pl.pallas_call(sample_kernel, out_shape=(jax.ShapeDtypeStruct((OWNERS * S...  26.7 us
    all_to_all x1, waiting for transfers between devices, per_device(): lax.all_to_all(send.reshape(OWNERS, SEND_ROWS, PTS), ('wide', 'narrow'),...  12.1 us
    ppermute x4, starting transfers between devices, swap(): return lax.ppermute(value, axis, pairs)  9.99 us
    all_to_all x1, starting transfers between devices, per_device(): lax.all_to_all(send.reshape(OWNERS, SEND_ROWS, PTS), ('wide', 'narrow'),...  9.48 us
    pallas_call x1, Pallas kernels, per_device(): pl.pallas_call(response_kernel, grid=(SZ,), out_shape=jax.ShapeDtypeStruc...  5.38 us
    another operation x3, local copies, waits for them, and re-layouts, mix_matrix(): full = jnp.where(rows == columns, jnp.tile(scales, (16, 16)), 0.0)  4.99 us
    pallas_call x1, Pallas kernels, per_device(): pl.pallas_call(mix_kernel, out_shape=jax.ShapeDtypeStruct((SLOTS * 16, PT...  2.09 us
  transfers between devices with their start and end apart: 5, of which 2 were waited for; matrix products, arithmetic and copies ran while one was open for 13% of the time, Pallas kernels for 7%

profile of v9, /device:TPU:1, one launch (start us, length us, event | category | flops | bytes accessed | tf_op | source)
XLA Modules:
  0.0 79.5 jit_solution(11032651929196301137)
XLA Ops:
  0.6 0.0 copy-start.1
  0.6 4.6 %collective-permute-start.1 = (bf16[8,64,128]{2,1,0:T(8,128)(2,1)}, bf16[8,64,128]{2,1,0:T(8,128)(2,1)S(1)}, u32[]{:S(2)}, u32[]{:S(2)}) collective-permute-start(bf16[8,64,128]{2,1,0:T(8,128)(2,1)} %param.9), channel_id=1, source_target_pairs={{4,8},{8,4},{12,16},{16,12},{20,24},{24,20},{28,32},{32,28},{36,40... | collective-permute-start | bytes 393224 | tf_op jit(solution)/shard_map/ppermute | solution.py:296
  5.3 0.1 collective-permute-start
  5.4 0.7 fusion.3
  6.1 0.9 %convert_reduce_fusion = s32[256]{0:T(256)S(1)} fusion(s32[256]{0:T(256)} %bitcast.17), kind=kLoop, calls=%fused_computation.4 | loop fusion | flops 327424 | bytes 2048 | tf_op jit(solution)/shard_map/reduce_sum | solution.py:332
  7.0 0.9 %broadcast_and_fusion = (s32[256,128]{1,0:T(8,128)S(1)}, s32[256,128]{1,0:T(8,128)S(1)}) fusion(s32[256,128]{1,0:T(8,128)} %param.11), kind=kLoop, calls=%fused_computation.12 | loop fusion | flops 196608 | bytes 393216 | tf_op jit(solution)/shard_map/and | solution.py:327
  7.9 0.7 multiply_add_fusion.slot_ref
  8.6 0.0 collective-permute-done.1
  8.6 0.0 collective-permute-done
  8.7 0.7 collective-permute-start.2
  9.4 0.8 %cosine_bitcast_fusion = (f32[8,1]{0,1:T(1,128)S(1)}, f32[8,1]{0,1:T(1,128)S(1)}, f32[8,1]{0,1:T(1,128)S(1)}, f32[1,8]{1,0:T(1,128)S(1)}) fusion(f32[2,8]{1,0:T(2,128)} %param.10), kind=kLoop, calls=%fused_computation.35 | loop fusion | flops 24 | bytes 192 | tf_op jit(solution)/shard_map/cos | solution.py:278
  10.2 4.6 %collective-permute-start.3 = (bf16[20,8,128]{2,1,0:T(8,128)(2,1)S(1)}, bf16[20,8,128]{2,1,0:T(8,128)(2,1)S(1)}, u32[]{:S(2)}, u32[]{:S(2)}) collective-permute-start(bf16[20,8,128]{2,1,0:T(8,128)(2,1)S(1)} %get-tuple-element.48), channel_id=1, source_target_pairs={{0,1},{1,0},{2,3},{3,2},{4,5},{5,4},{6,7},{7,6},{8,9},{9,8},{10,11... | collective-permute-start | bytes 122888 | tf_op jit(solution)/shard_map/ppermute | solution.py:296
  14.8 0.0 collective-permute-done.2.second_ref
  14.8 0.0 copy-done.1
  14.9 1.3 %collective-permute-done.3.first_ref = bf16[20,8,128]{2,1,0:T(8,128)(2,1)S(1)} collective-permute-done((bf16[20,8,128]{2,1,0:T(8,128)(2,1)S(1)}, bf16[20,8,128]{2,1,0:T(8,128)(2,1)S(1)}, u32[]{:S(2)}, u32[]{:S(2)}) %collective-permute-start.3) | collective-permute-done | bytes 40992 | tf_op jit(solution)/shard_map/ppermute | solution.py:296
  16.2 26.7 %sample.1 = (bf16[6144,128]{1,0:T(8,128)(2,1)}, bf16[2,512,768]{2,1,0:T(8,128)(2,1)S(1)}) custom-call(s32[256]{0:T(256)S(1)} %multiply_add_fusion.slot_ref, s32[256,128]{1,0:T(8,128)S(1)} %get-tuple-element.41.rows_ref, bf16[20,64,128]{2,1,0:T(8,128)(2,1)S(1)} %pad_maximum_fusion.center_ref, bf16[20,8,128]{2,1,0:T(8,128)(2,1)S(1)} %collective-permute-done.3.first_ref, ...), custom_call_target="tpu_custom_call" | custom-call | flops 4000000000 | bytes 8000000 | tf_op jit(solution)/shard_map/sample/pallas_call | solution.py:339
  42.9 9.5 %all-to-all-start = ((bf16[128,48,128]{2,1,0:T(8,128)(2,1)}), bf16[128,48,128]{2,1,0:T(8,128)(2,1)S(1)}, u32[]{:S(2)}, u32[]{:S(2)}) async-start(bf16[128,48,128]{2,1,0:T(8,128)(2,1)} %bitcast.5), calls=%async_computation | async-start | bytes 3145728 | tf_op jit(solution)/shard_map/all_to_all | solution.py:367
  52.4 0.1 copy.41
  52.4 0.1 copy.33
  52.5 0.1 copy.31
  52.6 0.1 copy.35
  52.7 0.1 stack.4
  52.8 0.5 scatter.9
  53.3 0.1 copy.42
  53.4 1.3 %tile.4 = f32[16,16,16,12]{1,0,3,2:T(8,128)} broadcast(f32[16,12]{0,1:T(8,128)S(1)} %copy.42), dimensions={1,3} | broadcast | bytes 197376 | tf_op jit(solution)/shard_map/tile | solution.py:304
  54.7 2.6 %tile.10 = f32[1,256,192]{1,2,0:T(8,128)} reshape(f32[16,16,16,12]{1,0,3,2:T(8,128)} %tile.4) | data formatting | bytes 393216 | tf_op jit(solution)/shard_map/tile | solution.py:304
  57.3 1.1 %copy.43 = f32[1,256,192]{2,1,0:T(8,128)S(1)} copy(f32[1,256,192]{1,2,0:T(8,128)} %tile.10) | data formatting | bytes 393216 | tf_op jit(solution)/shard_map/tile | solution.py:304
  58.4 0.2 subtract_convert_fusion
  58.6 0.2 fusion.2
  58.9 0.0 copy-start
  58.9 0.9 %copy-done = bf16[2,3,128,128]{3,2,1,0:T(8,128)(2,1)S(1)} copy-done((bf16[2,3,128,128]{3,2,1,0:T(8,128)(2,1)S(1)}, bf16[2,3,128,128]{3,2,1,0:T(8,128)(2,1)}, u32[]{:S(2)}) %copy-start) | copy-done | bytes 196632
  59.8 5.4 %respond.1 = bf16[16,8,64,128]{3,2,1,0:T(8,128)(2,1)} custom-call(f32[8,6]{1,0:T(8,128)S(1)} %broadcast_multiply_fusion.weight_ref, bf16[2,512,768]{2,1,0:T(8,128)(2,1)S(1)} %get-tuple-element.34.fields_ref, bf16[2,3,128,128]{3,2,1,0:T(8,128)(2,1)S(1)} %copy-done), custom_call_target="tpu_custom_call" | custom-call | flops 200000000 | bytes 4000000 | tf_op jit(solution)/shard_map/respond/pallas_call | solution.py:371
  65.2 12.1 %all-to-all-done = bf16[128,48,128]{2,1,0:T(8,128)(2,1)S(1)} async-done(((bf16[128,48,128]{2,1,0:T(8,128)(2,1)}), bf16[128,48,128]{2,1,0:T(8,128)(2,1)S(1)}, u32[]{:S(2)}, u32[]{:S(2)}) %all-to-all-start) | async-done | bytes 1572896 | tf_op jit(solution)/shard_map/all_to_all | solution.py:367
  77.3 2.1 %mix.1 = bf16[8192,128]{1,0:T(8,128)(2,1)} custom-call(bf16[2,256,192]{2,1,0:T(8,128)(2,1)S(1)} %pad_maximum_fusion.1.mix_ref, bf16[6144,128]{1,0:T(8,128)(2,1)S(1)} %bitcast.16), custom_call_target="tpu_custom_call" | custom-call | flops 1600000000 | bytes 4000000 | tf_op jit(solution)/shard_map/mix/pallas_call | solution.py:386
  (15 shorter events, 0.2 us)
Async XLA Ops:
  0.6 14.2 %copy-start.1 = (bf16[8,64,128]{2,1,0:T(8,128)(2,1)S(1)}, bf16[8,64,128]{2,1,0:T(8,128)(2,1)}, u32[]{:S(2)}) copy-start(bf16[8,64,128]{2,1,0:T(8,128)(2,1)} %param.9) | copy-start | bytes 393220
  0.6 8.0 %collective-permute-start.1 = (bf16[8,64,128]{2,1,0:T(8,128)(2,1)}, bf16[8,64,128]{2,1,0:T(8,128)(2,1)S(1)}, u32[]{:S(2)}, u32[]{:S(2)}) collective-permute-start(bf16[8,64,128]{2,1,0:T(8,128)(2,1)} %param.9), channel_id=1, source_target_pairs={{4,8},{8,4},{12,16},{16,12},{20,24},{24,20},{28,32},{32,28},{36,40... | collective-permute-start | bytes 393224 | tf_op jit(solution)/shard_map/ppermute | solution.py:296
  5.3 3.3 %collective-permute-start = (bf16[8,64,128]{2,1,0:T(8,128)(2,1)}, bf16[8,64,128]{2,1,0:T(8,128)(2,1)S(1)}, u32[]{:S(2)}, u32[]{:S(2)}) collective-permute-start(bf16[8,64,128]{2,1,0:T(8,128)(2,1)} %param.9), channel_id=1, source_target_pairs={{0,4},{4,0},{8,12},{12,8},{16,20},{20,16},{24,28},{28,24},{32,36},... | collective-permute-start | bytes 393224 | tf_op jit(solution)/shard_map/ppermute | solution.py:296
  8.7 6.1 %collective-permute-start.2 = (bf16[20,8,128]{2,1,0:T(8,128)(2,1)S(1)}, bf16[20,8,128]{2,1,0:T(8,128)(2,1)S(1)}, u32[]{:S(2)}, u32[]{:S(2)}) collective-permute-start(bf16[20,8,128]{2,1,0:T(8,128)(2,1)S(1)} %get-tuple-element.49), channel_id=1, source_target_pairs={{1,2},{2,1},{5,6},{6,5},{9,10},{10,9},{13,14},{14,13},{17,18},{18,... | collective-permute-start | bytes 122888 | tf_op jit(solution)/shard_map/ppermute | solution.py:296
  10.2 6.0 %collective-permute-start.3 = (bf16[20,8,128]{2,1,0:T(8,128)(2,1)S(1)}, bf16[20,8,128]{2,1,0:T(8,128)(2,1)S(1)}, u32[]{:S(2)}, u32[]{:S(2)}) collective-permute-start(bf16[20,8,128]{2,1,0:T(8,128)(2,1)S(1)} %get-tuple-element.48), channel_id=1, source_target_pairs={{0,1},{1,0},{2,3},{3,2},{4,5},{5,4},{6,7},{7,6},{8,9},{9,8},{10,11... | collective-permute-start | bytes 122888 | tf_op jit(solution)/shard_map/ppermute | solution.py:296
  42.9 34.4 %all-to-all-start = ((bf16[128,48,128]{2,1,0:T(8,128)(2,1)}), bf16[128,48,128]{2,1,0:T(8,128)(2,1)S(1)}, u32[]{:S(2)}, u32[]{:S(2)}) async-start(bf16[128,48,128]{2,1,0:T(8,128)(2,1)} %bitcast.5), calls=%async_computation | async-start | bytes 3145728 | tf_op jit(solution)/shard_map/all_to_all | solution.py:367
  58.9 0.9 %copy-start = (bf16[2,3,128,128]{3,2,1,0:T(8,128)(2,1)S(1)}, bf16[2,3,128,128]{3,2,1,0:T(8,128)(2,1)}, u32[]{:S(2)}) copy-start(bf16[2,3,128,128]{3,2,1,0:T(8,128)(2,1)} %constant.109.clone.x_band_ref) | copy-start | bytes 589828

commit v10 on v9

--- a/solution.py
+++ b/solution.py
@@ -23,7 +23,7 @@
 LANES = 128
 TILES = 256
 PTS = 128
-STEP_TILES = 32
+STEP_TILES = 64
 STEPS = TILES // STEP_TILES
 GROUP = 4
 PART = 512
@@ -31,7 +31,7 @@
 OWNERS = 128
 SLOTS = OWNERS * CAP
 SEND_ROWS = CAP * 2 * COMPS
-MIX_PARTS = 4
+MIX_PARTS = 8
 
 KINDS = ((2, 0, 0), (0, 2, 0), (0, 0, 2), (1, 1, 0), (1, 0, 1), (0, 1, 1))
 

time: 79.9 us -> 79.2 us (level)
  Pallas kernels: 34.1 us -> 33.3 us
where the time goes in v10:
time: 79.2 us; the launch traced here: 78.7 us
  Pallas kernels  33.3 us (42%)
  starting transfers between devices  19.5 us (25%)
  waiting for transfers between devices  13.4 us (17%)
  local copies, waits for them, and re-layouts  7.69 us (10%)
  other arithmetic  3.82 us (5%)
  between operations  1 us (1%)
    pallas_call x1, Pallas kernels, per_device(): pl.pallas_call(sample_kernel, out_shape=(jax.ShapeDtypeStruct((OWNERS * S...  25.9 us
    all_to_all x1, waiting for transfers between devices, per_device(): lax.all_to_all(send.reshape(OWNERS, SEND_ROWS, PTS), ('wide', 'narrow'),...  12.1 us
    ppermute x4, starting transfers between devices, swap(): return lax.ppermute(value, axis, pairs)  9.99 us
    all_to_all x1, starting transfers between devices, per_device(): lax.all_to_all(send.reshape(OWNERS, SEND_ROWS, PTS), ('wide', 'narrow'),...  9.49 us
    pallas_call x1, Pallas kernels, per_device(): pl.pallas_call(response_kernel, grid=(SZ,), out_shape=jax.ShapeDtypeStruc...  5.38 us
    another operation x3, local copies, waits for them, and re-layouts, mix_matrix(): full = jnp.where(rows == columns, jnp.tile(scales, (16, 16)), 0.0)  4.99 us
    pallas_call x1, Pallas kernels, per_device(): pl.pallas_call(mix_kernel, out_shape=jax.ShapeDtypeStruct((SLOTS * 16, PT...  2.03 us
  transfers between devices with their start and end apart: 5, of which 2 were waited for; matrix products, arithmetic and copies ran while one was open for 13% of the time, Pallas kernels for 7%

profile of v10, /device:TPU:1, one launch (start us, length us, event | category | flops | bytes accessed | tf_op | source)
XLA Modules:
  0.0 78.7 jit_solution(8024900165320911883)
XLA Ops:
  0.6 0.0 copy-start.1
  0.6 4.6 %collective-permute-start.1 = (bf16[8,64,128]{2,1,0:T(8,128)(2,1)}, bf16[8,64,128]{2,1,0:T(8,128)(2,1)S(1)}, u32[]{:S(2)}, u32[]{:S(2)}) collective-permute-start(bf16[8,64,128]{2,1,0:T(8,128)(2,1)} %param.9), channel_id=1, source_target_pairs={{4,8},{8,4},{12,16},{16,12},{20,24},{24,20},{28,32},{32,28},{36,40... | collective-permute-start | bytes 393224 | tf_op jit(solution)/shard_map/ppermute | solution.py:296
  5.3 0.1 collective-permute-start
  5.4 0.7 fusion.3
  6.1 0.9 %convert_reduce_fusion = s32[256]{0:T(256)S(1)} fusion(s32[256]{0:T(256)} %bitcast.17), kind=kLoop, calls=%fused_computation.4 | loop fusion | flops 327424 | bytes 2048 | tf_op jit(solution)/shard_map/reduce_sum | solution.py:332
  7.0 0.9 %broadcast_and_fusion = (s32[256,128]{1,0:T(8,128)S(1)}, s32[256,128]{1,0:T(8,128)S(1)}) fusion(s32[256,128]{1,0:T(8,128)} %param.11), kind=kLoop, calls=%fused_computation.12 | loop fusion | flops 196608 | bytes 393216 | tf_op jit(solution)/shard_map/and | solution.py:327
  7.9 0.7 multiply_add_fusion.slot_ref
  8.6 0.0 collective-permute-done.1
  8.6 0.0 collective-permute-done
  8.7 0.7 collective-permute-start.2
  9.4 0.8 %cosine_bitcast_fusion = (f32[8,1]{0,1:T(1,128)S(1)}, f32[8,1]{0,1:T(1,128)S(1)}, f32[8,1]{0,1:T(1,128)S(1)}, f32[1,8]{1,0:T(1,128)S(1)}) fusion(f32[2,8]{1,0:T(2,128)} %param.10), kind=kLoop, calls=%fused_computation.35 | loop fusion | flops 24 | bytes 192 | tf_op jit(solution)/shard_map/cos | solution.py:278
  10.2 4.6 %collective-permute-start.3 = (bf16[20,8,128]{2,1,0:T(8,128)(2,1)S(1)}, bf16[20,8,128]{2,1,0:T(8,128)(2,1)S(1)}, u32[]{:S(2)}, u32[]{:S(2)}) collective-permute-start(bf16[20,8,128]{2,1,0:T(8,128)(2,1)S(1)} %get-tuple-element.48), channel_id=1, source_target_pairs={{0,1},{1,0},{2,3},{3,2},{4,5},{5,4},{6,7},{7,6},{8,9},{9,8},{10,11... | collective-permute-start | bytes 122888 | tf_op jit(solution)/shard_map/ppermute | solution.py:296
  14.8 0.0 collective-permute-done.2.second_ref
  14.8 0.0 copy-done.1
  14.9 1.3 %collective-permute-done.3.first_ref = bf16[20,8,128]{2,1,0:T(8,128)(2,1)S(1)} collective-permute-done((bf16[20,8,128]{2,1,0:T(8,128)(2,1)S(1)}, bf16[20,8,128]{2,1,0:T(8,128)(2,1)S(1)}, u32[]{:S(2)}, u32[]{:S(2)}) %collective-permute-start.3) | collective-permute-done | bytes 40992 | tf_op jit(solution)/shard_map/ppermute | solution.py:296
  16.2 25.9 %sample.1 = (bf16[6144,128]{1,0:T(8,128)(2,1)}, bf16[2,512,768]{2,1,0:T(8,128)(2,1)S(1)}) custom-call(s32[256]{0:T(256)S(1)} %multiply_add_fusion.slot_ref, s32[256,128]{1,0:T(8,128)S(1)} %get-tuple-element.41.rows_ref, bf16[20,64,128]{2,1,0:T(8,128)(2,1)S(1)} %pad_maximum_fusion.center_ref, bf16[20,8,128]{2,1,0:T(8,128)(2,1)S(1)} %collective-permute-done.3.first_ref, ...), custom_call_target="tpu_custom_call" | custom-call | flops 4000000000 | bytes 8000000 | tf_op jit(solution)/shard_map/sample/pallas_call | solution.py:339
  42.1 9.5 %all-to-all-start = ((bf16[128,48,128]{2,1,0:T(8,128)(2,1)}), bf16[128,48,128]{2,1,0:T(8,128)(2,1)S(1)}, u32[]{:S(2)}, u32[]{:S(2)}) async-start(bf16[128,48,128]{2,1,0:T(8,128)(2,1)} %bitcast.5), calls=%async_computation | async-start | bytes 3145728 | tf_op jit(solution)/shard_map/all_to_all | solution.py:367
  51.6 0.1 copy.41
  51.7 0.1 copy.33
  51.8 0.1 copy.31
  51.8 0.1 copy.35
  51.9 0.1 stack.4
  52.0 0.5 scatter.9
  52.5 0.1 copy.42
  52.6 1.3 %tile.4 = f32[16,16,16,12]{1,0,3,2:T(8,128)} broadcast(f32[16,12]{0,1:T(8,128)S(1)} %copy.42), dimensions={1,3} | broadcast | bytes 197376 | tf_op jit(solution)/shard_map/tile | solution.py:304
  53.9 2.6 %tile.10 = f32[1,256,192]{1,2,0:T(8,128)} reshape(f32[16,16,16,12]{1,0,3,2:T(8,128)} %tile.4) | data formatting | bytes 393216 | tf_op jit(solution)/shard_map/tile | solution.py:304
  56.6 1.1 %copy.43 = f32[1,256,192]{2,1,0:T(8,128)S(1)} copy(f32[1,256,192]{1,2,0:T(8,128)} %tile.10) | data formatting | bytes 393216 | tf_op jit(solution)/shard_map/tile | solution.py:304
  57.7 0.2 subtract_convert_fusion
  57.9 0.2 fusion.2
  58.1 0.0 copy-start
  58.1 0.9 %copy-done = bf16[2,3,128,128]{3,2,1,0:T(8,128)(2,1)S(1)} copy-done((bf16[2,3,128,128]{3,2,1,0:T(8,128)(2,1)S(1)}, bf16[2,3,128,128]{3,2,1,0:T(8,128)(2,1)}, u32[]{:S(2)}) %copy-start) | copy-done | bytes 196632
  59.0 5.4 %respond.1 = bf16[16,8,64,128]{3,2,1,0:T(8,128)(2,1)} custom-call(f32[8,6]{1,0:T(8,128)S(1)} %broadcast_multiply_fusion.weight_ref, bf16[2,512,768]{2,1,0:T(8,128)(2,1)S(1)} %get-tuple-element.34.fields_ref, bf16[2,3,128,128]{3,2,1,0:T(8,128)(2,1)S(1)} %copy-done), custom_call_target="tpu_custom_call" | custom-call | flops 200000000 | bytes 4000000 | tf_op jit(solution)/shard_map/respond/pallas_call | solution.py:371
  64.4 12.1 %all-to-all-done = bf16[128,48,128]{2,1,0:T(8,128)(2,1)S(1)} async-done(((bf16[128,48,128]{2,1,0:T(8,128)(2,1)}), bf16[128,48,128]{2,1,0:T(8,128)(2,1)S(1)}, u32[]{:S(2)}, u32[]{:S(2)}) %all-to-all-start) | async-done | bytes 1572896 | tf_op jit(solution)/shard_map/all_to_all | solution.py:367
  76.5 2.0 %mix.1 = bf16[8192,128]{1,0:T(8,128)(2,1)} custom-call(bf16[2,256,192]{2,1,0:T(8,128)(2,1)S(1)} %pad_maximum_fusion.1.mix_ref, bf16[6144,128]{1,0:T(8,128)(2,1)S(1)} %bitcast.16), custom_call_target="tpu_custom_call" | custom-call | flops 1600000000 | bytes 4000000 | tf_op jit(solution)/shard_map/mix/pallas_call | solution.py:386
  (15 shorter events, 0.2 us)
Async XLA Ops:
  0.6 14.2 %copy-start.1 = (bf16[8,64,128]{2,1,0:T(8,128)(2,1)S(1)}, bf16[8,64,128]{2,1,0:T(8,128)(2,1)}, u32[]{:S(2)}) copy-start(bf16[8,64,128]{2,1,0:T(8,128)(2,1)} %param.9) | copy-start | bytes 393220
  0.6 8.0 %collective-permute-start.1 = (bf16[8,64,128]{2,1,0:T(8,128)(2,1)}, bf16[8,64,128]{2,1,0:T(8,128)(2,1)S(1)}, u32[]{:S(2)}, u32[]{:S(2)}) collective-permute-start(bf16[8,64,128]{2,1,0:T(8,128)(2,1)} %param.9), channel_id=1, source_target_pairs={{4,8},{8,4},{12,16},{16,12},{20,24},{24,20},{28,32},{32,28},{36,40... | collective-permute-start | bytes 393224 | tf_op jit(solution)/shard_map/ppermute | solution.py:296
  5.3 3.3 %collective-permute-start = (bf16[8,64,128]{2,1,0:T(8,128)(2,1)}, bf16[8,64,128]{2,1,0:T(8,128)(2,1)S(1)}, u32[]{:S(2)}, u32[]{:S(2)}) collective-permute-start(bf16[8,64,128]{2,1,0:T(8,128)(2,1)} %param.9), channel_id=1, source_target_pairs={{0,4},{4,0},{8,12},{12,8},{16,20},{20,16},{24,28},{28,24},{32,36},... | collective-permute-start | bytes 393224 | tf_op jit(solution)/shard_map/ppermute | solution.py:296
  8.7 6.1 %collective-permute-start.2 = (bf16[20,8,128]{2,1,0:T(8,128)(2,1)S(1)}, bf16[20,8,128]{2,1,0:T(8,128)(2,1)S(1)}, u32[]{:S(2)}, u32[]{:S(2)}) collective-permute-start(bf16[20,8,128]{2,1,0:T(8,128)(2,1)S(1)} %get-tuple-element.49), channel_id=1, source_target_pairs={{1,2},{2,1},{5,6},{6,5},{9,10},{10,9},{13,14},{14,13},{17,18},{18,... | collective-permute-start | bytes 122888 | tf_op jit(solution)/shard_map/ppermute | solution.py:296
  10.2 6.0 %collective-permute-start.3 = (bf16[20,8,128]{2,1,0:T(8,128)(2,1)S(1)}, bf16[20,8,128]{2,1,0:T(8,128)(2,1)S(1)}, u32[]{:S(2)}, u32[]{:S(2)}) collective-permute-start(bf16[20,8,128]{2,1,0:T(8,128)(2,1)S(1)} %get-tuple-element.48), channel_id=1, source_target_pairs={{0,1},{1,0},{2,3},{3,2},{4,5},{5,4},{6,7},{7,6},{8,9},{9,8},{10,11... | collective-permute-start | bytes 122888 | tf_op jit(solution)/shard_map/ppermute | solution.py:296
  42.1 34.4 %all-to-all-start = ((bf16[128,48,128]{2,1,0:T(8,128)(2,1)}), bf16[128,48,128]{2,1,0:T(8,128)(2,1)S(1)}, u32[]{:S(2)}, u32[]{:S(2)}) async-start(bf16[128,48,128]{2,1,0:T(8,128)(2,1)} %bitcast.5), calls=%async_computation | async-start | bytes 3145728 | tf_op jit(solution)/shard_map/all_to_all | solution.py:367
  58.1 0.9 %copy-start = (bf16[2,3,128,128]{3,2,1,0:T(8,128)(2,1)S(1)}, bf16[2,3,128,128]{3,2,1,0:T(8,128)(2,1)}, u32[]{:S(2)}) copy-start(bf16[2,3,128,128]{3,2,1,0:T(8,128)(2,1)} %constant.109.clone.x_band_ref) | copy-start | bytes 589828
